TPU v7x, 32 devices: a whole 2x2x4 slice. The times are simulated.
32 devices in a mesh: dp: 4 (over y, core), ctx: 8 (over z, x).
Axes of the slice: x: 2, y: 2, z: 4, core: 2. Of those that a mesh axis runs over, the one named last changes fastest.
Arguments:
- layer_input: bfloat16 [8, 1024, 1024], P('dp', 'ctx'), may hold values from -6 to 6
- doc_ids: int32 [8, 1024], P('dp'), may hold values from 0 to 4, as said below
- attn_gain: bfloat16 [1024], P(('dp', 'ctx')), may hold values from 0.099609375 to 1.8984375
- query_weight: bfloat16 [1024, 1024], P(('dp', 'ctx')), may hold values from -0.25 to 0.25
- key_weight: bfloat16 [1024, 1024], P(('dp', 'ctx')), may hold values from -0.1875 to 0.1875
- value_weight: bfloat16 [1024, 1024], P(('dp', 'ctx')), may hold values from -0.1875 to 0.1875
- out_weight: bfloat16 [1024, 1024], P(('dp', 'ctx')), may hold values from -1.5 to 1.5
- mlp_gain: bfloat16 [1024], P(('dp', 'ctx')), may hold values from 0.099609375 to 1.8984375
- gate_weight: bfloat16 [1024, 4096], P(('dp', 'ctx')), may hold values from -0.1875 to 0.1875
- up_weight: bfloat16 [1024, 4096], P(('dp', 'ctx')), may hold values from -0.1875 to 0.1875
- down_weight: bfloat16 [4096, 1024], P(('dp', 'ctx')), may hold values from -0.1875 to 0.1875
- out_grad: bfloat16 [8, 1024, 1024], P('dp', 'ctx'), may hold values from -6 to 6
Outputs:
- layer_output: bfloat16 [8, 1024, 1024], P('dp', 'ctx')
- input_grad: float32 [8, 1024, 1024], P('dp', 'ctx')
- attn_gain_grad: float32 [1024], P(('dp', 'ctx'))
- query_grad: float32 [1024, 1024], P(('dp', 'ctx'))
- key_grad: float32 [1024, 1024], P(('dp', 'ctx'))
- value_grad: float32 [1024, 1024], P(('dp', 'ctx'))
- out_proj_grad: float32 [1024, 1024], P(('dp', 'ctx'))
- mlp_gain_grad: float32 [1024], P(('dp', 'ctx'))
- gate_grad: float32 [1024, 4096], P(('dp', 'ctx'))
- up_grad: float32 [1024, 4096], P(('dp', 'ctx'))
- down_grad: float32 [4096, 1024], P(('dp', 'ctx'))
Inputs may be any that keep to these rules, and one draw needn't show every extreme that they name: Within each sequence doc_ids start at 0 and never fall; the rows of one value form one document of 60 to 800 rows, except the document at one end of a sequence, which may be shorter; every sequence holds one document of exactly 800 rows, at its start or at its end; in the first sequence all other documents but the one at its other end have exactly 60 rows.
All inputs are finite; a program needn't handle non-finite values.
Results may differ from a plain program's by a relative error of at most 0.015.
Values may be sent and summed in bfloat16 or wider, within the bound.
A program may use at most 256 MiB of HBM per device.

v0:
```python
import jax
import jax.numpy as jnp
from jax import lax
from jax.sharding import PartitionSpec as P

HEAD = 64


EPS = 1e-05


def product(left, right):
    return jnp.dot(left, right, preferred_element_type=jnp.float32)


def product_left(left, right):
    return lax.dot_general(
        left, right, (((0,), (0,)), ((), ())), preferred_element_type=jnp.float32
    )


def product_right(left, right):
    return lax.dot_general(
        left, right, (((1,), (1,)), ((), ())), preferred_element_type=jnp.float32
    )


def normalize(rows, gain):
    inverse = lax.rsqrt(jnp.mean(rows * rows, axis=-1, keepdims=True) + EPS)
    return (rows * inverse * gain, inverse)


def norm_back(rows, inverse, gain, upstream):
    normed = rows * inverse
    scaled = upstream * gain
    grad_rows = inverse * (scaled - normed * jnp.mean(scaled * normed, axis=-1, keepdims=True))
    return (grad_rows, jnp.sum(upstream * normed, axis=0))


def head_pair(array, start):
    piece = lax.dynamic_slice_in_dim(array, start, 2 * HEAD, 2)
    return piece.reshape(array.shape[0], array.shape[1], 2, HEAD)


def pair_scores(query, keys, allowed, start):
    scores = jnp.einsum(
        "sqhd,skhd->shqk",
        head_pair(query, start),
        head_pair(keys, start),
        preferred_element_type=jnp.float32,
    ) * HEAD ** (-0.5)
    return jnp.where(allowed[:, None], scores, -1e30)


def attend(query, keys, values, allowed):
    groups, rows, width = query.shape

    def step(index, carry):
        mixed_all, logsum = carry
        start = index * 2 * HEAD
        scores = pair_scores(query, keys, allowed, start)
        top = jnp.max(scores, axis=-1, keepdims=True)
        lifted = jnp.exp(scores - top)
        total = jnp.sum(lifted, axis=-1, keepdims=True)
        probs = (lifted / total).astype(jnp.bfloat16)
        mixed = jnp.einsum(
            "shqk,skhd->sqhd", probs, head_pair(values, start), preferred_element_type=jnp.float32
        )
        mixed_all = lax.dynamic_update_slice_in_dim(
            mixed_all, mixed.reshape(groups, rows, 2 * HEAD).astype(jnp.bfloat16), start, 2
        )
        logsum = lax.dynamic_update_slice_in_dim(
            logsum, (top + jnp.log(total))[..., 0], index * 2, 1
        )
        return (mixed_all, logsum)

    start_state = (
        jnp.zeros((groups, rows, width), jnp.bfloat16),
        jnp.zeros((groups, width // HEAD, rows), jnp.float32),
    )
    return lax.fori_loop(0, width // (2 * HEAD), step, start_state)


def attend_back(query, keys, values, allowed, logsum, grad_mixed):
    groups, rows, width = query.shape
    length = keys.shape[1]
    scale = HEAD ** (-0.5)

    def step(index, carry):
        grad_query, grad_keys, grad_values = carry
        start = index * 2 * HEAD
        scores = pair_scores(query, keys, allowed, start)
        kept = lax.dynamic_slice_in_dim(logsum, index * 2, 2, 1)
        probs = jnp.exp(scores - kept[..., None])
        upstream = head_pair(grad_mixed, start)
        grad_probs = jnp.einsum(
            "sqhd,skhd->shqk",
            upstream,
            head_pair(values, start),
            preferred_element_type=jnp.float32,
        )
        grad_scores = (
            probs * (grad_probs - jnp.sum(probs * grad_probs, axis=-1, keepdims=True))
        ).astype(jnp.bfloat16)
        part_query = (
            jnp.einsum(
                "shqk,skhd->sqhd",
                grad_scores,
                head_pair(keys, start),
                preferred_element_type=jnp.float32,
            )
            * scale
        )
        part_keys = (
            jnp.einsum(
                "shqk,sqhd->skhd",
                grad_scores,
                head_pair(query, start),
                preferred_element_type=jnp.float32,
            )
            * scale
        )
        part_values = jnp.einsum(
            "shqk,sqhd->skhd",
            probs.astype(jnp.bfloat16),
            upstream,
            preferred_element_type=jnp.float32,
        )
        grad_query = lax.dynamic_update_slice_in_dim(
            grad_query, part_query.reshape(groups, rows, 2 * HEAD), start, 2
        )
        grad_keys = lax.dynamic_update_slice_in_dim(
            grad_keys, part_keys.reshape(groups, length, 2 * HEAD), start, 2
        )
        grad_values = lax.dynamic_update_slice_in_dim(
            grad_values, part_values.reshape(groups, length, 2 * HEAD), start, 2
        )
        return (grad_query, grad_keys, grad_values)

    start_state = (
        jnp.zeros((groups, rows, width), jnp.float32),
        jnp.zeros((groups, length, width), jnp.float32),
        jnp.zeros((groups, length, width), jnp.float32),
    )
    return lax.fori_loop(0, width // (2 * HEAD), step, start_state)


def on_device(
    layer_input,
    doc_ids,
    attn_gain,
    query_weight,
    key_weight,
    value_weight,
    out_weight,
    mlp_gain,
    gate_weight,
    up_weight,
    down_weight,
    out_grad,
):
    groups, rows, width = layer_input.shape
    length = doc_ids.shape[1]
    gathered = (
        lax.all_gather(attn_gain, ("dp", "ctx"), axis=0, tiled=True),
        lax.all_gather(query_weight, ("dp", "ctx"), axis=0, tiled=True),
        lax.all_gather(key_weight, ("dp", "ctx"), axis=0, tiled=True),
        lax.all_gather(value_weight, ("dp", "ctx"), axis=0, tiled=True),
        lax.all_gather(out_weight, ("dp", "ctx"), axis=0, tiled=True),
        lax.all_gather(mlp_gain, ("dp", "ctx"), axis=0, tiled=True),
        lax.all_gather(gate_weight, ("dp", "ctx"), axis=0, tiled=True),
        lax.all_gather(up_weight, ("dp", "ctx"), axis=0, tiled=True),
        lax.all_gather(down_weight, ("dp", "ctx"), axis=0, tiled=True),
    )
    gain_one, w_query, w_key, w_value, w_out, gain_two, w_gate, w_up, w_down = gathered
    first = lax.axis_index("ctx") * rows
    places = jnp.arange(length)
    own_ids = lax.dynamic_slice_in_dim(doc_ids, first, rows, 1)
    own_places = first + jnp.arange(rows)
    allowed = (own_ids[:, :, None] == doc_ids[:, None, :]) & (
        places[None, None, :] <= own_places[None, :, None]
    )
    inputs = layer_input.reshape(groups * rows, width).astype(jnp.float32)
    gain_attn = gain_one.astype(jnp.float32)
    normed_full, inverse_one = normalize(inputs, gain_attn)
    normed = normed_full.astype(jnp.bfloat16)
    query = product(normed, w_query).astype(jnp.bfloat16).reshape(groups, rows, width)
    keys_own = product(normed, w_key).astype(jnp.bfloat16).reshape(groups, rows, width)
    values_own = product(normed, w_value).astype(jnp.bfloat16).reshape(groups, rows, width)
    keys, values = (
        lax.all_gather(keys_own, "ctx", axis=1, tiled=True),
        lax.all_gather(values_own, "ctx", axis=1, tiled=True),
    )
    attended, logsum = attend(query, keys, values, allowed)
    attended_rows = attended.reshape(groups * rows, width)
    middle = inputs + product(attended_rows, w_out)
    gain_mlp = gain_two.astype(jnp.float32)
    normed_two_full, inverse_two = normalize(middle, gain_mlp)
    normed_two = normed_two_full.astype(jnp.bfloat16)
    gate = product(normed_two, w_gate)
    upward = product(normed_two, w_up)
    sigma = jax.nn.sigmoid(gate)
    hidden = (gate * sigma * upward).astype(jnp.bfloat16)
    layer_output = (middle + product(hidden, w_down)).astype(jnp.bfloat16)
    gathered_back = (
        lax.all_gather(attn_gain, ("dp", "ctx"), axis=0, tiled=True),
        lax.all_gather(query_weight, ("dp", "ctx"), axis=0, tiled=True),
        lax.all_gather(key_weight, ("dp", "ctx"), axis=0, tiled=True),
        lax.all_gather(value_weight, ("dp", "ctx"), axis=0, tiled=True),
        lax.all_gather(out_weight, ("dp", "ctx"), axis=0, tiled=True),
        lax.all_gather(mlp_gain, ("dp", "ctx"), axis=0, tiled=True),
        lax.all_gather(gate_weight, ("dp", "ctx"), axis=0, tiled=True),
        lax.all_gather(up_weight, ("dp", "ctx"), axis=0, tiled=True),
        lax.all_gather(down_weight, ("dp", "ctx"), axis=0, tiled=True),
    )
    gain_one, w_query, w_key, w_value, w_out, gain_two, w_gate, w_up, w_down = gathered_back
    upstream = out_grad.reshape(groups * rows, width)
    down_grad = product_left(hidden, upstream)
    grad_hidden = product_right(upstream, w_down)
    grad_gate = (grad_hidden * upward * sigma * (1.0 + gate * (1.0 - sigma))).astype(jnp.bfloat16)
    grad_up = (grad_hidden * gate * sigma).astype(jnp.bfloat16)
    gate_grad = product_left(normed_two, grad_gate)
    up_grad = product_left(normed_two, grad_up)
    grad_normed_two = product_right(grad_gate, w_gate) + product_right(grad_up, w_up)
    grad_middle, mlp_gain_grad = norm_back(
        middle, inverse_two, gain_two.astype(jnp.float32), grad_normed_two
    )
    grad_middle = grad_middle + upstream.astype(jnp.float32)
    grad_branch = grad_middle.astype(jnp.bfloat16)
    out_proj_grad = product_left(attended_rows, grad_branch)
    grad_attended = (
        product_right(grad_branch, w_out).astype(jnp.bfloat16).reshape(groups, rows, width)
    )
    grad_query, grad_keys_all, grad_values_all = attend_back(
        query, keys, values, allowed, logsum, grad_attended
    )
    grad_keys, grad_values = (
        lax.psum_scatter(
            grad_keys_all.astype(jnp.bfloat16), "ctx", scatter_dimension=1, tiled=True
        ).astype(jnp.float32),
        lax.psum_scatter(
            grad_values_all.astype(jnp.bfloat16), "ctx", scatter_dimension=1, tiled=True
        ).astype(jnp.float32),
    )
    grad_query = grad_query.astype(jnp.bfloat16).reshape(groups * rows, width)
    grad_keys = grad_keys.astype(jnp.bfloat16).reshape(groups * rows, width)
    grad_values = grad_values.astype(jnp.bfloat16).reshape(groups * rows, width)
    query_grad = product_left(normed, grad_query)
    key_grad = product_left(normed, grad_keys)
    value_grad = product_left(normed, grad_values)
    grad_normed = (
        product_right(grad_query, w_query)
        + product_right(grad_keys, w_key)
        + product_right(grad_values, w_value)
    )
    grad_inputs, attn_gain_grad = norm_back(
        inputs, inverse_one, gain_one.astype(jnp.float32), grad_normed
    )
    input_grad = (grad_middle + grad_inputs).reshape(groups, rows, width)
    shares = (
        lax.psum_scatter(attn_gain_grad, ("dp", "ctx"), scatter_dimension=0, tiled=True),
        lax.psum_scatter(query_grad, ("dp", "ctx"), scatter_dimension=0, tiled=True),
        lax.psum_scatter(key_grad, ("dp", "ctx"), scatter_dimension=0, tiled=True),
        lax.psum_scatter(value_grad, ("dp", "ctx"), scatter_dimension=0, tiled=True),
        lax.psum_scatter(out_proj_grad, ("dp", "ctx"), scatter_dimension=0, tiled=True),
        lax.psum_scatter(mlp_gain_grad, ("dp", "ctx"), scatter_dimension=0, tiled=True),
        lax.psum_scatter(gate_grad, ("dp", "ctx"), scatter_dimension=0, tiled=True),
        lax.psum_scatter(up_grad, ("dp", "ctx"), scatter_dimension=0, tiled=True),
        lax.psum_scatter(down_grad, ("dp", "ctx"), scatter_dimension=0, tiled=True),
    )
    return (
        layer_output.reshape(groups, rows, width),
        input_grad,
        shares[0],
        shares[1],
        shares[2],
        shares[3],
        shares[4],
        shares[5],
        shares[6],
        shares[7],
        shares[8],
    )


def solution(mesh):
    placed = (
        P("dp", "ctx", None),
        P("dp", None),
        P(("dp", "ctx")),
        P(("dp", "ctx"), None),
        P(("dp", "ctx"), None),
        P(("dp", "ctx"), None),
        P(("dp", "ctx"), None),
        P(("dp", "ctx")),
        P(("dp", "ctx"), None),
        P(("dp", "ctx"), None),
        P(("dp", "ctx"), None),
        P("dp", "ctx", None),
    )
    return jax.shard_map(
        on_device,
        mesh=mesh,
        in_specs=placed,
        out_specs=(
            P("dp", "ctx", None),
            P("dp", "ctx", None),
            P(("dp", "ctx")),
            P(("dp", "ctx"), None),
            P(("dp", "ctx"), None),
            P(("dp", "ctx"), None),
            P(("dp", "ctx"), None),
            P(("dp", "ctx")),
            P(("dp", "ctx"), None),
            P(("dp", "ctx"), None),
            P(("dp", "ctx"), None),
        ),
        check_vma=False,
    )
```

profile of v0, /device:TPU:19, one launch (start us, length us, event | category | flops | bytes accessed | tf_op | source)
XLA Modules:
  0.0 2604.8 jit_solution(7120969927249212955)
XLA Ops:
  11.1 39.5 %all-reduce.5 = (bf16[1024]{0:T(1024)(128)(2,1)S(1)}, bf16[1024]{0:T(1024)(128)(2,1)S(1)}) all-reduce(bf16[1024]{0:T(1024)(128)(2,1)S(1)} %dynamic-update-slice, bf16[1024]{0:T(1024)(128)(2,1)S(1)} %dynamic-update-slice.1), channel_id=1, replica_groups=mesh['dp'=4,'ctx'=8] {'dp','ctx'}, use_global_device_ids=true, to_apply=%add | all-reduce | flops 2048 | bytes 8192
  53.1 14.4 all-gather.10.cloned.1.call-done
  67.5 2.3 convolution_convert_fusion.4
  70.9 55.0 %all-gather.16.cloned.1.call-done = bf16[1024,1024]{1,0:T(8,128)(2,1)} async-done(((bf16[32,1024]{1,0:T(8,128)(2,1)}), bf16[1024,1024]{1,0:T(8,128)(2,1)}) %all-gather.16.cloned.1.call-update) | async-done | bytes 2097168 | tf_op jit(solution)/shard_map/all_gather | solution.py:167
  125.9 2.3 convolution_convert_fusion.2
  132.8 51.4 %all-gather.14.cloned.1.call-done = bf16[1024,1024]{1,0:T(8,128)(2,1)} async-done(((bf16[32,1024]{1,0:T(8,128)(2,1)}), bf16[1024,1024]{1,0:T(8,128)(2,1)}) %all-gather.14.cloned.1.call-update) | async-done | bytes 2097168 | tf_op jit(solution)/shard_map/all_gather | solution.py:166
  184.2 2.3 convolution_convert_fusion.3
  187.5 72.0 %all-gather.12.cloned.1.call-done = bf16[2,1024,1024]{1,2,0:T(8,128)(2,1)} async-done(((bf16[2,128,1024]{1,2,0:T(8,128)(2,1)}), bf16[2,1024,1024]{1,2,0:T(8,128)(2,1)}) %all-gather.12.cloned.1.call-update) | async-done | bytes 4194320 | tf_op jit(solution)/shard_map/all_gather | solution.py:192
  259.6 75.7 %all-gather.18.cloned.1.call-done = bf16[2,1024,1024]{1,2,0:T(8,128)(2,1)} async-done(((bf16[2,128,1024]{1,2,0:T(8,128)(2,1)}), bf16[2,1024,1024]{1,2,0:T(8,128)(2,1)}) %all-gather.18.cloned.1.call-update) | async-done | bytes 4194320 | tf_op jit(solution)/shard_map/all_gather | solution.py:191
  336.1 56.5 %while.38 = (s32[]{:T(128)}, bf16[2,128,1024]{2,1,0:T(8,128)(2,1)}, f32[2,16,128]{2,1,0:T(8,128)S(1)}, bf16[2,1024,1024]{1,2,0:T(8,128)(2,1)}, bf16[2,128,1024]{...) while((s32[]{:T(128)}, bf16[2,128,1024]{2,1,0:T(8,128)(2,1)}, ...), condition=%wide.region_4.5_spmd.clone, body=%wide.region_1.4_spmd.clone.sunk | while | flops 141065728 | bytes 11166969 | solution.py:81
  336.1 2.2 constant_dynamic-slice_fusion.16
  343.3 2.1 constant_dynamic-slice_fusion.16
  350.3 2.1 constant_dynamic-slice_fusion.16
  357.4 2.1 constant_dynamic-slice_fusion.16
  371.5 2.1 constant_dynamic-slice_fusion.16
  378.5 2.1 constant_dynamic-slice_fusion.16
  385.6 2.1 constant_dynamic-slice_fusion.16
  394.0 2.6 multiply_reduce_fusion.5
  396.7 77.6 %all-gather.22.cloned.1.call-done = bf16[1024,4096]{1,0:T(8,128)(2,1)} async-done(((bf16[32,4096]{1,0:T(8,128)(2,1)}), bf16[1024,4096]{1,0:T(8,128)(2,1)}) %all-gather.22.cloned.1.call-update) | async-done | bytes 8388624 | tf_op jit(solution)/shard_map/all_gather | solution.py:171
  474.3 7.7 fusion.17
  482.0 71.3 %all-gather.24.cloned.1.call-done = bf16[1024,4096]{1,0:T(8,128)(2,1)} async-done(((bf16[32,4096]{1,0:T(8,128)(2,1)}), bf16[1024,4096]{1,0:T(8,128)(2,1)}) %all-gather.24.cloned.1.call-update) | async-done | bytes 8388624 | tf_op jit(solution)/shard_map/all_gather | solution.py:172
  553.3 7.7 fusion.18
  561.0 71.3 %all-gather.26.cloned.1.call-done = bf16[4096,1024]{1,0:T(8,128)(2,1)} async-done(((bf16[128,1024]{1,0:T(8,128)(2,1)}), bf16[4096,1024]{1,0:T(8,128)(2,1)}) %all-gather.26.cloned.1.call-update) | async-done | bytes 8388624 | tf_op jit(solution)/shard_map/all_gather | solution.py:173
  632.3 12.5 multiply_convert_fusion.1
  644.9 7.3 fusion.19
  652.2 2.6 multiply_reduce_fusion.1
  658.4 2.5 broadcast.154.clone
  660.9 2.6 broadcast.154.clone2
  664.3 99.2 %while.39 = (s32[]{:T(128)}, bf16[2,128,1024]{2,1,0:T(8,128)(2,1)}, bf16[2,1024,1024]{2,1,0:T(8,128)(2,1)}, bf16[2,1024,1024]{2,1,0:T(8,128)(2,1)}, bf16[2,1024,...) while((s32[]{:T(128)}, bf16[2,128,1024]{2,1,0:T(8,128)(2,1)}, ...), condition=%wide.region_9.0_spmd.clone, body=%wide.region_7.0_spmd.clone.sunk | while | flops 341376512 | bytes 38882672 | solution.py:145
  764.7 2.8 convolution_bitcast_fusion.2
  768.8 2.7 fusion.12
  771.9 78.3 %reduce-scatter.10.cloned.1.call-done = bf16[2,128,1024]{2,1,0:T(8,128)(2,1)} async-done(((bf16[2,1024,1024]{2,1,0:T(8,128)(2,1)}), bf16[2,128,1024]{2,1,0:T(8,128)(2,1)}) %reduce-scatter.10.cloned.1.call-update) | async-done | bytes 524304 | tf_op jit(solution)/shard_map/reduce_scatter | solution.py:238
  850.2 3.8 convolution_bitcast_fusion.1
  854.1 88.0 %reduce-scatter.12.cloned.1.call-done = bf16[2,128,1024]{2,1,0:T(8,128)(2,1)} async-done(((bf16[2,1024,1024]{2,1,0:T(8,128)(2,1)}), bf16[2,128,1024]{2,1,0:T(8,128)(2,1)}) %reduce-scatter.12.cloned.1.call-update) | async-done | bytes 524304 | tf_op jit(solution)/shard_map/reduce_scatter | solution.py:241
  942.1 3.9 convolution_bitcast_fusion
  947.0 9.7 fusion.21
  956.8 9.7 fusion.22
  967.6 9.7 fusion.23
  977.4 2.5 fusion.20
  979.9 6.7 fusion.11
  989.5 40.0 %all-reduce.4 = (f32[1024]{0:T(1024)S(1)}, f32[1024]{0:T(1024)S(1)}) all-reduce(f32[1024]{0:T(1024)S(1)} %get-tuple-element.554, f32[1024]{0:T(1024)S(1)} %get-tuple-element.552), channel_id=4, replica_groups=mesh['dp'=4,'ctx'=8] {'dp','ctx'}, use_global_device_ids=true, to_apply=%region_14.15.clone | all-reduce | flops 2048 | bytes 16384
  1031.9 50.6 %reduce-scatter.14.cloned.1.call-done = f32[32,1024]{1,0:T(8,128)} async-done(((f32[1024,1024]{1,0:T(8,128)}), f32[32,1024]{1,0:T(8,128)}) %reduce-scatter.14.cloned.1.call-update) | async-done | bytes 131088 | tf_op jit(solution)/shard_map/reduce_scatter | solution.py:262
  1082.4 143.3 %reduce-scatter.20.cloned.1.call-done = f32[32,1024]{1,0:T(8,128)} async-done(((f32[1024,1024]{1,0:T(8,128)}), f32[32,1024]{1,0:T(8,128)}) %reduce-scatter.20.cloned.1.call-update) | async-done | bytes 131088 | tf_op jit(solution)/shard_map/reduce_scatter | solution.py:265
  1225.7 144.2 %reduce-scatter.16.cloned.1.call-done = f32[32,1024]{1,0:T(8,128)} async-done(((f32[1024,1024]{1,0:T(8,128)}), f32[32,1024]{1,0:T(8,128)}) %reduce-scatter.16.cloned.1.call-update) | async-done | bytes 131088 | tf_op jit(solution)/shard_map/reduce_scatter | solution.py:263
  1369.9 144.2 %reduce-scatter.18.cloned.1.call-done = f32[32,1024]{1,0:T(8,128)} async-done(((f32[1024,1024]{1,0:T(8,128)}), f32[32,1024]{1,0:T(8,128)}) %reduce-scatter.18.cloned.1.call-update) | async-done | bytes 131088 | tf_op jit(solution)/shard_map/reduce_scatter | solution.py:264
  1514.1 363.3 %reduce-scatter.22.cloned.1.call-done = f32[32,4096]{1,0:T(8,128)} async-done(((f32[1024,4096]{1,0:T(8,128)}), f32[32,4096]{1,0:T(8,128)}) %reduce-scatter.22.cloned.1.call-update) | async-done | bytes 524304 | tf_op jit(solution)/shard_map/reduce_scatter | solution.py:267
  1877.5 360.1 %reduce-scatter.24.cloned.1.call-done = f32[32,4096]{1,0:T(8,128)} async-done(((f32[1024,4096]{1,0:T(8,128)}), f32[32,4096]{1,0:T(8,128)}) %reduce-scatter.24.cloned.1.call-update) | async-done | bytes 524304 | tf_op jit(solution)/shard_map/reduce_scatter | solution.py:268
  2237.6 360.1 %reduce-scatter.26.cloned.1.call-done = f32[128,1024]{1,0:T(8,128)} async-done(((f32[4096,1024]{1,0:T(8,128)}), f32[128,1024]{1,0:T(8,128)}) %reduce-scatter.26.cloned.1.call-update) | async-done | bytes 524304 | tf_op jit(solution)/shard_map/reduce_scatter | solution.py:269
  (371 shorter events, 169.7 us)
Async XLA Ops:
  7.2 60.3 %all-gather.10.cloned.1.call-start = ((), (), s32[]{:S(2)}) async-start(), calls=%async_computation.9 | async-start | bytes 2162688 | tf_op jit(solution)/shard_map/all_gather | solution.py:168
  7.9 118.0 %all-gather.16.cloned.1.call-start = ((), (), s32[]{:S(2)}) async-start(), calls=%async_computation.12 | async-start | bytes 2162688 | tf_op jit(solution)/shard_map/all_gather | solution.py:167
  8.7 175.6 %all-gather.14.cloned.1.call-start = ((), (), s32[]{:S(2)}) async-start(), calls=%async_computation.11 | async-start | bytes 2162688 | tf_op jit(solution)/shard_map/all_gather | solution.py:166
  9.4 250.2 %all-gather.12.cloned.1.call-start = ((), (), s32[]{:S(2)}) async-start(), calls=%async_computation.10 | async-start | bytes 4718592 | tf_op jit(solution)/shard_map/all_gather | solution.py:192
  51.8 17.9 copy-start.24
  70.8 264.5 %all-gather.18.cloned.1.call-start = ((), (), s32[]{:S(2)}) async-start(), calls=%async_computation.13 | async-start | bytes 4718592 | tf_op jit(solution)/shard_map/all_gather | solution.py:191
  128.2 4.6 copy-start.23
  129.2 264.8 %all-gather.20.cloned.1.call-start = ((), (), s32[]{:S(2)}) async-start(), calls=%async_computation.14 | async-start | bytes 2162688 | tf_op jit(solution)/shard_map/all_gather | solution.py:169
  129.8 344.5 %all-gather.22.cloned.1.call-start = ((), (), s32[]{:S(2)}) async-start(), calls=%async_computation.15 | async-start | bytes 8650752 | tf_op jit(solution)/shard_map/all_gather | solution.py:171
  130.5 422.8 %all-gather.24.cloned.1.call-start = ((), (), s32[]{:S(2)}) async-start(), calls=%async_computation.16 | async-start | bytes 8650752 | tf_op jit(solution)/shard_map/all_gather | solution.py:172
  131.3 501.0 %all-gather.26.cloned.1.call-start = ((), (), s32[]{:S(2)}) async-start(), calls=%async_computation.17 | async-start | bytes 8650752 | tf_op jit(solution)/shard_map/all_gather | solution.py:173
  132.0 718.2 %reduce-scatter.10.cloned.1.call-start = ((), (), s32[]{:S(2)}) async-start(), calls=%async_computation.18 | async-start | bytes 4718592 | tf_op jit(solution)/shard_map/reduce_scatter | solution.py:238
  336.1 57.8 %copy-start.3 = (bf16[2,128,1024]{2,1,0:T(8,128)(2,1)S(1)}, bf16[2,128,1024]{2,1,0:T(8,128)(2,1)}, u32[]{:S(2)}) copy-start(bf16[2,128,1024]{2,1,0:T(8,128)(2,1)} %param.16) | copy-start | bytes 1572868
  396.5 258.3 %copy-start.7 = (f32[256,1024]{1,0:T(8,128)}, f32[256,1024]{1,0:T(8,128)S(1)}, u32[]{:S(2)}) copy-start(f32[256,1024]{1,0:T(8,128)S(1)} %get-tuple-element.616) | copy-start | bytes 3145732
  396.7 156.6 %copy-start.10 = (bf16[256,1024]{1,0:T(8,128)(2,1)}, bf16[256,1024]{1,0:T(8,128)(2,1)S(1)}, u32[]{:S(2)}) copy-start(bf16[256,1024]{1,0:T(8,128)(2,1)S(1)} %multiply_convert_fusion.5) | copy-start | bytes 1572868
  482.0 150.3 %copy-start.19 = (bf16[2,128,1024]{2,1,0:T(8,128)(2,1)S(1)}, bf16[2,128,1024]{2,1,0:T(8,128)(2,1)}, u32[]{:S(2)}) copy-start(bf16[2,128,1024]{2,1,0:T(8,128)(2,1)} %param.27) | copy-start | bytes 1572868
  644.9 7.3 copy-start.22
  644.9 7.3 copy-start.21
  644.9 7.3 copy-start.26
  654.9 2.0 copy-start.9
  667.9 2.2 copy-start.1
  674.0 1.4 copy-start.2
  680.3 2.2 copy-start.1
  686.4 1.5 copy-start.2
  692.7 2.2 copy-start.1
  698.8 1.5 copy-start.2
  705.2 2.2 copy-start.1
  717.5 2.2 copy-start.1
  729.9 2.2 copy-start.1
  736.0 1.4 copy-start.2
  742.3 2.2 copy-start.1
  748.4 1.4 copy-start.2
  754.7 2.2 copy-start.1
  760.8 1.4 copy-start.2
  763.5 178.7 %reduce-scatter.12.cloned.1.call-start = ((), (), s32[]{:S(2)}) async-start(), calls=%async_computation.19 | async-start | bytes 4718592 | tf_op jit(solution)/shard_map/reduce_scatter | solution.py:241
  764.2 318.2 %reduce-scatter.14.cloned.1.call-start = ((), (), s32[]{:S(2)}) async-start(), calls=%async_computation.20 | async-start | bytes 4325376 | tf_op jit(solution)/shard_map/reduce_scatter | solution.py:262
  767.5 458.2 %reduce-scatter.20.cloned.1.call-start = ((), (), s32[]{:S(2)}) async-start(), calls=%async_computation.23 | async-start | bytes 4325376 | tf_op jit(solution)/shard_map/reduce_scatter | solution.py:265
  771.6 598.3 %reduce-scatter.16.cloned.1.call-start = ((), (), s32[]{:S(2)}) async-start(), calls=%async_computation.21 | async-start | bytes 4325376 | tf_op jit(solution)/shard_map/reduce_scatter | solution.py:263
  854.1 660.1 %reduce-scatter.18.cloned.1.call-start = ((), (), s32[]{:S(2)}) async-start(), calls=%async_computation.22 | async-start | bytes 4325376 | tf_op jit(solution)/shard_map/reduce_scatter | solution.py:264
  946.0 931.5 %reduce-scatter.22.cloned.1.call-start = ((), (), s32[]{:S(2)}) async-start(), calls=%async_computation.24 | async-start | bytes 17301504 | tf_op jit(solution)/shard_map/reduce_scatter | solution.py:267
  956.8 1280.8 %reduce-scatter.24.cloned.1.call-start = ((), (), s32[]{:S(2)}) async-start(), calls=%async_computation.25 | async-start | bytes 17301504 | tf_op jit(solution)/shard_map/reduce_scatter | solution.py:268
  966.6 1631.1 %reduce-scatter.26.cloned.1.call-start = ((), (), s32[]{:S(2)}) async-start(), calls=%async_computation.26 | async-start | bytes 17301504 | tf_op jit(solution)/shard_map/reduce_scatter | solution.py:269
  977.3 2.5 copy-start.8
  977.3 2.6 copy-start.14
  979.9 6.7 copy-start.15
  979.9 6.7 copy-start.18
  986.7 1.8 copy-start.17
  986.7 1.8 copy-start.25
  (18 other events, 22.6 us)
Sparse Core Ops, SparseCore 0:
  11.0 56.4 all-gather.9
  70.4 55.3 all-gather.15
  128.9 55.3 all-gather.13
  186.7 72.8 all-gather.11
  262.1 73.1 all-gather.17
  338.1 55.7 all-gather.19
  396.9 77.3 all-gather.21
  477.3 75.9 all-gather.23
  556.3 75.9 all-gather.25
  763.6 86.5 reduce-scatter.9
  854.3 87.8 reduce-scatter.11
  944.8 137.5 reduce-scatter.13
  1085.3 140.3 reduce-scatter.19
  1228.4 141.4 reduce-scatter.15
  1372.6 141.4 reduce-scatter.17
  1516.9 360.5 reduce-scatter.21
  1880.2 357.3 reduce-scatter.23
  2240.3 357.3 reduce-scatter.25
where the time goes:
time: 2620 us; the launch traced here: 2600 us
  waiting for transfers between devices  2230 us (85%)
  matrix products  155 us (6%)
  local copies, waits for them, and re-layouts  108 us (4%)
  blocking collectives  79.4 us (3%)
    reduce_scatter x1, waiting for transfers between devices, on_device(): lax.psum_scatter(gate_grad, ('dp', 'ctx'), scatter_dimension=0, tiled=True)  363 us
    reduce_scatter x1, waiting for transfers between devices, on_device(): lax.psum_scatter(up_grad, ('dp', 'ctx'), scatter_dimension=0, tiled=True)  360 us
    reduce_scatter x1, waiting for transfers between devices, on_device(): lax.psum_scatter(down_grad, ('dp', 'ctx'), scatter_dimension=0, tiled=True)  360 us
    reduce_scatter x1, waiting for transfers between devices, on_device(): lax.psum_scatter(value_grad, ('dp', 'ctx'), scatter_dimension=0, tiled=True)  144 us
    reduce_scatter x1, waiting for transfers between devices, on_device(): lax.psum_scatter(key_grad, ('dp', 'ctx'), scatter_dimension=0, tiled=True)  144 us
    reduce_scatter x1, waiting for transfers between devices, on_device(): lax.psum_scatter(out_proj_grad, ('dp', 'ctx'), scatter_dimension=0, tiled...  143 us
    reduce_scatter x1, waiting for transfers between devices, on_device(): lax.psum_scatter(grad_values_all.astype(jnp.bfloat16), 'ctx', scatter_dim...  88 us
    unnamed x2, blocking collectives  79.4 us
  transfers between devices with their start and end apart: 18, of which 18 were waited for; matrix products, arithmetic and copies ran while one was open for 6% of the time, Pallas kernels for 0%

commit v1 on v0

--- a/solution.py
+++ b/solution.py
@@ -1,25 +1,973 @@
+import functools
+
 import jax
 import jax.numpy as jnp
 from jax import lax
+from jax.experimental import pallas as pl
+from jax.experimental.pallas import tpu as pltpu
 from jax.sharding import PartitionSpec as P
 
 HEAD = 64
 
 
 EPS = 1e-05
+MESH = pl.DeviceIdType.MESH
+F32 = jnp.float32
+BF16 = jnp.bfloat16
+LOG2E = 1.4426950408889634
+ANY = pl.BlockSpec(memory_space=pl.ANY)
+VMEM = pl.BlockSpec(memory_space=pltpu.VMEM)
+
+
+class Wires:
+    def __init__(self, send, recv):
+        dp, ctx = lax.axis_index("dp"), lax.axis_index("ctx")
+        self.x, self.y = ctx % 2, dp // 2
+        self.z, self.k = ctx // 2, dp % 2
+        self.send, self.recv = send, recv
+        self.used = 0
+
+    def slots(self, count):
+        first = self.used
+        self.used += count
+        return first
+
+    def at(self, x, y, z, k):
+        return (2 * y + k, 2 * z + x)
+
+    def copy(self, source, target, device, slot, recv_slot=None):
+        return pltpu.make_async_remote_copy(
+            src_ref=source,
+            dst_ref=target,
+            send_sem=self.send.at[slot],
+            recv_sem=self.recv.at[slot if recv_slot is None else recv_slot],
+            device_id=device,
+            device_id_type=MESH,
+        )
+
+    def greet(self, peers):
+        barrier = pltpu.get_barrier_semaphore()
+        for peer in peers:
+            pl.semaphore_signal(barrier, inc=1, device_id=peer, device_id_type=MESH)
+        pl.semaphore_wait(barrier, len(peers))
+
+    def group_peers(self):
+        x, y, z, k = self.x, self.y, self.z, self.k
+        return [self.at(1 - x, y, z, k), self.at(x, y, z, 1 - k), self.at(1 - x, y, z, 1 - k)]
+
+    def line_peers(self):
+        x, y, z, k = self.x, self.y, self.z, self.k
+        return [self.at(x, y, (z + i) % 4, k) for i in (1, 2, 3)]
+
+    def cross_peers(self):
+        x, y, z, k = self.x, self.y, self.z, self.k
+        return [self.at(x, y, (z + i) % 4, 1 - k) for i in (1, 2, 3)]
+
+    def pair_peer(self):
+        return self.at(self.x, 1 - self.y, self.z, self.k)
+
+
+class Spread:
+    def __init__(self, wires, block, own=None):
+        self.w, self.block, self.own = wires, block, own
+        self.lines, self.pairs = wires.slots(4), wires.slots(4)
+
+    def line(self, i, z, own=None):
+        w = self.w
+        ref = self.block(w.y, z)
+        target = w.at(w.x, w.y, (w.z + i) % 4, w.k)
+        return w.copy(ref if own is None else own, ref, target, self.lines + i)
+
+    def pair(self, i, y, own=None):
+        w = self.w
+        ref = self.block(y, (w.z + 4 - i) % 4)
+        return w.copy(ref if own is None else own, ref, w.pair_peer(), self.pairs + i)
+
+    def start(self):
+        for i in (2, 1, 3):
+            self.line(i, self.w.z, self.own).start()
+        self.pair(0, self.w.y, self.own).start()
+
+    def forward(self, i):
+        self.line(i, (self.w.z + 4 - i) % 4).wait_recv()
+        self.pair(i, self.w.y).start()
+
+    def arrive(self, i):
+        self.pair(i, 1 - self.w.y).wait_recv()
+
+    def drain(self):
+        for i in (1, 2, 3):
+            self.line(i, self.w.z, self.own).wait_send()
+        for i in range(4):
+            self.pair(i, self.w.y).wait_send()
+
+
+class Share:
+    def __init__(self, wires, block, own=None):
+        self.w, self.block, self.own = wires, block, own
+        self.first = wires.slots(3)
+
+    def piece(self, i):
+        w = self.w
+        core, across = w.at(w.x, w.y, w.z, 1 - w.k), w.at(1 - w.x, w.y, w.z, w.k)
+        ref = self.block(w.x if i < 2 else 1 - w.x, w.k)
+        source = ref if self.own is None or i == 2 else self.own
+        return w.copy(source, ref, across if i == 0 else core, self.first + i)
+
+    def landed(self, i):
+        w = self.w
+        ref = self.block(*[(1 - w.x, w.k), (w.x, 1 - w.k), (1 - w.x, 1 - w.k)][i])
+        return w.copy(ref, ref, w.at(w.x, w.y, w.z, 1 - w.k), self.first + i)
+
+    def start(self):
+        self.piece(0).start()
+        self.piece(1).start()
+
+    def forward(self):
+        self.landed(0).wait_recv()
+        self.piece(2).start()
+
+    def arrive(self):
+        self.landed(1).wait_recv()
+        self.landed(2).wait_recv()
+
+    def drain(self):
+        for i in range(3):
+            self.piece(i).wait_send()
+
+
+class Deal:
+    def __init__(self, wires, outgoing, incoming):
+        self.w, self.outgoing, self.incoming = wires, outgoing, incoming
+        self.first = wires.slots(3)
+
+    def mate(self, i):
+        w = self.w
+        return [(1 - w.x, w.k), (w.x, 1 - w.k), (1 - w.x, 1 - w.k)][i]
+
+    def piece(self, i):
+        w = self.w
+        x, k = self.mate(i)
+        return w.copy(
+            self.outgoing(x, k), self.incoming(w.x, w.k), w.at(x, w.y, w.z, k), self.first + i
+        )
+
+    def landed(self, i):
+        x, k = self.mate(i)
+        ref = self.incoming(x, k)
+        return self.w.copy(ref, ref, self.w.at(x, self.w.y, self.w.z, k), self.first + i)
+
+    def start(self):
+        for i in range(3):
+            self.piece(i).start()
+
+    def arrive(self):
+        for i in range(3):
+            self.landed(i).wait_recv()
+
+    def drain(self):
+        for i in range(3):
+            self.piece(i).wait_send()
+
+
+class Visit:
+    def __init__(self, wires, home, full, local):
+        self.w, self.home, self.full, self.local = wires, home, full, local
+        self.first = wires.slots(2)
+        w = wires
+        self.own = [jnp.logical_and(w.z == 2 * w.k + j, w.z % 2 == w.k) for j in range(2)]
+
+    def piece(self, j):
+        w = self.w
+        return w.copy(
+            self.home.at[j],
+            self.full(w.x, w.z),
+            w.at(w.x, w.y, 2 * w.k + j, w.z % 2),
+            self.first + j,
+            self.first + w.z // 2,
+        )
+
+    def stay(self, j):
+        return pltpu.make_async_copy(self.home.at[j], self.full(self.w.x, self.w.z), self.local)
+
+    def landed(self, i):
+        w = self.w
+        ref = self.full(w.x, w.k + 2 * i)
+        return w.copy(ref, ref, w.pair_peer(), self.first + i)
+
+    def here(self, i):
+        w = self.w
+        return jnp.logical_and(w.k + 2 * i == w.z, w.z // 2 == w.k)
+
+    def start(self):
+        for j in range(2):
+            pl.when(self.own[j])(lambda: self.stay(j).start())
+            pl.when(jnp.logical_not(self.own[j]))(lambda: self.piece(j).start())
+
+    def arrive(self):
+        for j in range(2):
+            pl.when(self.own[j])(lambda: self.stay(j).wait())
+        for i in range(2):
+            pl.when(jnp.logical_not(self.here(i)))(lambda: self.landed(i).wait_recv())
+
+    def drain(self):
+        for j in range(2):
+            pl.when(jnp.logical_not(self.own[j]))(lambda: self.piece(j).wait_send())
+
+
+class Return:
+    def __init__(self, wires, done, home, local):
+        self.w, self.done, self.home, self.local = wires, done, home, local
+        self.first = wires.slots(2)
+
+    def own(self, i):
+        w = self.w
+        return jnp.logical_and(2 * i + w.k == w.z, w.z // 2 == w.k)
+
+    def piece(self, i):
+        w = self.w
+        return w.copy(
+            self.done.at[i],
+            self.home.at[w.z % 2],
+            w.at(w.x, w.y, 2 * i + w.k, w.z // 2),
+            self.first + i,
+            self.first + w.z % 2,
+        )
+
+    def stay(self, i):
+        return pltpu.make_async_copy(self.done.at[i], self.home.at[self.w.z % 2], self.local)
+
+    def here(self, j):
+        w = self.w
+        return jnp.logical_and(2 * w.k + j == w.z, w.z % 2 == w.k)
+
+    def landed(self, j):
+        ref = self.home.at[j]
+        return self.w.copy(ref, ref, self.w.pair_peer(), self.first + j)
+
+    def start(self):
+        for i in range(2):
+            pl.when(self.own(i))(lambda: self.stay(i).start())
+            pl.when(jnp.logical_not(self.own(i)))(lambda: self.piece(i).start())
+
+    def arrive(self):
+        for i in range(2):
+            pl.when(self.own(i))(lambda: self.stay(i).wait())
+        for j in range(2):
+            pl.when(jnp.logical_not(self.here(j)))(lambda: self.landed(j).wait_recv())
+
+    def drain(self):
+        for i in range(2):
+            pl.when(jnp.logical_not(self.own(i)))(lambda: self.piece(i).wait_send())
+
+
+def sems(count):
+    return [
+        pltpu.SemaphoreType.DMA((count,)),
+        pltpu.SemaphoreType.DMA((count,)),
+        pltpu.SemaphoreType.DMA,
+    ]
+
+
+def kernel_call(body, name, outs, ins, out_specs, scratch, collective=None):
+    return pl.pallas_call(
+        body,
+        name=name,
+        out_shape=outs,
+        in_specs=ins,
+        out_specs=out_specs,
+        scratch_shapes=scratch,
+        compiler_params=pltpu.CompilerParams(
+            collective_id=collective,
+            has_side_effects=collective is not None,
+            vmem_limit_bytes=58 << 20,
+        ),
+    )
+
+
+def shaped(*shape, dtype=BF16):
+    return jax.ShapeDtypeStruct(shape, dtype)
+
+
+def pack_rows(columns, shards, packed):
+    for rank in range(4):
+        at = 0
+        for shard in shards:
+            for start, width in columns(rank):
+                packed[rank, :, at : at + width] = shard[:, start : start + width]
+                at += width
+
+
+def head_columns(rank):
+    return [(256 * rank, 256)]
+
+
+def hidden_columns(rank):
+    x, k = rank // 2, rank % 2
+    return [(128 * (8 * (2 * y + k) + 2 * z + x), 128) for y in range(2) for z in range(4)]
+
+
+def gather_body(
+    rows, cots, ids, wq, wk, wv, wo, wg, wu, wd, gains,
+    rows_all, cots_all, ids_all, heads_all, out_all, hidden_all, down_all, gains_all,
+    heads_pack, hidden_pack, send, recv, local,
+):
+    w = Wires(send, recv)
+    x, y, z, k = w.x, w.y, w.z, w.k
+    w.greet(w.group_peers() + w.line_peers() + w.cross_peers() + [w.pair_peer()])
+
+    def stay(source, target, index):
+        copy = pltpu.make_async_copy(source, target, local.at[index])
+        copy.start()
+        return copy
+
+    visit_rows = Visit(w, rows, lambda x, z: rows_all.at[z // 2, z % 2, x], local.at[0])
+    visit_rows.start()
+    pack_rows(head_columns, (wq, wk, wv), heads_pack)
+    rank = 2 * x + k
+    deal_heads = Deal(
+        w, lambda x, k: heads_pack.at[2 * x + k], lambda sx, sk: heads_all.at[y, sk, z, sx]
+    )
+    deal_heads.start()
+    stays = [
+        stay(heads_pack.at[rank], heads_all.at[y, k, z, x], 1),
+        stay(wo, out_all.at[y, k, z, x], 2),
+        stay(gains, gains_all.at[y, k, z, x], 3),
+        stay(wd, down_all.at[y, z], 4),
+        stay(ids, ids_all.at[k], 5),
+    ]
+    slot = w.slots(1)
+    swap = w.copy(ids, ids_all.at[k], w.at(x, y, z, 1 - k), slot)
+    swap.start()
+    spread_gains = Spread(w, lambda y, z: gains_all.at[y, k, z, x], gains)
+    spread_gains.start()
+    spread_out = Spread(w, lambda y, z: out_all.at[y, k, z, x], wo)
+    spread_out.start()
+    pack_rows(hidden_columns, (wg, wu), hidden_pack)
+    deal_hidden = Deal(
+        w, lambda x, k: hidden_pack.at[2 * x + k], lambda sx, sk: hidden_all.at[y, sk, z, sx]
+    )
+    deal_hidden.start()
+    stays.append(stay(hidden_pack.at[rank], hidden_all.at[y, k, z, x], 6))
+    visit_cots = Visit(w, cots, lambda x, z: cots_all.at[z // 2, z % 2, x], local.at[7])
+    visit_cots.start()
+    for copy in stays:
+        copy.wait()
+    deal_heads.arrive()
+    spread_heads = Spread(w, lambda y, z: heads_all.at[y, :, z])
+    spread_heads.start()
+    visit_rows.arrive()
+    share_rows = Share(w, lambda x, k: rows_all.at[:, k, x])
+    share_rows.start()
+    deal_hidden.arrive()
+    spread_hidden = Spread(w, lambda y, z: hidden_all.at[y, :, z])
+    spread_hidden.start()
+    share_rows.forward()
+    spread_down = Spread(w, lambda y, z: down_all.at[y, z], wd)
+    spread_down.start()
+    visit_cots.arrive()
+    share_cots = Share(w, lambda x, k: cots_all.at[:, k, x])
+    share_cots.start()
+    spreads = [spread_gains, spread_heads, spread_out, spread_hidden, spread_down]
+    for spread in spreads:
+        for i in (1, 3, 2):
+            spread.forward(i)
+    share_cots.forward()
+    for spread in (spread_gains, spread_out):
+        for i in range(4):
+            spread.arrive(i)
+    share_gains = Share(w, lambda x, k: gains_all.at[:, k, :, x])
+    share_gains.start()
+    share_out = Share(w, lambda x, k: out_all.at[:, k, :, x])
+    share_out.start()
+    for spread in (spread_heads, spread_hidden, spread_down):
+        for i in range(4):
+            spread.arrive(i)
+    share_gains.forward()
+    share_out.forward()
+    shares = [share_rows, share_cots, share_gains, share_out]
+    for share in shares:
+        share.arrive()
+    swap.wait()
+    for part in [visit_rows, visit_cots, deal_heads, deal_hidden] + spreads + shares:
+        part.drain()
+
+
+def gather(rows, cots, ids, wq, wk, wv, wo, wg, wu, wd, gains):
+    r, d, f = rows.shape[1], rows.shape[2], wg.shape[1]
+    piece = wq.shape[0]
+    outs = (
+        shaped(2, 2, 2, r, d),
+        shaped(2, 2, 2, r, d),
+        shaped(2, *ids.shape, dtype=jnp.int32),
+        shaped(2, 2, 4, 2, piece, 3 * d // 4),
+        shaped(2, 2, 4, 2, piece, d),
+        shaped(2, 2, 4, 2, piece, f // 2),
+        shaped(2, 4, wd.shape[0], d),
+        shaped(2, 2, 4, 2, *gains.shape),
+    )
+    return kernel_call(
+        gather_body,
+        "gather",
+        outs,
+        [ANY, ANY, ANY, VMEM, VMEM, VMEM, ANY, VMEM, VMEM, ANY, ANY],
+        (ANY,) * len(outs),
+        [pltpu.VMEM((4, piece, 3 * d // 4), BF16), pltpu.VMEM((4, piece, f // 2), BF16)]
+        + sems(96)[:2]
+        + [pltpu.SemaphoreType.DMA((8,))],
+        collective=0,
+    )(rows, cots, ids, wq, wk, wv, wo, wg, wu, wd, gains)
+
+
+def share_body(block, whole, send, recv, local):
+    w = Wires(send, recv)
+    w.greet(w.group_peers()[:2])
+    share = Share(w, lambda x, k: whole.at[x, k], block)
+    stay = pltpu.make_async_copy(block, whole.at[w.x, w.k], local)
+    stay.start()
+    share.start()
+    share.forward()
+    share.arrive()
+    stay.wait()
+    share.drain()
+
+
+def share_group(block, collective):
+    return kernel_call(
+        share_body,
+        "share",
+        shaped(2, 2, *block.shape),
+        [ANY],
+        ANY,
+        sems(4),
+        collective=collective,
+    )(block)
+
+
+def sum_body(part, total, got_core, got_across, out_across, send, recv, local):
+    w = Wires(send, recv)
+    x, k = w.x, w.k
+    w.greet(w.group_peers()[:2])
+    slots = w.slots(2)
+    first = w.copy(part.at[:, 1 - k], got_core, w.at(x, w.y, w.z, 1 - k), slots)
+    second = w.copy(out_across, got_across, w.at(1 - x, w.y, w.z, k), slots + 1)
+    first.start()
+    first.wait()
+    for i in range(2):
+        out_across[i] = (
+            part[i, k, 1 - x].astype(F32) + got_core[i, 1 - x].astype(F32)
+        ).astype(BF16)
+    second.start()
+    for i in range(2):
+        total[i] = part[i, k, x].astype(F32) + got_core[i, x].astype(F32)
+    second.wait()
+    for i in range(2):
+        total[i] += got_across[i].astype(F32)
+
+
+def sum_group(part, collective):
+    _, _, _, r, d = part.shape
+    return kernel_call(
+        sum_body,
+        "sum_group",
+        shaped(2, r, d, dtype=F32),
+        [VMEM],
+        VMEM,
+        [
+            pltpu.VMEM((2, 2, r, d), BF16),
+            pltpu.VMEM((2, r, d), BF16),
+            pltpu.VMEM((2, r, d), BF16),
+        ]
+        + sems(2),
+        collective=collective,
+    )(part)
+
+
+def home_body(done, home, send, recv, local):
+    w = Wires(send, recv)
+    x, y, z, k = w.x, w.y, w.z, w.k
+    w.greet(w.line_peers() + w.cross_peers() + [w.at(x, y, z, 1 - k)])
+    back = Return(w, done, home, local)
+    back.start()
+    back.arrive()
+    back.drain()
+
+
+def send_home(done, collective):
+    return kernel_call(
+        home_body,
+        "send_home",
+        shaped(*done.shape, dtype=done.dtype),
+        [ANY],
+        ANY,
+        sems(2),
+        collective=collective,
+    )(done)
+
+
+class Fold:
+    def __init__(self, wires, part, got_pair, out_line, got_line, mine, ours):
+        self.w, self.part = wires, part
+        self.got_pair, self.out_line, self.got_line, self.mine = got_pair, out_line, got_line, mine
+        self.ours = ours
+        self.pairs, self.lines = wires.slots(1), wires.slots(4)
+
+    def pair(self):
+        w = self.w
+        return w.copy(self.part(1 - w.y), self.got_pair, w.pair_peer(), self.pairs)
+
+    def line(self, i):
+        w = self.w
+        z = (w.z + i) % 4
+        return w.copy(
+            self.out_line.at[z], self.got_line.at[i - 1], w.at(w.x, w.y, z, w.k), self.lines + i
+        )
+
+    def start(self):
+        self.pair().start()
+
+    def send(self):
+        w = self.w
+        self.pair().wait_recv()
+        for i in (2, 1, 3):
+            z = (w.z + i) % 4
+            self.out_line[z] = (
+                self.ours(z).astype(F32) + self.got_pair[z].astype(F32)
+            ).astype(self.out_line.dtype)
+            self.line(i).start()
+        self.mine[...] = self.ours(w.z).astype(F32) + self.got_pair[w.z].astype(F32)
+
+    def finish(self):
+        for i in (2, 1, 3):
+            self.line(i).wait_recv()
+            self.mine[...] += self.got_line[i - 1].astype(F32)
+
+    def drain(self):
+        self.pair().wait_send()
+        for i in (1, 2, 3):
+            self.line(i).wait_send()
+
+
+def reduce_body(
+    heads, out, hidden, down, gains,
+    q_out, k_out, v_out, o_out, g_out, u_out, d_out, gain_out,
+    heads_pair, heads_line, heads_got, heads_mine, heads_deal, heads_all,
+    hidden_pair, hidden_line, hidden_got, hidden_mine, hidden_deal, hidden_all,
+    down_pair, down_line, down_got,
+    out_pair, out_line, out_got, out_mine, out_deal, out_home,
+    gains_pair, gains_line, gains_got, gains_mine, gains_all,
+    send, recv, local,
+):
+    w = Wires(send, recv)
+    x, y, z, k = w.x, w.y, w.z, w.k
+    rank = 2 * x + k
+    w.greet(w.group_peers() + w.line_peers() + [w.pair_peer()])
+    folds = [
+        Fold(w, lambda y: down.at[y], down_pair, down_line, down_got, d_out, lambda z: down[y, z]),
+        Fold(
+            w, lambda y: hidden.at[y], hidden_pair, hidden_line, hidden_got, hidden_mine,
+            lambda z: hidden[y, z],
+        ),
+        Fold(
+            w, lambda y: heads.at[y], heads_pair, heads_line, heads_got, heads_mine,
+            lambda z: heads[y, z],
+        ),
+        Fold(
+            w, lambda y: gains.at[y], gains_pair, gains_line, gains_got, gains_mine,
+            lambda z: gains[y, z],
+        ),
+    ]
+    for fold in folds:
+        fold.start()
+    base = w.slots(6)
+    owner = y == x
+    out_across = w.copy(out, out_pair, w.pair_peer(), base)
+    pl.when(jnp.logical_not(owner))(lambda: out_across.start())
+
+    def out_piece(i):
+        zi = (z + i) % 4
+        return w.copy(out_line.at[zi], out_got.at[i - 1], w.at(x, y, zi, k), base + i)
+
+    for fold in folds[:2]:
+        fold.send()
+
+    @pl.when(owner)
+    def _():
+        out_across.wait_recv()
+        for i in (2, 1, 3):
+            zi = (z + i) % 4
+            out_line[zi] = (out[zi].astype(F32) + out_pair[zi].astype(F32)).astype(BF16)
+            out_piece(i).start()
+        out_mine[...] = out[z].astype(F32) + out_pair[z].astype(F32)
+
+    for fold in folds[2:]:
+        fold.send()
+    for fold in folds[:2]:
+        fold.finish()
+    hidden_deal[...] = hidden_mine[...].astype(BF16)
+    deal_hidden = Deal(w, lambda x, k: hidden_deal.at[k, x], lambda x, k: hidden_all.at[2 * x + k])
+    deal_hidden.start()
+    for fold in folds[2:]:
+        fold.finish()
+    heads_deal[...] = heads_mine[...].astype(BF16)
+    deal_heads = Deal(w, lambda x, k: heads_deal.at[k, x], lambda x, k: heads_all.at[2 * x + k])
+    deal_heads.start()
+    gains_all[rank] = gains_mine[...]
+    deal_gains = Deal(w, lambda x, k: gains_mine, lambda x, k: gains_all.at[2 * x + k])
+    deal_gains.start()
+    out_last = w.copy(out_deal, out_home, w.at(1 - x, y, z, k), base + 4)
+
+    @pl.when(owner)
+    def _():
+        for i in (2, 1, 3):
+            out_piece(i).wait_recv()
+            out_mine[...] += out_got[i - 1].astype(F32)
+        out_deal[...] = out_mine[1 - x].astype(BF16)
+        out_last.start()
+        o_out[...] = out_mine[x]
+
+    hidden_all[rank] = hidden_deal[k, x]
+    heads_all[rank] = heads_deal[k, x]
+    deal_hidden.arrive()
+    for r in range(4):
+        for half, target in enumerate((g_out, u_out)):
+            for j, (start, width) in enumerate(hidden_columns(r)):
+                at = 128 * j + half * 1024
+                target[:, start : start + width] = hidden_all[r, :, at : at + width].astype(F32)
+    deal_heads.arrive()
+    for r in range(4):
+        for j, target in enumerate((q_out, k_out, v_out)):
+            at = 256 * j
+            target[:, 256 * r : 256 * r + 256] = heads_all[r, :, at : at + 256].astype(F32)
+    deal_gains.arrive()
+    gain_out[...] = gains_all[0] + gains_all[1] + gains_all[2] + gains_all[3]
+
+    @pl.when(jnp.logical_not(owner))
+    def _():
+        out_last.wait_recv()
+        o_out[...] = out_home[...].astype(F32)
+
+    for part in folds + [deal_hidden, deal_heads, deal_gains]:
+        part.drain()
+
+    @pl.when(owner)
+    def _():
+        for i in (1, 2, 3):
+            out_piece(i).wait_send()
+        out_last.wait_send()
+
+    pl.when(jnp.logical_not(owner))(lambda: out_across.wait_send())
+
+
+def reduce_all(heads, out, hidden, down, gains):
+    p, h, u = heads.shape[4], heads.shape[5], hidden.shape[5]
+    d = down.shape[3]
+    r = down.shape[2]
+    outs = (
+        shaped(p, d, dtype=F32),
+        shaped(p, d, dtype=F32),
+        shaped(p, d, dtype=F32),
+        shaped(p, d, dtype=F32),
+        shaped(p, 2 * u, dtype=F32),
+        shaped(p, 2 * u, dtype=F32),
+        shaped(r, d, dtype=F32),
+        shaped(8, 128, dtype=F32),
+    )
+
+    def room(*shape, dtype=BF16):
+        return pltpu.VMEM(shape, dtype)
+
+    scratch = []
+    for width in (h, u):
+        scratch += [
+            room(4, 2, 2, p, width),
+            room(4, 2, 2, p, width),
+            room(3, 2, 2, p, width),
+            room(2, 2, p, width, dtype=F32),
+            room(2, 2, p, width),
+            room(4, p, width),
+        ]
+    scratch += [room(4, r, d), room(4, r, d), room(3, r, d)]
+    scratch += [
+        room(4, 2, p, d),
+        room(4, 2, p, d),
+        room(3, 2, p, d),
+        room(2, p, d, dtype=F32),
+        room(p, d),
+        room(p, d),
+    ]
+    scratch += [room(4, 8, 128, dtype=F32), room(4, 8, 128, dtype=F32)]
+    scratch += [room(3, 8, 128, dtype=F32), room(8, 128, dtype=F32), room(4, 8, 128, dtype=F32)]
+    return kernel_call(
+        reduce_body,
+        "reduce_all",
+        outs,
+        [VMEM] * 5,
+        (VMEM,) * len(outs),
+        scratch + sems(40),
+        collective=7,
+    )(heads, out, hidden, down, gains)
+
+
+def allowed_keys(ids_col, ids_row, keys, start):
+    same = ids_col[:keys, :1] == ids_row[:, start : start + 256]
+    key = lax.broadcasted_iota(jnp.int32, (keys, 256), 0)
+    query = lax.broadcasted_iota(jnp.int32, (keys, 256), 1) + start
+    return jnp.logical_and(same, key <= query)
+
+
+def dots(left, right, dims):
+    return lax.dot_general(left, right, (dims, ((), ())), preferred_element_type=F32)
+
+
+def only_head(array, head):
+    lane = lax.broadcasted_iota(jnp.int32, array.shape, 1)
+    return jnp.where(lane // HEAD == head, array, jnp.zeros_like(array))
+
+
+def attend_body(q, k, v_turned, ids_col, ids_row, mixed, logsum):
+    head = pl.program_id(0)
+    for block in range(4):
+        start, keys = 256 * block, 256 * block + 256
+        query = only_head(q[start : start + 256, :], head)
+        scores = dots(k[:keys, :], query, ((1,), (1,)))
+        mask = allowed_keys(ids_col, ids_row, keys, start)
+        scores = jnp.where(mask, scores * (HEAD**-0.5 * LOG2E), -1e30)
+        top = jnp.max(scores, axis=0, keepdims=True)
+        lifted = jnp.exp2(scores - top)
+        total = jnp.sum(lifted, axis=0, keepdims=True)
+        probs = (lifted * (1.0 / total)).astype(BF16)
+        values = v_turned[pl.ds(pl.multiple_of(head * HEAD, HEAD), HEAD), :keys]
+        mixed[:, start : start + 256] = dots(values, probs, ((1,), (0,))).astype(BF16)
+        logsum[0, :, start : start + 256] = top + jnp.log2(total)
+
+
+def attend(q, k, v_turned, ids_col, ids_row):
+    rows, width = q.shape
+    heads = width // HEAD
+    fixed = pl.BlockSpec(memory_space=pltpu.VMEM)
+    return pl.pallas_call(
+        attend_body,
+        name="attend",
+        grid=(heads,),
+        out_shape=(shaped(width, rows), shaped(heads, 1, rows, dtype=F32)),
+        in_specs=[fixed] * 5,
+        out_specs=(
+            pl.BlockSpec((HEAD, rows), lambda h: (h, 0)),
+            pl.BlockSpec((1, 1, rows), lambda h: (h, 0, 0)),
+        ),
+        compiler_params=pltpu.CompilerParams(vmem_limit_bytes=58 << 20),
+    )(q, k, v_turned, ids_col, ids_row)
+
+
+def attend_back_body(
+    q, k, v, k_turned, grad, grad_turned, mixed_turned, logsum, ids_col, ids_row,
+    grad_q, grad_k, grad_v,
+):
+    head = pl.program_id(0)
+
+    @pl.when(head == 0)
+    def _():
+        grad_k[...] = jnp.zeros_like(grad_k)
+        grad_v[...] = jnp.zeros_like(grad_v)
+
+    own = pl.ds(pl.multiple_of(head * HEAD, HEAD), HEAD)
+    for block in range(4):
+        start, keys = 256 * block, 256 * block + 256
+        span = slice(start, start + 256)
+        query = only_head(q[span, :], head)
+        upstream = only_head(grad[span, :], head)
+        scores = dots(k[:keys, :], query, ((1,), (1,)))
+        mask = allowed_keys(ids_col, ids_row, keys, start)
+        scores = jnp.where(mask, scores * (HEAD**-0.5 * LOG2E), -1e30)
+        probs = jnp.exp2(scores - logsum[0, :, span])
+        grad_probs = dots(v[:keys, :], upstream, ((1,), (1,)))
+        centre = jnp.sum(
+            grad_turned[own, span].astype(F32) * mixed_turned[own, span].astype(F32),
+            axis=0,
+            keepdims=True,
+        )
+        grad_scores = (probs * (grad_probs - centre)).astype(BF16)
+        grad_q[:, span] = (
+            dots(k_turned[own, :keys], grad_scores, ((1,), (0,))) * HEAD**-0.5
+        ).astype(BF16)
+        grad_k[:keys, :] += dots(grad_scores, query, ((1,), (0,)))
+        grad_v[:keys, :] += dots(probs.astype(BF16), upstream, ((1,), (0,)))
+
+
+def attend_back(q, k, v, k_turned, grad, grad_turned, mixed_turned, logsum, ids_col, ids_row):
+    rows, width = q.shape
+    heads = width // HEAD
+    fixed = pl.BlockSpec(memory_space=pltpu.VMEM)
+    return pl.pallas_call(
+        attend_back_body,
+        name="attend_back",
+        grid=(heads,),
+        out_shape=(
+            shaped(width, rows),
+            shaped(rows, width, dtype=F32),
+            shaped(rows, width, dtype=F32),
+        ),
+        in_specs=[fixed] * 7
+        + [pl.BlockSpec((1, 1, rows), lambda h: (h, 0, 0))]
+        + [fixed] * 2,
+        out_specs=(
+            pl.BlockSpec((HEAD, rows), lambda h: (h, 0)),
+            pl.BlockSpec((rows, width), lambda h: (0, 0)),
+            pl.BlockSpec((rows, width), lambda h: (0, 0)),
+        ),
+        compiler_params=pltpu.CompilerParams(vmem_limit_bytes=58 << 20),
+    )(q, k, v, k_turned, grad, grad_turned, mixed_turned, logsum, ids_col, ids_row)
 
 
 def product(left, right):
+    return jnp.dot(left, right, preferred_element_type=F32)
+
+
+def product_left(left, right):
+    return dots(left, right, ((0,), (0,)))
+
+
+def product_right(left, right):
+    return dots(left, right, ((1,), (1,)))
+
+
+def norm_back(rows, inverse, gain, upstream):
+    normed = rows * inverse
+    scaled = upstream * gain
+    grad_rows = inverse * (scaled - normed * jnp.mean(scaled * normed, axis=-1, keepdims=True))
+    return (grad_rows, jnp.sum(upstream * normed, axis=0))
+
+
+def inverse_size(rows):
+    return lax.rsqrt(jnp.mean(rows * rows, axis=-1, keepdims=True) + EPS)
+
+
+def grouped(
+    layer_input, doc_ids, attn_gain, query_weight, key_weight, value_weight, out_weight,
+    mlp_gain, gate_weight, up_weight, down_weight, out_grad,
+):
+    dp, ctx = lax.axis_index("dp"), lax.axis_index("ctx")
+    x, y, z, k = ctx % 2, dp // 2, ctx // 2, dp % 2
+    rank = 2 * x + k
+    _, block, width = layer_input.shape
+    length = doc_ids.shape[1]
+    piece = attn_gain.shape[0]
+    gains = jnp.zeros((16, 128), BF16)
+    gains = gains.at[0, :piece].set(attn_gain).at[1, :piece].set(mlp_gain)
+    rows_all, cots_all, ids_all, heads_all, out_all, hidden_all, down_all, gains_all = gather(
+        layer_input, out_grad, doc_ids, query_weight, key_weight, value_weight, out_weight,
+        gate_weight, up_weight, down_weight, gains,
+    )
+    inputs16 = rows_all.reshape(length, width)
+    cots = cots_all.reshape(length, width)
+    ids = lax.dynamic_slice(ids_all, (z // 2, z % 2, 0), (1, 1, length)).reshape(1, length)
+    ids_col = jnp.broadcast_to(ids.reshape(length, 1), (length, 128))
+    w_heads = heads_all.reshape(width, -1)
+    share = width // 4
+    w_query, w_key, w_value = (w_heads[:, i * share : (i + 1) * share] for i in range(3))
+    w_out = out_all.reshape(width, width)
+    w_hidden = hidden_all.reshape(width, -1)
+    units = w_hidden.shape[1] // 2
+    w_gate, w_up = w_hidden[:, :units], w_hidden[:, units:]
+    w_down = down_all.reshape(units, width)
+    gain_one = gains_all[..., 0, :piece].reshape(width).astype(F32)
+    gain_two = gains_all[..., 1, :piece].reshape(width).astype(F32)
+
+    inputs = inputs16.astype(F32)
+    inverse_one = inverse_size(inputs)
+    normed = (inputs * inverse_one * gain_one).astype(BF16)
+    query = product(normed, w_query).astype(BF16)
+    keys = product(normed, w_key).astype(BF16)
+    values = product(normed, w_value).astype(BF16)
+    mixed_turned, logsum = attend(query, keys, values.T, ids_col, ids)
+    mixed_all = share_group(mixed_turned.T, 1)
+    mixed_all = jnp.transpose(mixed_all, (2, 0, 1, 3)).reshape(length, width)
+    middle = inputs + product(mixed_all, w_out)
+    inverse_two = inverse_size(middle)
+    normed_two = (middle * inverse_two * gain_two).astype(BF16)
+    gate = product(normed_two, w_gate)
+    upward = product(normed_two, w_up)
+    sigma = jax.nn.sigmoid(gate)
+    hidden = (gate * sigma * upward).astype(BF16)
+    out_part = product(hidden, w_down).astype(BF16)
+    down_grad = product_left(hidden, cots).astype(BF16)
+    grad_hidden = product_right(cots, w_down)
+    grad_gate = (grad_hidden * upward * sigma * (1.0 + gate * (1.0 - sigma))).astype(BF16)
+    grad_up = (grad_hidden * gate * sigma).astype(BF16)
+    gate_grad = product_left(normed_two, grad_gate).astype(BF16)
+    up_grad = product_left(normed_two, grad_up).astype(BF16)
+    norm_part = (product_right(grad_gate, w_gate) + product_right(grad_up, w_up)).astype(BF16)
+
+    six = (2, 2, 2, block, width)
+    out_own = sum_group(out_part.reshape(six), 2)
+    grad_normed_two = sum_group(norm_part.reshape(six), 3)
+
+    def own_rows(array):
+        parts = array.reshape(2, 2, 2, block, -1)
+        return lax.dynamic_slice(
+            parts, (0, k, x, 0, 0), (2, 1, 1, block, parts.shape[-1])
+        ).reshape(2 * block, -1)
+
+    middle_own = own_rows(middle)
+    output_own = (middle_own + out_own.reshape(2 * block, width)).astype(BF16)
+    grad_middle, mlp_gain_part = norm_back(
+        middle_own, own_rows(inverse_two), gain_two, grad_normed_two.reshape(2 * block, width)
+    )
+    grad_middle = grad_middle + own_rows(cots).astype(F32)
+    branch = share_group(grad_middle.astype(BF16).reshape(2, block, width), 4)
+    branch = jnp.transpose(branch, (2, 1, 0, 3, 4)).reshape(length, width)
+    layer_output = send_home(output_own.reshape(2, block, width), 5)
+    w_out_own = lax.dynamic_slice(w_out, (rank * share, 0), (share, width))
+    grad_mixed = product_right(branch, w_out_own).astype(BF16)
+    out_proj_grad = dots(mixed_turned, branch, ((1,), (0,))).astype(BF16)
+    grad_q, grad_k, grad_v = attend_back(
+        query, keys, values, keys.T, grad_mixed, grad_mixed.T, mixed_turned, logsum, ids_col, ids
+    )
+    grad_heads = jnp.concatenate(
+        [grad_q.T, (grad_k * HEAD**-0.5).astype(BF16), grad_v.astype(BF16)], axis=1
+    )
+    heads_grad = product_left(normed, grad_heads).astype(BF16)
+    first_part = product_right(grad_heads, w_heads).astype(BF16)
+    grad_normed = sum_group(first_part.reshape(six), 6)
+    grad_inputs, attn_gain_part = norm_back(
+        own_rows(inputs), own_rows(inverse_one), gain_one, grad_normed.reshape(2 * block, width)
+    )
+    input_own = (grad_middle + grad_inputs).astype(BF16)
+    input_grad = send_home(input_own.reshape(2, block, width), 8).astype(F32)
+
+    def by_owner(array):
+        shaped_rows = array.reshape(2, 2, 4, 2, piece, -1)
+        return jnp.transpose(shaped_rows, (0, 2, 1, 3, 4, 5))
+
+    gain_parts = jnp.stack([attn_gain_part, mlp_gain_part])
+    gain_parts = jnp.transpose(gain_parts.reshape(2, 2, 2, 4, 2, piece), (1, 3, 0, 2, 4, 5))
+    gain_parts = jnp.pad(gain_parts.reshape(2, 4, 2, 4 * piece), ((0, 0), (0, 0), (0, 6), (0, 0)))
+    q_grad, k_grad, v_grad, o_grad, g_grad, u_grad, d_grad, gain_grads = reduce_all(
+        by_owner(heads_grad),
+        out_proj_grad.reshape(4, 2, piece, width),
+        by_owner(jnp.concatenate([gate_grad, up_grad], axis=1)),
+        down_grad.reshape(2, 4, units // 8, width),
+        gain_parts,
+    )
+    gain_own = lax.dynamic_slice(gain_grads, (0, piece * (2 * k + x)), (2, piece))
+    return (
+        layer_output, input_grad, gain_own[0], q_grad, k_grad, v_grad, o_grad, gain_own[1],
+        g_grad, u_grad, d_grad,
+    )
+
+
+def plain_product(left, right):
     return jnp.dot(left, right, preferred_element_type=jnp.float32)
 
 
-def product_left(left, right):
+def plain_product_left(left, right):
     return lax.dot_general(
         left, right, (((0,), (0,)), ((), ())), preferred_element_type=jnp.float32
     )
 
 
-def product_right(left, right):
+def plain_product_right(left, right):
     return lax.dot_general(
         left, right, (((1,), (1,)), ((), ())), preferred_element_type=jnp.float32
     )
@@ -30,7 +978,7 @@
     return (rows * inverse * gain, inverse)
 
 
-def norm_back(rows, inverse, gain, upstream):
+def plain_norm_back(rows, inverse, gain, upstream):
     normed = rows * inverse
     scaled = upstream * gain
     grad_rows = inverse * (scaled - normed * jnp.mean(scaled * normed, axis=-1, keepdims=True))
@@ -52,7 +1000,7 @@
     return jnp.where(allowed[:, None], scores, -1e30)
 
 
-def attend(query, keys, values, allowed):
+def plain_attend(query, keys, values, allowed):
     groups, rows, width = query.shape
 
     def step(index, carry):
@@ -81,7 +1029,7 @@
     return lax.fori_loop(0, width // (2 * HEAD), step, start_state)
 
 
-def attend_back(query, keys, values, allowed, logsum, grad_mixed):
+def plain_attend_back(query, keys, values, allowed, logsum, grad_mixed):
     groups, rows, width = query.shape
     length = keys.shape[1]
     scale = HEAD ** (-0.5)
@@ -184,24 +1132,24 @@
     gain_attn = gain_one.astype(jnp.float32)
     normed_full, inverse_one = normalize(inputs, gain_attn)
     normed = normed_full.astype(jnp.bfloat16)
-    query = product(normed, w_query).astype(jnp.bfloat16).reshape(groups, rows, width)
-    keys_own = product(normed, w_key).astype(jnp.bfloat16).reshape(groups, rows, width)
-    values_own = product(normed, w_value).astype(jnp.bfloat16).reshape(groups, rows, width)
+    query = plain_product(normed, w_query).astype(jnp.bfloat16).reshape(groups, rows, width)
+    keys_own = plain_product(normed, w_key).astype(jnp.bfloat16).reshape(groups, rows, width)
+    values_own = plain_product(normed, w_value).astype(jnp.bfloat16).reshape(groups, rows, width)
     keys, values = (
         lax.all_gather(keys_own, "ctx", axis=1, tiled=True),
         lax.all_gather(values_own, "ctx", axis=1, tiled=True),
     )
-    attended, logsum = attend(query, keys, values, allowed)
+    attended, logsum = plain_attend(query, keys, values, allowed)
     attended_rows = attended.reshape(groups * rows, width)
-    middle = inputs + product(attended_rows, w_out)
+    middle = inputs + plain_product(attended_rows, w_out)
     gain_mlp = gain_two.astype(jnp.float32)
     normed_two_full, inverse_two = normalize(middle, gain_mlp)
     normed_two = normed_two_full.astype(jnp.bfloat16)
-    gate = product(normed_two, w_gate)
-    upward = product(normed_two, w_up)
+    gate = plain_product(normed_two, w_gate)
+    upward = plain_product(normed_two, w_up)
     sigma = jax.nn.sigmoid(gate)
     hidden = (gate * sigma * upward).astype(jnp.bfloat16)
-    layer_output = (middle + product(hidden, w_down)).astype(jnp.bfloat16)
+    layer_output = (middle + plain_product(hidden, w_down)).astype(jnp.bfloat16)
     gathered_back = (
         lax.all_gather(attn_gain, ("dp", "ctx"), axis=0, tiled=True),
         lax.all_gather(query_weight, ("dp", "ctx"), axis=0, tiled=True),
@@ -215,23 +1163,23 @@
     )
     gain_one, w_query, w_key, w_value, w_out, gain_two, w_gate, w_up, w_down = gathered_back
     upstream = out_grad.reshape(groups * rows, width)
-    down_grad = product_left(hidden, upstream)
-    grad_hidden = product_right(upstream, w_down)
+    down_grad = plain_product_left(hidden, upstream)
+    grad_hidden = plain_product_right(upstream, w_down)
     grad_gate = (grad_hidden * upward * sigma * (1.0 + gate * (1.0 - sigma))).astype(jnp.bfloat16)
     grad_up = (grad_hidden * gate * sigma).astype(jnp.bfloat16)
-    gate_grad = product_left(normed_two, grad_gate)
-    up_grad = product_left(normed_two, grad_up)
-    grad_normed_two = product_right(grad_gate, w_gate) + product_right(grad_up, w_up)
-    grad_middle, mlp_gain_grad = norm_back(
+    gate_grad = plain_product_left(normed_two, grad_gate)
+    up_grad = plain_product_left(normed_two, grad_up)
+    grad_normed_two = plain_product_right(grad_gate, w_gate) + plain_product_right(grad_up, w_up)
+    grad_middle, mlp_gain_grad = plain_norm_back(
         middle, inverse_two, gain_two.astype(jnp.float32), grad_normed_two
     )
     grad_middle = grad_middle + upstream.astype(jnp.float32)
     grad_branch = grad_middle.astype(jnp.bfloat16)
-    out_proj_grad = product_left(attended_rows, grad_branch)
+    out_proj_grad = plain_product_left(attended_rows, grad_branch)
     grad_attended = (
-        product_right(grad_branch, w_out).astype(jnp.bfloat16).reshape(groups, rows, width)
-    )
-    grad_query, grad_keys_all, grad_values_all = attend_back(
+        plain_product_right(grad_branch, w_out).astype(jnp.bfloat16).reshape(groups, rows, width)
+    )
+    grad_query, grad_keys_all, grad_values_all = plain_attend_back(
         query, keys, values, allowed, logsum, grad_attended
     )
     grad_keys, grad_values = (
@@ -245,15 +1193,15 @@
     grad_query = grad_query.astype(jnp.bfloat16).reshape(groups * rows, width)
     grad_keys = grad_keys.astype(jnp.bfloat16).reshape(groups * rows, width)
     grad_values = grad_values.astype(jnp.bfloat16).reshape(groups * rows, width)
-    query_grad = product_left(normed, grad_query)
-    key_grad = product_left(normed, grad_keys)
-    value_grad = product_left(normed, grad_values)
+    query_grad = plain_product_left(normed, grad_query)
+    key_grad = plain_product_left(normed, grad_keys)
+    value_grad = plain_product_left(normed, grad_values)
     grad_normed = (
-        product_right(grad_query, w_query)
-        + product_right(grad_keys, w_key)
-        + product_right(grad_values, w_value)
-    )
-    grad_inputs, attn_gain_grad = norm_back(
+        plain_product_right(grad_query, w_query)
+        + plain_product_right(grad_keys, w_key)
+        + plain_product_right(grad_values, w_value)
+    )
+    grad_inputs, attn_gain_grad = plain_norm_back(
         inputs, inverse_one, gain_one.astype(jnp.float32), grad_normed
     )
     input_grad = (grad_middle + grad_inputs).reshape(groups, rows, width)
@@ -298,8 +1246,10 @@
         P(("dp", "ctx"), None),
         P("dp", "ctx", None),
     )
+    fits = mesh.shape["dp"] == 4 and mesh.shape["ctx"] == 8
+    body = grouped if fits else on_device
     return jax.shard_map(
-        on_device,
+        body,
         mesh=mesh,
         in_specs=placed,
         out_specs=(

time: 2620 us -> 602 us (0.23)
  waiting for transfers between devices: 2230 us -> 0 us
  Pallas kernels: 0 us -> 462 us
  matrix products: 155 us -> 56.6 us
  blocking collectives: 79.4 us -> 0 us
  local copies, waits for them, and re-layouts: 108 us -> 49.5 us
    reduce_scatter x9 -> x0, waiting for transfers between devices: 1730 us -> none  [the longest x1 363 us: on_device(): lax.psum_scatter(gate_grad, ('dp', 'ctx'), scatter_dimension=0, tiled=True)]
    all_gather x9 -> x0, waiting for transfers between devices: 490 us -> none  [the longest x1 77.6 us: on_device(): lax.all_gather(gate_weight, ('dp', 'ctx'), axis=0, tiled=True)]
    pallas_call x0 -> x11, Pallas kernels: none -> 462 us  [the longest x1 159 us: gather(): kernel_call(gather_body, 'gather', outs, [ANY, ANY, ANY, VMEM, VMEM, VMEM...]
    dot_general x77 -> x17, matrix products: 155 us -> 56.6 us  [the longest x10 31.8 us: dots(): lax.dot_general(left, right, (dims, ((), ())), preferred_element_type=F32)]
    unnamed x2 -> x0, blocking collectives: 79.4 us -> none
    dynamic_slice x65 -> x3, local copies, waits for them, and re-layouts: 56.3 us -> 1.47 us  [the longest x1 0.76 us: grouped(): lax.dynamic_slice(gain_grads, (0, piece * (2 * k + x)), (2, piece))]
  transfers between devices with their start and end apart: 18 -> 0, of which waited for: 18 -> 0; matrix products, arithmetic and copies ran while one was open for 6% -> 0% of each run, Pallas kernels for 0% -> 0%
where the time goes in v1:
time: 602 us; the launch traced here: 591 us
  Pallas kernels  462 us (77%)
  matrix products  56.6 us (9%)
  local copies, waits for them, and re-layouts  49.5 us (8%)
  other arithmetic  21.1 us (4%)
    pallas_call x1, Pallas kernels, gather(): kernel_call(gather_body, 'gather', outs, [ANY, ANY, ANY, VMEM, VMEM, VMEM...  159 us
    pallas_call x1, Pallas kernels, reduce_all(): kernel_call(reduce_body, 'reduce_all', outs, [VMEM] * 5, (VMEM,) * len(ou...  153 us
    pallas_call x3, Pallas kernels, sum_group(): kernel_call(sum_body, 'sum_group', shaped(2, r, d, dtype=F32), [VMEM], VM...  59.4 us
    pallas_call x2, Pallas kernels, share_group(): kernel_call(share_body, 'share', shaped(2, 2, *block.shape), [ANY], ANY,...  35.8 us
    dot_general x10, matrix products, dots(): lax.dot_general(left, right, (dims, ((), ())), preferred_element_type=F32)  31.8 us
    pallas_call x2, Pallas kernels, send_home(): kernel_call(home_body, 'send_home', shaped(*done.shape, dtype=done.dtype)...  29.8 us
    dot_general x7, matrix products, product(): return jnp.dot(left, right, preferred_element_type=F32)  24.8 us
    unnamed x82, local copies, waits for them, and re-layouts  14 us

profile of v1, /device:TPU:19, one launch (start us, length us, event | category | flops | bytes accessed | tf_op | source)
XLA Modules:
  0.0 591.3 jit_solution(15489707850303949024)
XLA Ops:
  2.7 159.4 %gather.1 = (bf16[2,2,2,128,1024]{4,3,2,1,0:T(8,128)(2,1)}, bf16[2,2,2,128,1024]{4,3,2,1,0:T(8,128)(2,1)}, s32[2,2,1024]{2,1,0:T(2,128)}, bf16[2,2,4,2,32,768]{5...) custom-call(bf16[2,128,1024]{2,1,0:T(8,128)(2,1)} %rows.1, ...), custom_call_target="tpu_custom_call" | custom-call | tf_op jit(solution)/shard_map/gather/pallas_call | solution.py:409
  162.2 1.4 fusion.42.ids_row
  165.3 2.1 multiply_reduce_fusion.1
  169.1 1.4 copy-done.8
  170.5 1.8 convolution_convert_fusion.9
  173.3 2.4 convolution_convert_fusion.8.v
  176.7 3.2 convolution_convert_fusion.10.q
  179.9 12.0 %attend.1 = (bf16[256,1024]{1,0:T(8,128)(2,1)}, f32[4,1,1024]{2,1,0:T(1,128)}) custom-call(bf16[1024,256]{1,0:T(8,128)(2,1)} %convolution_convert_fusion.10.q, bf16[1024,256]{1,0:T(8,128)(2,1)} %copy.34.k, bf16[256,1024]{1,0:T(8,128)(2,1)} %copy.35.v_turned, s32[1024,128]{1,0:T(8,128)} %broadcast_in_dim.5.ids_col, s32[1,1024]{1,0:T(1,128)} %fusion.42.ids_row), custom_call_target="tpu_custom_call" | custom-call | tf_op jit(solution)/shard_map/attend/pallas_call | solution.py:749
  191.9 2.0 copy.36
  194.0 17.5 %share.2 = bf16[2,2,1024,256]{3,2,1,0:T(8,128)(2,1)} custom-call(bf16[1024,256]{1,0:T(8,128)(2,1)} %bitcast.117), custom_call_target="tpu_custom_call" | custom-call | tf_op jit(solution)/shard_map/share/pallas_call | solution.py:436
  211.5 4.5 copy.37
  216.0 6.8 %multiply_reduce_fusion = (f32[1024]{0:T(1024)S(1)}, f32[1024,1024]{1,0:T(8,128)}) fusion(bf16[1024,1024]{0,1:T(8,128)(2,1)} %bitcast.123, bf16[1024,1024]{1,0:T(8,128)(2,1)} %bitcast.147, bf16[2,2,2,128,1024]{4,3,2,1,0:T(8,128)(2,1)S(1)} %copy-done), kind=kOutput, calls=%fused_computation.12 | convolution fusion | flops 2151676928 | bytes 10489856 | tf_op jit(solution)/shard_map/dot_general | solution.py:824
  222.9 2.8 multiply_convert_fusion.3
  226.4 2.4 fusion.3
  228.8 2.4 fusion.7
  231.2 5.6 multiply_convert_fusion
  236.8 2.4 fusion.5
  239.2 3.8 add_convert_fusion
  242.9 19.4 %sum_group.4 = f32[2,128,1024]{2,1,0:T(8,128)} custom-call(bf16[2,2,2,128,1024]{4,3,2,1,0:T(8,128)(2,1)} %bitcast.118), custom_call_target="tpu_custom_call" | custom-call | tf_op jit(solution)/shard_map/sum_group/pallas_call | solution.py:470
  262.4 2.0 multiply_reduce_fusion.2
  264.4 2.5 fusion.17.block
  266.9 18.3 %share.3 = bf16[2,2,2,128,1024]{4,3,2,1,0:T(8,128)(2,1)} custom-call(bf16[2,128,1024]{2,1,0:T(8,128)(2,1)} %fusion.17.block), custom_call_target="tpu_custom_call" | custom-call | tf_op jit(solution)/shard_map/share/pallas_call | solution.py:436
  285.2 3.1 copy.40
  288.2 3.2 convolution_convert_fusion.7
  291.5 2.0 copy.43.grad
  293.5 13.1 %attend_back.1 = (bf16[256,1024]{1,0:T(8,128)(2,1)}, f32[1024,256]{1,0:T(8,128)}, f32[1024,256]{1,0:T(8,128)}) custom-call(bf16[1024,256]{1,0:T(8,128)(2,1)} %convolution_convert_fusion.10.q, bf16[1024,256]{1,0:T(8,128)(2,1)} %copy.34.k, bf16[1024,256]{1,0:T(8,128)(2,1)} %copy-done.7, bf16[256,1024]{1,0:T(8,128)(2,1)} %bitcast.114, ...), custom_call_target="tpu_custom_call" | custom-call | tf_op jit(solution)/shard_map/attend_back/pallas_call | solution.py:802
  306.6 2.0 copy.44
  308.7 1.4 convert_element_type.144
  310.9 3.1 convolution_convert_fusion.4
  314.0 19.9 %sum_group.5 = f32[2,128,1024]{2,1,0:T(8,128)} custom-call(bf16[2,2,2,128,1024]{4,3,2,1,0:T(8,128)(2,1)} %bitcast.120), custom_call_target="tpu_custom_call" | custom-call | tf_op jit(solution)/shard_map/sum_group/pallas_call | solution.py:470
  335.5 1.8 copy-done.4
  338.2 4.1 convolution_convert_fusion.1
  342.4 2.4 convolution_convert_fusion.2
  344.8 2.4 pad_maximum_fusion
  347.2 6.7 %copy.46 = bf16[1024,2048]{1,0:T(8,128)(2,1)} copy(bf16[1024,2048]{0,1:T(8,128)(2,1)} %pad_maximum_fusion) | data formatting | bytes 8388608 | tf_op jit(solution)/shard_map/concatenate | solution.py:949
  354.0 4.9 copy.58
  358.9 1.9 convolution_convert_fusion.5
  360.8 1.3 copy.59
  363.1 1.5 convolution_convert_fusion.6
  364.6 3.7 convolution_convert_fusion
  368.4 153.0 %reduce_all.1 = (f32[32,1024]{1,0:T(8,128)}, f32[32,1024]{1,0:T(8,128)}, f32[32,1024]{1,0:T(8,128)}, f32[32,1024]{1,0:T(8,128)}, f32[32,4096]{1,0:T(8,128)}, /*i...) custom-call(bf16[2,4,2,2,32,768]{5,4,3,2,1,0:T(8,128)(2,1)} %bitcast.113, ...), custom_call_target="tpu_custom_call" | custom-call | tf_op jit(solution)/shard_map/reduce_all/pallas_call | solution.py:701
  522.7 5.9 convolution_convert_fusion.3
  528.6 20.1 %sum_group.3 = f32[2,128,1024]{2,1,0:T(8,128)} custom-call(bf16[2,2,2,128,1024]{4,3,2,1,0:T(8,128)(2,1)} %bitcast.119), custom_call_target="tpu_custom_call" | custom-call | tf_op jit(solution)/shard_map/sum_group/pallas_call | solution.py:470
  548.7 3.3 add_convert_fusion.1
  552.1 14.9 %send_home.3 = bf16[2,128,1024]{2,1,0:T(8,128)(2,1)} custom-call(bf16[2,128,1024]{2,1,0:T(8,128)(2,1)} %get-tuple-element.86.done), custom_call_target="tpu_custom_call" | custom-call | tf_op jit(solution)/shard_map/send_home/pallas_call | solution.py:497
  567.0 2.2 convert_element_type.147
  569.3 14.8 %send_home.2 = bf16[2,128,1024]{2,1,0:T(8,128)(2,1)} custom-call(bf16[2,128,1024]{2,1,0:T(8,128)(2,1)} %get-tuple-element.87.done), custom_call_target="tpu_custom_call" | custom-call | tf_op jit(solution)/shard_map/send_home/pallas_call | solution.py:497
  584.1 1.9 copy.69
  (106 shorter events, 18.9 us)
Async XLA Ops:
  2.1 0.6 copy-start.29
  162.1 6.4 %copy-start = (bf16[2,2,2,128,1024]{4,3,2,1,0:T(8,128)(2,1)S(1)}, bf16[2,2,2,128,1024]{4,3,2,1,0:T(8,128)(2,1)}, u32[]{:S(2)}) copy-start(bf16[2,2,2,128,1024]{4,3,2,1,0:T(8,128)(2,1)} %get-tuple-element.56) | copy-start | bytes 6291460
  169.1 1.4 copy-start.8
  172.3 3.4 copy-start.6
  175.7 4.2 copy-start.7
  222.9 3.5 copy-start.30
  225.7 3.1 copy-start.10
  228.8 2.4 copy-start.14
  228.8 2.4 copy-start.31
  236.7 2.4 copy-start.33
  236.7 2.4 copy-start.36
  262.4 2.0 copy-start.1
  308.7 1.5 copy-start.13
  308.7 1.7 copy-start.23
  308.7 2.2 copy-start.32
  310.1 3.9 copy-start.16
  310.9 3.1 copy-start.18
  333.9 1.2 copy-start.2
  335.1 2.1 copy-start.4
  335.1 3.1 copy-start.11
  338.2 4.1 copy-start.34
  353.9 4.9 copy-start.9
  353.9 4.9 copy-start.17
  353.9 4.9 copy-start.19
  353.9 4.9 copy-start.24
  358.9 5.8 copy-start.35
  360.8 1.3 copy-start.5
  360.8 2.3 copy-start.12
  362.1 2.5 copy-start.15
  528.6 20.1 %copy-start.3 = (f32[2,128,1024]{2,1,0:T(8,128)S(1)}, f32[2,128,1024]{2,1,0:T(8,128)}, u32[]{:S(2)}) copy-start(f32[2,128,1024]{2,1,0:T(8,128)} %sum_group.5) | copy-start | bytes 3145732
  567.0 19.0 %copy-start.28 = (f32[32,1024]{1,0:T(8,128)S(1)}, f32[32,1024]{1,0:T(8,128)}, u32[]{:S(2)}) copy-start(f32[32,1024]{1,0:T(8,128)} %get-tuple-element.106) | copy-start | bytes 393220
  567.0 19.7 %copy-start.27 = (f32[32,1024]{1,0:T(8,128)S(1)}, f32[32,1024]{1,0:T(8,128)}, u32[]{:S(2)}) copy-start(f32[32,1024]{1,0:T(8,128)} %get-tuple-element.107) | copy-start | bytes 393220
  567.0 20.3 %copy-start.26 = (f32[32,1024]{1,0:T(8,128)S(1)}, f32[32,1024]{1,0:T(8,128)}, u32[]{:S(2)}) copy-start(f32[32,1024]{1,0:T(8,128)} %get-tuple-element.108) | copy-start | bytes 393220
  567.0 21.0 %copy-start.25 = (f32[32,1024]{1,0:T(8,128)S(1)}, f32[32,1024]{1,0:T(8,128)}, u32[]{:S(2)}) copy-start(f32[32,1024]{1,0:T(8,128)} %get-tuple-element.109) | copy-start | bytes 393220
  567.0 21.6 %copy-start.22 = (f32[32,4096]{1,0:T(8,128)S(1)}, f32[32,4096]{1,0:T(8,128)}, u32[]{:S(2)}) copy-start(f32[32,4096]{1,0:T(8,128)} %get-tuple-element.111) | copy-start | bytes 1572868
  569.2 20.2 %copy-start.21 = (f32[32,4096]{1,0:T(8,128)S(1)}, f32[32,4096]{1,0:T(8,128)}, u32[]{:S(2)}) copy-start(f32[32,4096]{1,0:T(8,128)} %get-tuple-element.112) | copy-start | bytes 1572868
  584.1 6.2 %copy-start.20 = (f32[128,1024]{1,0:T(8,128)S(1)}, f32[128,1024]{1,0:T(8,128)}, u32[]{:S(2)}) copy-start(f32[128,1024]{1,0:T(8,128)} %get-tuple-element.113) | copy-start | bytes 1572868

commit v2 on v0

--- a/solution.py
+++ b/solution.py
@@ -1,25 +1,1014 @@
+import functools
+
 import jax
 import jax.numpy as jnp
 from jax import lax
+from jax.experimental import pallas as pl
+from jax.experimental.pallas import tpu as pltpu
 from jax.sharding import PartitionSpec as P
 
 HEAD = 64
 
 
 EPS = 1e-05
-
-
-def product(left, right):
+MESH = pl.DeviceIdType.MESH
+F32 = jnp.float32
+BF16 = jnp.bfloat16
+LOG2E = 1.4426950408889634
+ANY = pl.BlockSpec(memory_space=pl.ANY)
+VMEM = pl.BlockSpec(memory_space=pltpu.VMEM)
+
+
+class Wires:
+    def __init__(self, send, recv):
+        dp, ctx = lax.axis_index("dp"), lax.axis_index("ctx")
+        self.x, self.y = ctx % 2, dp // 2
+        self.z, self.k = ctx // 2, dp % 2
+        self.send, self.recv = send, recv
+        self.used = 0
+
+    def slots(self, count):
+        first = self.used
+        self.used += count
+        return first
+
+    def at(self, x, y, z, k):
+        return (2 * y + k, 2 * z + x)
+
+    def copy(self, source, target, device, slot, recv_slot=None):
+        return pltpu.make_async_remote_copy(
+            src_ref=source,
+            dst_ref=target,
+            send_sem=self.send.at[slot],
+            recv_sem=self.recv.at[slot if recv_slot is None else recv_slot],
+            device_id=device,
+            device_id_type=MESH,
+        )
+
+    def greet(self, peers):
+        barrier = pltpu.get_barrier_semaphore()
+        for peer in peers:
+            pl.semaphore_signal(barrier, inc=1, device_id=peer, device_id_type=MESH)
+        pl.semaphore_wait(barrier, len(peers))
+
+    def group_peers(self):
+        x, y, z, k = self.x, self.y, self.z, self.k
+        return [self.at(1 - x, y, z, k), self.at(x, y, z, 1 - k), self.at(1 - x, y, z, 1 - k)]
+
+    def line_peers(self):
+        x, y, z, k = self.x, self.y, self.z, self.k
+        return [self.at(x, y, (z + i) % 4, k) for i in (1, 2, 3)]
+
+    def cross_peers(self):
+        x, y, z, k = self.x, self.y, self.z, self.k
+        return [self.at(x, y, (z + i) % 4, 1 - k) for i in (1, 2, 3)]
+
+    def pair_peer(self):
+        return self.at(self.x, 1 - self.y, self.z, self.k)
+
+
+class Spread:
+    def __init__(self, wires, block, own=None):
+        self.w, self.block, self.own = wires, block, own
+        self.lines, self.pairs = wires.slots(4), wires.slots(4)
+
+    def line(self, i, z, own=None):
+        w = self.w
+        ref = self.block(w.y, z)
+        target = w.at(w.x, w.y, (w.z + i) % 4, w.k)
+        return w.copy(ref if own is None else own, ref, target, self.lines + i)
+
+    def pair(self, i, y, own=None):
+        w = self.w
+        ref = self.block(y, (w.z + 4 - i) % 4)
+        return w.copy(ref if own is None else own, ref, w.pair_peer(), self.pairs + i)
+
+    def start(self):
+        for i in (2, 1, 3):
+            self.line(i, self.w.z, self.own).start()
+        self.pair(0, self.w.y, self.own).start()
+
+    def forward(self, i):
+        self.line(i, (self.w.z + 4 - i) % 4).wait_recv()
+        self.pair(i, self.w.y).start()
+
+    def arrive(self, i):
+        self.pair(i, 1 - self.w.y).wait_recv()
+
+    def drain(self):
+        for i in (1, 2, 3):
+            self.line(i, self.w.z, self.own).wait_send()
+        for i in range(4):
+            self.pair(i, self.w.y).wait_send()
+
+
+class Share:
+    def __init__(self, wires, block, own=None):
+        self.w, self.block, self.own = wires, block, own
+        self.first = wires.slots(3)
+
+    def piece(self, i):
+        w = self.w
+        core, across = w.at(w.x, w.y, w.z, 1 - w.k), w.at(1 - w.x, w.y, w.z, w.k)
+        ref = self.block(w.x if i < 2 else 1 - w.x, w.k)
+        source = ref if self.own is None or i == 2 else self.own
+        return w.copy(source, ref, across if i == 0 else core, self.first + i)
+
+    def landed(self, i):
+        w = self.w
+        ref = self.block(*[(1 - w.x, w.k), (w.x, 1 - w.k), (1 - w.x, 1 - w.k)][i])
+        return w.copy(ref, ref, w.at(w.x, w.y, w.z, 1 - w.k), self.first + i)
+
+    def start(self):
+        self.piece(0).start()
+        self.piece(1).start()
+
+    def forward(self):
+        self.landed(0).wait_recv()
+        self.piece(2).start()
+
+    def arrive(self):
+        self.landed(1).wait_recv()
+        self.landed(2).wait_recv()
+
+    def drain(self):
+        for i in range(3):
+            self.piece(i).wait_send()
+
+
+class Deal:
+    def __init__(self, wires, outgoing, incoming):
+        self.w, self.outgoing, self.incoming = wires, outgoing, incoming
+        self.first = wires.slots(3)
+
+    def mate(self, i):
+        w = self.w
+        return [(1 - w.x, w.k), (w.x, 1 - w.k), (1 - w.x, 1 - w.k)][i]
+
+    def piece(self, i):
+        w = self.w
+        x, k = self.mate(i)
+        return w.copy(
+            self.outgoing(x, k), self.incoming(w.x, w.k), w.at(x, w.y, w.z, k), self.first + i
+        )
+
+    def landed(self, i):
+        x, k = self.mate(i)
+        ref = self.incoming(x, k)
+        return self.w.copy(ref, ref, self.w.at(x, self.w.y, self.w.z, k), self.first + i)
+
+    def start(self):
+        for i in range(3):
+            self.piece(i).start()
+
+    def arrive(self):
+        for i in range(3):
+            self.landed(i).wait_recv()
+
+    def drain(self):
+        for i in range(3):
+            self.piece(i).wait_send()
+
+
+class Visit:
+    def __init__(self, wires, home, full, local):
+        self.w, self.home, self.full, self.local = wires, home, full, local
+        self.first = wires.slots(2)
+        w = wires
+        self.own = [jnp.logical_and(w.z == 2 * w.k + j, w.z % 2 == w.k) for j in range(2)]
+
+    def piece(self, j):
+        w = self.w
+        return w.copy(
+            self.home.at[j],
+            self.full(w.x, w.z),
+            w.at(w.x, w.y, 2 * w.k + j, w.z % 2),
+            self.first + j,
+            self.first + w.z // 2,
+        )
+
+    def stay(self, j):
+        return pltpu.make_async_copy(self.home.at[j], self.full(self.w.x, self.w.z), self.local)
+
+    def landed(self, i):
+        w = self.w
+        ref = self.full(w.x, w.k + 2 * i)
+        return w.copy(ref, ref, w.pair_peer(), self.first + i)
+
+    def here(self, i):
+        w = self.w
+        return jnp.logical_and(w.k + 2 * i == w.z, w.z // 2 == w.k)
+
+    def start(self):
+        for j in range(2):
+            pl.when(self.own[j])(lambda: self.stay(j).start())
+            pl.when(jnp.logical_not(self.own[j]))(lambda: self.piece(j).start())
+
+    def arrive(self):
+        for j in range(2):
+            pl.when(self.own[j])(lambda: self.stay(j).wait())
+        for i in range(2):
+            pl.when(jnp.logical_not(self.here(i)))(lambda: self.landed(i).wait_recv())
+
+    def drain(self):
+        for j in range(2):
+            pl.when(jnp.logical_not(self.own[j]))(lambda: self.piece(j).wait_send())
+
+
+class Return:
+    def __init__(self, wires, done, home, local):
+        self.w, self.done, self.home, self.local = wires, done, home, local
+        self.first = wires.slots(2)
+
+    def own(self, i):
+        w = self.w
+        return jnp.logical_and(2 * i + w.k == w.z, w.z // 2 == w.k)
+
+    def piece(self, i):
+        w = self.w
+        return w.copy(
+            self.done(i),
+            self.home.at[w.z % 2],
+            w.at(w.x, w.y, 2 * i + w.k, w.z // 2),
+            self.first + i,
+            self.first + w.z % 2,
+        )
+
+    def stay(self, i):
+        return pltpu.make_async_copy(self.done(i), self.home.at[self.w.z % 2], self.local)
+
+    def here(self, j):
+        w = self.w
+        return jnp.logical_and(2 * w.k + j == w.z, w.z % 2 == w.k)
+
+    def landed(self, j):
+        ref = self.home.at[j]
+        return self.w.copy(ref, ref, self.w.pair_peer(), self.first + j)
+
+    def start(self):
+        for i in range(2):
+            pl.when(self.own(i))(lambda: self.stay(i).start())
+            pl.when(jnp.logical_not(self.own(i)))(lambda: self.piece(i).start())
+
+    def arrive(self):
+        for i in range(2):
+            pl.when(self.own(i))(lambda: self.stay(i).wait())
+        for j in range(2):
+            pl.when(jnp.logical_not(self.here(j)))(lambda: self.landed(j).wait_recv())
+
+    def drain(self):
+        for i in range(2):
+            pl.when(jnp.logical_not(self.own(i)))(lambda: self.piece(i).wait_send())
+
+
+def shaped(*shape, dtype=BF16):
+    return jax.ShapeDtypeStruct(shape, dtype)
+
+
+def pack_rows(columns, shards, packed):
+    for rank in range(4):
+        at = 0
+        for shard in shards:
+            for start, width in columns(rank):
+                packed[rank, :, at : at + width] = shard[:, start : start + width]
+                at += width
+
+
+def head_columns(rank):
+    return [(256 * rank, 256)]
+
+
+def hidden_columns(rank):
+    x, k = rank // 2, rank % 2
+    return [(128 * (8 * (2 * y + k) + 2 * z + x), 128) for y in range(2) for z in range(4)]
+
+
+class Total:
+    def __init__(self, wires, part, got_core, got_across):
+        self.w, self.part, self.got_core, self.got_across = wires, part, got_core, got_across
+        self.first = wires.slots(4)
+        self.half = part.shape[2] // 2
+
+    def core(self, i):
+        w = self.w
+        return w.copy(
+            self.part.at[0, i], self.got_core.at[i], w.at(w.x, w.y, w.z, 1 - w.k), self.first + i
+        )
+
+    def rows(self, x):
+        return pl.ds(pl.multiple_of(self.half * x, self.half), self.half)
+
+    def across(self, i):
+        w = self.w
+        return w.copy(
+            self.part.at[1, i, self.rows(1 - w.x)],
+            self.got_across.at[i],
+            w.at(1 - w.x, w.y, w.z, w.k),
+            self.first + 2 + i,
+        )
+
+    def give(self, i, value):
+        self.part[0, i] = value.astype(BF16)
+        self.core(i).start()
+
+    def keep(self, i, value):
+        self.core(i).wait_recv()
+        self.part[1, i] = (value + self.got_core[i].astype(F32)).astype(BF16)
+        self.across(i).start()
+
+    def take(self, i):
+        self.across(i).wait_recv()
+        own = self.part[1, i, self.rows(self.w.x)]
+        return own.astype(F32) + self.got_across[i].astype(F32)
+
+    def drain(self):
+        for i in range(2):
+            self.core(i).wait_send()
+            self.across(i).wait_send()
+
+
+class Fold:
+    def __init__(self, wires, whole, block, got_pair, pair_block, got_line):
+        self.w, self.whole, self.block = wires, whole, block
+        self.got_pair, self.pair_block, self.got_line = got_pair, pair_block, got_line
+        self.pairs, self.lines = wires.slots(1), wires.slots(4)
+
+    def pair(self):
+        w = self.w
+        return w.copy(self.whole(1 - w.y), self.got_pair, w.pair_peer(), self.pairs)
+
+    def line(self, i):
+        w = self.w
+        z = (w.z + i) % 4
+        return w.copy(
+            self.block(w.y, z), self.got_line.at[i - 1], w.at(w.x, w.y, z, w.k), self.lines + i
+        )
+
+    def both(self, z):
+        return self.block(self.w.y, z)[...].astype(F32) + self.pair_block(z)[...].astype(F32)
+
+    def start(self):
+        self.pair().start()
+
+    def send(self):
+        w = self.w
+        self.pair().wait_recv()
+        for i in (2, 1, 3):
+            z = (w.z + i) % 4
+            self.block(w.y, z)[...] = self.both(z).astype(self.got_line.dtype)
+            self.line(i).start()
+
+    def finish(self):
+        total = self.both(self.w.z)
+        for i in (1, 3, 2):
+            self.line(i).wait_recv()
+            total += self.got_line[i - 1].astype(F32)
+        return total
+
+    def drain(self):
+        self.pair().wait_send()
+        for i in (1, 2, 3):
+            self.line(i).wait_send()
+
+
+def dots(left, right, dims):
+    return lax.dot_general(left, right, (dims, ((), ())), preferred_element_type=F32)
+
+
+NN, NT, TN = ((1,), (0,)), ((1,), (1,)), ((0,), (0,))
+
+
+def only_head(array, head):
+    lane = lax.broadcasted_iota(jnp.int32, array.shape, 1)
+    return jnp.where(lane // HEAD == head, array, jnp.zeros_like(array))
+
+
+def inverse_size(rows):
+    return lax.rsqrt(jnp.mean(rows * rows, axis=-1, keepdims=True) + EPS)
+
+
+def norm_back(rows, gain, upstream):
+    inverse = inverse_size(rows)
+    normed = rows * inverse
+    scaled = upstream * gain
+    grad_rows = inverse * (scaled - normed * jnp.mean(scaled * normed, axis=-1, keepdims=True))
+    return grad_rows, jnp.sum(upstream * normed, axis=0, keepdims=True)
+
+
+SCRATCH = [
+    ("rows_all", (2, 2, 2, 128, 1024), BF16),
+    ("cots_all", (2, 2, 2, 128, 1024), BF16),
+    ("ids_all", (2, 2, 1, 1024), jnp.int32),
+    ("heads_all", (2, 2, 4, 2, 32, 768), BF16),
+    ("out_all", (2, 2, 4, 2, 32, 1024), BF16),
+    ("hidden_all", (2, 2, 4, 2, 32, 2048), BF16),
+    ("down_all", (2, 4, 128, 1024), BF16),
+    ("gains_all", (2, 2, 4, 2, 16, 128), BF16),
+    ("heads_pack", (4, 32, 768), BF16),
+    ("hidden_pack", (4, 32, 2048), BF16),
+    ("normed", (1024, 1024), BF16),
+    ("query", (1024, 256), BF16),
+    ("keys", (1024, 256), BF16),
+    ("values", (1024, 256), BF16),
+    ("keys_turned", (256, 1024), BF16),
+    ("values_turned", (256, 1024), BF16),
+    ("mixed_turned", (256, 1024), BF16),
+    ("mixed_all", (2, 2, 256, 1024), BF16),
+    ("logsum", (4, 1, 1024), F32),
+    ("gain_rows", (2, 1, 1024), F32),
+    ("ids_row", (1, 1024), F32),
+    ("ids_col", (1024, 128), F32),
+    ("middle_keep", (2, 256, 1024), F32),
+    ("normed_two", (1024, 1024), BF16),
+    ("hidden", (1024, 1024), BF16),
+    ("grad_gate", (1024, 1024), BF16),
+    ("grad_up", (1024, 1024), BF16),
+    ("part_norm", (2, 2, 256, 1024), BF16),
+    ("core_out", (2, 256, 1024), BF16),
+    ("core_norm", (2, 256, 1024), BF16),
+    ("across_out", (2, 128, 1024), BF16),
+    ("across_norm", (2, 128, 1024), BF16),
+    ("branch", (2, 2, 2, 128, 1024), BF16),
+    ("grad_keys", (1024, 256), F32),
+    ("grad_values", (1024, 256), F32),
+    ("heads_part", (2, 2, 4, 2, 32, 768), BF16),
+    ("out_part", (4, 2, 32, 1024), BF16),
+    ("gains_part", (2, 4, 8, 128), F32),
+    ("heads_pair", (2, 4, 2, 32, 768), BF16),
+    ("hidden_pair", (2, 4, 2, 32, 2048), BF16),
+    ("down_pair", (4, 128, 1024), BF16),
+    ("out_pair", (4, 2, 32, 1024), BF16),
+    ("gains_pair", (4, 8, 128), F32),
+    ("heads_line", (3, 2, 2, 32, 768), BF16),
+    ("hidden_line", (3, 2, 2, 32, 2048), BF16),
+    ("down_line", (3, 128, 1024), BF16),
+    ("out_line", (3, 2, 32, 1024), BF16),
+    ("gains_line", (3, 8, 128), F32),
+    ("heads_dealt", (4, 32, 768), BF16),
+    ("hidden_dealt", (4, 32, 2048), BF16),
+    ("gains_deal", (8, 128), F32),
+    ("gains_dealt", (4, 8, 128), F32),
+    ("out_deal", (32, 1024), BF16),
+    ("out_home", (32, 1024), BF16),
+    ("done_out", (2, 128, 1024), BF16),
+    ("input_home", (2, 128, 1024), BF16),
+]
+
+
+def layer_body(
+    rows, cots, ids, wq, wk, wv, wo, wg, wu, wd, gains,
+    output, input_grad, q_out, k_out, v_out, o_out, g_out, u_out, d_out, gain_out,
+    *scratch,
+):
+    send, recv, local = scratch[-3:]
+    m = type("Memory", (), dict(zip([name for name, _, _ in SCRATCH], scratch)))
+    w = Wires(send, recv)
+    x, y, z, k = w.x, w.y, w.z, w.k
+    rank = 2 * x + k
+    w.greet(w.group_peers() + w.line_peers() + w.cross_peers() + [w.pair_peer()])
+
+    used = [0]
+
+    def spare():
+        used[0] += 1
+        return local.at[used[0] - 1]
+
+    def stay(source, target):
+        copy = pltpu.make_async_copy(source, target, spare())
+        copy.start()
+        return copy
+
+    def sequence_block(ref):
+        return lambda x, z: ref.at[z // 2, z % 2, x]
+
+    visit_rows = Visit(w, rows, sequence_block(m.rows_all), spare())
+    visit_rows.start()
+    pack_rows(head_columns, (wq, wk, wv), m.heads_pack)
+    deal_heads = Deal(
+        w, lambda x, k: m.heads_pack.at[2 * x + k], lambda sx, sk: m.heads_all.at[y, sk, z, sx]
+    )
+    deal_heads.start()
+    stays = [
+        stay(m.heads_pack.at[rank], m.heads_all.at[y, k, z, x]),
+        stay(wo, m.out_all.at[y, k, z, x]),
+        stay(gains, m.gains_all.at[y, k, z, x]),
+        stay(wd, m.down_all.at[y, z]),
+        stay(ids, m.ids_all.at[k]),
+    ]
+    swap = w.copy(ids, m.ids_all.at[k], w.at(x, y, z, 1 - k), w.slots(1))
+    swap.start()
+    spread_gains = Spread(w, lambda y, z: m.gains_all.at[y, k, z, x], gains)
+    spread_gains.start()
+    pack_rows(hidden_columns, (wg, wu), m.hidden_pack)
+    stays.append(stay(m.hidden_pack.at[rank], m.hidden_all.at[y, k, z, x]))
+    deal_hidden = Deal(
+        w, lambda x, k: m.hidden_pack.at[2 * x + k], lambda sx, sk: m.hidden_all.at[y, sk, z, sx]
+    )
+    for copy in stays:
+        copy.wait()
+    deal_heads.arrive()
+    spread_heads = Spread(w, lambda y, z: m.heads_all.at[y, :, z])
+    spread_heads.start()
+    visit_rows.arrive()
+    share_rows = Share(w, lambda x, k: m.rows_all.at[:, k, x])
+    share_rows.start()
+    deal_hidden.start()
+    for i in (1, 3, 2):
+        spread_gains.forward(i)
+    spread_out = Spread(w, lambda y, z: m.out_all.at[y, k, z, x], wo)
+    spread_out.start()
+    share_rows.forward()
+    deal_hidden.arrive()
+    spread_hidden = Spread(w, lambda y, z: m.hidden_all.at[y, :, z])
+    spread_hidden.start()
+    for i in (1, 3, 2):
+        spread_heads.forward(i)
+    for i in range(4):
+        spread_gains.arrive(i)
+    share_gains = Share(w, lambda x, k: m.gains_all.at[:, k, :, x])
+    share_gains.start()
+    swap.wait()
+    m.ids_row[...] = m.ids_all[z // 2, z % 2].astype(F32)
+    for j in range(8):
+        piece = slice(128 * j, 128 * j + 128)
+        m.ids_col[piece, :] = jnp.broadcast_to(m.ids_row[:, piece], (128, 128)).T
+    share_gains.forward()
+    share_rows.arrive()
+    share_gains.arrive()
+    for j in range(8):
+        four = [
+            m.gains_all[j // 4, (j // 2) % 2, 2 * (j % 2) + i // 2, i % 2].astype(F32)
+            for i in range(4)
+        ]
+        total = four[0] + four[1] + four[2] + four[3]
+        for i in range(2):
+            m.gain_rows[i, :, 128 * j : 128 * j + 128] = total[i : i + 1, :]
+
+    def first_norm(b, _):
+        block = m.rows_all[b // 2, b % 2].reshape(256, 1024).astype(F32)
+        span = pl.ds(pl.multiple_of(256 * b, 256), 256)
+        m.normed[span, :] = (block * inverse_size(block) * m.gain_rows[0]).astype(BF16)
+        return 0
+
+    lax.fori_loop(0, 4, first_norm, 0)
+    visit_cots = Visit(w, cots, sequence_block(m.cots_all), spare())
+    visit_cots.start()
+    for i in (1, 3, 2):
+        spread_out.forward(i)
+    for i in range(4):
+        spread_heads.arrive(i)
+    heads = m.heads_all[...].reshape(1024, 768)
+    for b in range(4):
+        span = slice(256 * b, 256 * b + 256)
+        made = dots(m.normed[span, :], heads, NN).astype(BF16)
+        m.query[span, :], m.keys[span, :] = made[:, :256], made[:, 256:512]
+        m.values[span, :] = made[:, 512:]
+        m.keys_turned[:, span] = made[:, 256:512].T
+        m.values_turned[:, span] = made[:, 512:].T
+    for i in range(4):
+        spread_out.arrive(i)
+    share_out = Share(w, lambda x, k: m.out_all.at[:, k, :, x])
+    share_out.start()
+    spread_down = Spread(w, lambda y, z: m.down_all.at[y, z], wd)
+    spread_down.start()
+    visit_cots.arrive()
+    share_cots = Share(w, lambda x, k: m.cots_all.at[:, k, x])
+    share_cots.start()
+
+    def bias_of(b):
+        start, count = 256 * b, 256 * b + 256
+        column = m.ids_col[:count, :]
+        same = jnp.concatenate([column, column], axis=1) == m.ids_row[:, start : start + 256]
+        key = lax.broadcasted_iota(jnp.int32, (count, 256), 0)
+        place = lax.broadcasted_iota(jnp.int32, (count, 256), 1) + start
+        return jnp.where(jnp.logical_and(same, key <= place), 0.0, -1e30).astype(F32)
+
+    def head_rows(h):
+        return pl.ds(pl.multiple_of(h * HEAD, HEAD), HEAD)
+
+    def rank_columns(x, k):
+        return pl.ds(pl.multiple_of(256 * (2 * x + k), 256), 256)
+
+    def mix(b):
+        span, count = slice(256 * b, 256 * b + 256), 256 * b + 256
+        bias = bias_of(b)
+
+        def one(h, _):
+            scores = dots(m.keys[:count, :], only_head(m.query[span, :], h), NT)
+            scores = scores * (HEAD**-0.5 * LOG2E) + bias
+            top = jnp.max(scores, axis=0, keepdims=True)
+            lifted = jnp.exp2(scores - top)
+            total = jnp.sum(lifted, axis=0, keepdims=True)
+            probs = (lifted * (1.0 / total)).astype(BF16)
+            mixed = dots(m.values_turned[head_rows(h), :count], probs, NN)
+            m.mixed_turned[head_rows(h), span] = mixed.astype(BF16)
+            m.logsum[h, :, span] = top + jnp.log2(total)
+            return 0
+
+        lax.fori_loop(0, 4, one, 0)
+        m.mixed_all[b // 2, b % 2, :, rank_columns(x, k)] = m.mixed_turned[:, span].T
+
+    def share_mixed(b):
+        return Share(w, lambda x, k: m.mixed_all.at[b // 2, b % 2, :, rank_columns(x, k)])
+
+    shares = [share_mixed(b) for b in range(4)]
+    mix(0)
+    shares[0].start()
+    spread_hidden.forward(1)
+    mix(1)
+    shares[1].start()
+    shares[0].forward()
+    share_out.forward()
+    share_cots.forward()
+    spread_hidden.forward(3)
+    mix(2)
+    shares[2].start()
+    shares[1].forward()
+    spread_hidden.forward(2)
+    mix(3)
+    shares[3].start()
+    shares[2].forward()
+    share_out.arrive()
+
+    for b in range(4):
+        span = slice(256 * b, 256 * b + 256)
+        if b == 2:
+            shares[3].forward()
+        shares[b].arrive()
+        middle = m.rows_all[b // 2, b % 2].reshape(256, 1024).astype(F32)
+        whole = m.out_all[...].reshape(1024, 1024)
+        middle = middle + dots(m.mixed_all[b // 2, b % 2], whole, NN)
+        m.normed_two[span, :] = (middle * inverse_size(middle) * m.gain_rows[1]).astype(BF16)
+
+        @pl.when(k == b % 2)
+        def _():
+            m.middle_keep[b // 2] = middle
+
+    for i in (1, 3, 2):
+        spread_down.forward(i)
+    for i in range(4):
+        spread_hidden.arrive(i)
+    for i in range(4):
+        spread_down.arrive(i)
+    share_cots.arrive()
+    for share in shares:
+        share.drain()
+    total_out = Total(w, m.mixed_all, m.core_out, m.across_out)
+    total_norm = Total(w, m.part_norm, m.core_norm, m.across_norm)
+
+    def feed(i, part):
+        span = pl.ds(pl.multiple_of(256 * (2 * i + part), 256), 256)
+        upstream = m.cots_all[i, part].reshape(256, 1024)
+        normed_two = m.normed_two[span, :]
+        for n in range(4):
+            columns = slice(256 * n, 256 * n + 256)
+            gate_tile = m.hidden_all[..., 256 * n : 256 * n + 256].reshape(1024, 256)
+            up_tile = m.hidden_all[..., 1024 + 256 * n : 1280 + 256 * n].reshape(1024, 256)
+            down_tile = m.down_all[n // 2, 2 * (n % 2) : 2 * (n % 2) + 2].reshape(256, 1024)
+            gate = dots(normed_two, gate_tile, NN)
+            upward = dots(normed_two, up_tile, NN)
+            grad_hidden = dots(upstream, down_tile, NT)
+            sigma = 1.0 / (1.0 + jnp.exp(-gate))
+            silu = gate * sigma
+            m.hidden[span, columns] = (silu * upward).astype(BF16)
+            m.grad_up[span, columns] = (grad_hidden * silu).astype(BF16)
+            m.grad_gate[span, columns] = (
+                grad_hidden * upward * (sigma + silu * (1.0 - sigma))
+            ).astype(BF16)
+        norm_part = dots(
+            m.grad_gate[span, :], m.hidden_all[..., :1024].reshape(1024, 1024), NT
+        ) + dots(m.grad_up[span, :], m.hidden_all[..., 1024:].reshape(1024, 1024), NT)
+        return span, norm_part
+
+    def out_of(span):
+        return dots(m.hidden[span, :], m.down_all[...].reshape(1024, 1024), NN)
+
+    def give(i, _):
+        span, norm_part = feed(i, 1 - k)
+        total_norm.give(i, norm_part)
+        total_out.give(i, out_of(span))
+        return 0
+
+    def keep(i, _):
+        span, norm_part = feed(i, k)
+        total_norm.keep(i, norm_part)
+        total_out.keep(i, out_of(span))
+        return 0
+
+    lax.fori_loop(0, 2, give, 0)
+    lax.fori_loop(0, 2, keep, 0)
+    spread_down.drain()
+    spread_hidden.drain()
+
+    def lanes(plane, half):
+        return pl.ds(pl.multiple_of(512 * plane + 256 * half, 256), 256)
+
+    def down_part(plane):
+        def one(half, _):
+            made = dots(m.hidden[:, lanes(plane, half)], m.cots_all[...].reshape(1024, 1024), TN)
+            m.down_all[plane, pl.ds(2 * half, 2)] = made.astype(BF16).reshape(2, 128, 1024)
+            return 0
+
+        lax.fori_loop(0, 2, one, 0)
+
+    def hidden_part(plane):
+        def one(half, _):
+            left = m.normed_two[:, lanes(plane, half)]
+            for j, right in enumerate((m.grad_gate, m.grad_up)):
+                made = dots(left, right[...], TN).astype(BF16).reshape(4, 2, 32, 1024)
+                m.hidden_all[plane, half, :, :, :, 1024 * j : 1024 * j + 1024] = made
+            return 0
+
+        lax.fori_loop(0, 2, one, 0)
+
+    fold_down = Fold(
+        w, lambda y: m.down_all.at[y], lambda y, z: m.down_all.at[y, z],
+        m.down_pair, lambda z: m.down_pair.at[z], m.down_line,
+    )
+    fold_hidden = Fold(
+        w, lambda y: m.hidden_all.at[y], lambda y, z: m.hidden_all.at[y, :, z],
+        m.hidden_pair, lambda z: m.hidden_pair.at[:, z], m.hidden_line,
+    )
+    fold_heads = Fold(
+        w, lambda y: m.heads_part.at[y], lambda y, z: m.heads_part.at[y, :, z],
+        m.heads_pair, lambda z: m.heads_pair.at[:, z], m.heads_line,
+    )
+    fold_gains = Fold(
+        w, lambda y: m.gains_part.at[y], lambda y, z: m.gains_part.at[y, z],
+        m.gains_pair, lambda z: m.gains_pair.at[z], m.gains_line,
+    )
+    down_part(1 - y)
+    fold_down.start()
+    hidden_part(1 - y)
+    fold_hidden.start()
+
+    share_branch = Share(w, lambda x, k: m.branch.at[:, k, x])
+    own_half = total_norm.rows(x)
+    gain_sum = jnp.zeros((1, 1024), F32)
+    for i in range(2):
+        grad, term = norm_back(
+            m.middle_keep[i, own_half], m.gain_rows[1], total_norm.take(i)
+        )
+        gain_sum = gain_sum + term
+        m.done_out[i] = (m.middle_keep[i, own_half] + total_out.take(i)).astype(BF16)
+        grad = grad + m.cots_all[i, k, x].astype(F32)
+        m.middle_keep[i, own_half] = grad
+        m.branch[i, k, x] = grad.astype(BF16)
+    share_branch.start()
+    return_out = Return(w, lambda i: m.done_out.at[i], output, spare())
+    return_out.start()
+
+    def gain_rows_part(row, total):
+        for plane in range(2):
+            for zz in range(4):
+                for half in range(2):
+                    at = 512 * plane + 256 * half + 128 * (zz // 2)
+                    m.gains_part[plane, zz, 2 * row + half : 2 * row + half + 1, :] = total[
+                        :, at : at + 128
+                    ]
+
+    m.gains_part[...] = jnp.zeros_like(m.gains_part)
+    gain_rows_part(1, gain_sum)
+    down_part(y)
+    share_branch.forward()
+    hidden_part(y)
+    share_branch.arrive()
+
+    grad_mixed, grad_mixed_turned = m.grad_up.at[:, :256], m.hidden.at[:256]
+    grad_heads = m.grad_gate.at[:, :768]
+    out_own = m.out_all[x, k].reshape(256, 1024)
+    for b in range(4):
+        span = slice(256 * b, 256 * b + 256)
+        made = dots(m.branch[b // 2, b % 2].reshape(256, 1024), out_own, NT).astype(BF16)
+        grad_mixed[span, :] = made
+        grad_mixed_turned[:, span] = made.T
+    m.out_part[...] = (
+        dots(m.mixed_turned[...], m.branch[...].reshape(1024, 1024), NN)
+        .astype(BF16)
+        .reshape(4, 2, 32, 1024)
+    )
+    base = w.slots(6)
+    owner = y == x
+    out_across = w.copy(m.out_part, m.out_pair, w.pair_peer(), base)
+    pl.when(jnp.logical_not(owner))(lambda: out_across.start())
+    m.grad_keys[...] = jnp.zeros_like(m.grad_keys)
+    m.grad_values[...] = jnp.zeros_like(m.grad_values)
+
+    def unmix(b):
+        span, count = slice(256 * b, 256 * b + 256), 256 * b + 256
+        bias = bias_of(b)
+
+        def one(h, _):
+            query, upstream = only_head(m.query[span, :], h), only_head(grad_mixed[span, :], h)
+            scores = dots(m.keys[:count, :], query, NT)
+            scores = scores * (HEAD**-0.5 * LOG2E) + bias
+            probs = jnp.exp2(scores - m.logsum[h, :, span])
+            grad_probs = dots(m.values[:count, :], upstream, NT)
+            centre = jnp.sum(
+                grad_mixed_turned[head_rows(h), span].astype(F32)
+                * m.mixed_turned[head_rows(h), span].astype(F32),
+                axis=0,
+                keepdims=True,
+            )
+            grad_scores = (probs * (grad_probs - centre)).astype(BF16)
+            turned = dots(m.keys_turned[head_rows(h), :count], grad_scores, NN)
+            grad_mixed_turned[head_rows(h), span] = (turned * HEAD**-0.5).astype(BF16)
+            m.grad_keys[:count, :] += dots(grad_scores, query, NN)
+            m.grad_values[:count, :] += dots(probs.astype(BF16), upstream, NN)
+            return 0
+
+        lax.fori_loop(0, 4, one, 0)
+        grad_heads[span, :256] = grad_mixed_turned[:, span].T
+
+    for b in range(4):
+        unmix(b)
+    grad_heads[:, 256:512] = (m.grad_keys[...] * HEAD**-0.5).astype(BF16)
+    grad_heads[:, 512:] = m.grad_values[...].astype(BF16)
+
+    def heads_part(plane):
+        for half in range(2):
+            made = dots(m.normed[:, lanes(plane, half)], grad_heads[...], TN)
+            m.heads_part[plane, half] = made.astype(BF16).reshape(4, 2, 32, 768)
+
+    heads_part(1 - y)
+    fold_heads.start()
+    total_norm.drain()
+    total_first = Total(w, m.part_norm, m.core_norm, m.across_norm)
+
+    def first_part(i, part):
+        span = pl.ds(pl.multiple_of(256 * (2 * i + part), 256), 256)
+        return dots(grad_heads[span, :], m.heads_all[...].reshape(1024, 768), NT)
+
+    for i in range(2):
+        total_first.give(i, first_part(i, 1 - k))
+    for i in range(2):
+        total_first.keep(i, first_part(i, k))
+    heads_part(y)
+    fold_down.send()
+    gain_sum = jnp.zeros((1, 1024), F32)
+
+    def done_in(i):
+        return m.normed_two.at[pl.ds(128 * i, 128)]
+
+    for i in range(2):
+        grad, term = norm_back(
+            m.rows_all[i, k, x].astype(F32), m.gain_rows[0], total_first.take(i)
+        )
+        gain_sum = gain_sum + term
+        done_in(i)[...] = (m.middle_keep[i, own_half] + grad).astype(BF16)
+    return_in = Return(w, done_in, m.input_home, spare())
+    return_in.start()
+    gain_rows_part(0, gain_sum)
+    fold_gains.start()
+
+    def out_piece(i):
+        zi = (z + i) % 4
+        return w.copy(m.out_part.at[zi], m.out_line.at[i - 1], w.at(x, y, zi, k), base + i)
+
+    @pl.when(owner)
+    def _():
+        out_across.wait_recv()
+        for i in (2, 1, 3):
+            zi = (z + i) % 4
+            m.out_part[zi] = (m.out_part[zi].astype(F32) + m.out_pair[zi].astype(F32)).astype(BF16)
+            out_piece(i).start()
+
+    fold_hidden.send()
+    d_out[...] = fold_down.finish()
+    fold_gains.send()
+    fold_heads.send()
+    return_in.arrive()
+    input_grad[...] = m.input_home[...].astype(F32)
+    out_last = w.copy(m.out_deal, m.out_home, w.at(1 - x, y, z, k), base + 4)
+
+    @pl.when(owner)
+    def _():
+        out_total = m.out_part[z].astype(F32) + m.out_pair[z].astype(F32)
+        for i in (1, 3, 2):
+            out_piece(i).wait_recv()
+            out_total += m.out_line[i - 1].astype(F32)
+        first, second = out_total[0], out_total[1]
+        m.out_deal[...] = jnp.where(x == 0, second, first).astype(BF16)
+        out_last.start()
+        o_out[...] = jnp.where(x == 0, first, second)
+
+    deal_hidden.drain()
+    deal_heads.drain()
+    m.hidden_pack[...] = fold_hidden.finish().astype(BF16).reshape(4, 32, 2048)
+    deal_hidden_grad = Deal(
+        w, lambda x, k: m.hidden_pack.at[2 * k + x], lambda x, k: m.hidden_dealt.at[2 * x + k]
+    )
+    deal_hidden_grad.start()
+    m.gains_deal[...] = fold_gains.finish()
+    m.gains_dealt[rank] = m.gains_deal[...]
+    deal_gains = Deal(w, lambda x, k: m.gains_deal, lambda x, k: m.gains_dealt.at[2 * x + k])
+    deal_gains.start()
+    m.heads_pack[...] = fold_heads.finish().astype(BF16).reshape(4, 32, 768)
+    deal_heads_grad = Deal(
+        w, lambda x, k: m.heads_pack.at[2 * k + x], lambda x, k: m.heads_dealt.at[2 * x + k]
+    )
+    deal_heads_grad.start()
+    m.hidden_dealt[rank] = m.hidden_pack[2 * k + x]
+    m.heads_dealt[rank] = m.heads_pack[2 * k + x]
+    deal_hidden_grad.arrive()
+    for r in range(4):
+        for half, target in enumerate((g_out, u_out)):
+            for j, (start, width) in enumerate(hidden_columns(r)):
+                at = 128 * j + half * 1024
+                target[:, start : start + width] = m.hidden_dealt[r, :, at : at + width].astype(F32)
+    deal_gains.arrive()
+    gain_out[...] = m.gains_dealt[0] + m.gains_dealt[1] + m.gains_dealt[2] + m.gains_dealt[3]
+    deal_heads_grad.arrive()
+    for r in range(4):
+        for j, target in enumerate((q_out, k_out, v_out)):
+            at = 256 * j
+            target[:, 256 * r : 256 * r + 256] = m.heads_dealt[r, :, at : at + 256].astype(F32)
+
+    @pl.when(jnp.logical_not(owner))
+    def _():
+        out_last.wait_recv()
+        o_out[...] = m.out_home[...].astype(F32)
+
+    return_out.arrive()
+    for part in [
+        visit_rows, visit_cots, spread_gains, spread_heads, spread_out,
+        share_rows, share_cots, share_gains, share_out, share_branch, total_out, total_first,
+        fold_down, fold_hidden, fold_heads, fold_gains, return_out, return_in,
+        deal_hidden_grad, deal_heads_grad, deal_gains,
+    ]:
+        part.drain()
+
+    @pl.when(owner)
+    def _():
+        for i in (1, 2, 3):
+            out_piece(i).wait_send()
+        out_last.wait_send()
+
+    pl.when(jnp.logical_not(owner))(lambda: out_across.wait_send())
+
+
+def grouped(
+    layer_input, doc_ids, attn_gain, query_weight, key_weight, value_weight, out_weight,
+    mlp_gain, gate_weight, up_weight, down_weight, out_grad,
+):
+    dp, ctx = lax.axis_index("dp"), lax.axis_index("ctx")
+    x, y, z, k = ctx % 2, dp // 2, ctx // 2, dp % 2
+    piece = attn_gain.shape[0]
+    lane = piece * (2 * (z % 2) + x)
+    gains = jnp.zeros((16, 128), BF16)
+    gains = lax.dynamic_update_slice(gains, jnp.stack([attn_gain, mlp_gain]), (0, lane))
+    d, f = layer_input.shape[2], gate_weight.shape[1]
+    outs = (
+        shaped(*layer_input.shape),
+        shaped(*layer_input.shape, dtype=F32),
+        shaped(piece, d, dtype=F32),
+        shaped(piece, d, dtype=F32),
+        shaped(piece, d, dtype=F32),
+        shaped(piece, d, dtype=F32),
+        shaped(piece, f, dtype=F32),
+        shaped(piece, f, dtype=F32),
+        shaped(*down_weight.shape, dtype=F32),
+        shaped(8, 128, dtype=F32),
+    )
+    rooms = [pltpu.VMEM(shape, dtype) for _, shape, dtype in SCRATCH]
+    made = pl.pallas_call(
+        layer_body,
+        name="layer",
+        out_shape=outs,
+        in_specs=[ANY, ANY, ANY, VMEM, VMEM, VMEM, ANY, VMEM, VMEM, ANY, ANY],
+        out_specs=(ANY,) + (VMEM,) * 9,
+        scratch_shapes=rooms
+        + [
+            pltpu.SemaphoreType.DMA((160,)),
+            pltpu.SemaphoreType.DMA((160,)),
+            pltpu.SemaphoreType.DMA((16,)),
+        ],
+        compiler_params=pltpu.CompilerParams(
+            collective_id=0, has_side_effects=True, vmem_limit_bytes=61 << 20
+        ),
+    )(
+        layer_input, out_grad, doc_ids.reshape(2, 1, -1), query_weight, key_weight, value_weight,
+        out_weight, gate_weight, up_weight, down_weight, gains,
+    )
+    output, input_grad, q, k_, v, o, g, u, down, gain = made
+
+    def gain_of(row):
+        return lax.dynamic_slice(gain, (row + k, lane), (1, piece)).reshape(piece)
+
+    return (output, input_grad, gain_of(0), q, k_, v, o, gain_of(2), g, u, down)
+
+
+def plain_product(left, right):
     return jnp.dot(left, right, preferred_element_type=jnp.float32)
 
 
-def product_left(left, right):
+def plain_product_left(left, right):
     return lax.dot_general(
         left, right, (((0,), (0,)), ((), ())), preferred_element_type=jnp.float32
     )
 
 
-def product_right(left, right):
+def plain_product_right(left, right):
     return lax.dot_general(
         left, right, (((1,), (1,)), ((), ())), preferred_element_type=jnp.float32
     )
@@ -30,7 +1019,7 @@
     return (rows * inverse * gain, inverse)
 
 
-def norm_back(rows, inverse, gain, upstream):
+def plain_norm_back(rows, inverse, gain, upstream):
     normed = rows * inverse
     scaled = upstream * gain
     grad_rows = inverse * (scaled - normed * jnp.mean(scaled * normed, axis=-1, keepdims=True))
@@ -52,7 +1041,7 @@
     return jnp.where(allowed[:, None], scores, -1e30)
 
 
-def attend(query, keys, values, allowed):
+def plain_attend(query, keys, values, allowed):
     groups, rows, width = query.shape
 
     def step(index, carry):
@@ -81,7 +1070,7 @@
     return lax.fori_loop(0, width // (2 * HEAD), step, start_state)
 
 
-def attend_back(query, keys, values, allowed, logsum, grad_mixed):
+def plain_attend_back(query, keys, values, allowed, logsum, grad_mixed):
     groups, rows, width = query.shape
     length = keys.shape[1]
     scale = HEAD ** (-0.5)
@@ -184,24 +1173,24 @@
     gain_attn = gain_one.astype(jnp.float32)
     normed_full, inverse_one = normalize(inputs, gain_attn)
     normed = normed_full.astype(jnp.bfloat16)
-    query = product(normed, w_query).astype(jnp.bfloat16).reshape(groups, rows, width)
-    keys_own = product(normed, w_key).astype(jnp.bfloat16).reshape(groups, rows, width)
-    values_own = product(normed, w_value).astype(jnp.bfloat16).reshape(groups, rows, width)
+    query = plain_product(normed, w_query).astype(jnp.bfloat16).reshape(groups, rows, width)
+    keys_own = plain_product(normed, w_key).astype(jnp.bfloat16).reshape(groups, rows, width)
+    values_own = plain_product(normed, w_value).astype(jnp.bfloat16).reshape(groups, rows, width)
     keys, values = (
         lax.all_gather(keys_own, "ctx", axis=1, tiled=True),
         lax.all_gather(values_own, "ctx", axis=1, tiled=True),
     )
-    attended, logsum = attend(query, keys, values, allowed)
+    attended, logsum = plain_attend(query, keys, values, allowed)
     attended_rows = attended.reshape(groups * rows, width)
-    middle = inputs + product(attended_rows, w_out)
+    middle = inputs + plain_product(attended_rows, w_out)
     gain_mlp = gain_two.astype(jnp.float32)
     normed_two_full, inverse_two = normalize(middle, gain_mlp)
     normed_two = normed_two_full.astype(jnp.bfloat16)
-    gate = product(normed_two, w_gate)
-    upward = product(normed_two, w_up)
+    gate = plain_product(normed_two, w_gate)
+    upward = plain_product(normed_two, w_up)
     sigma = jax.nn.sigmoid(gate)
     hidden = (gate * sigma * upward).astype(jnp.bfloat16)
-    layer_output = (middle + product(hidden, w_down)).astype(jnp.bfloat16)
+    layer_output = (middle + plain_product(hidden, w_down)).astype(jnp.bfloat16)
     gathered_back = (
         lax.all_gather(attn_gain, ("dp", "ctx"), axis=0, tiled=True),
         lax.all_gather(query_weight, ("dp", "ctx"), axis=0, tiled=True),
@@ -215,23 +1204,23 @@
     )
     gain_one, w_query, w_key, w_value, w_out, gain_two, w_gate, w_up, w_down = gathered_back
     upstream = out_grad.reshape(groups * rows, width)
-    down_grad = product_left(hidden, upstream)
-    grad_hidden = product_right(upstream, w_down)
+    down_grad = plain_product_left(hidden, upstream)
+    grad_hidden = plain_product_right(upstream, w_down)
     grad_gate = (grad_hidden * upward * sigma * (1.0 + gate * (1.0 - sigma))).astype(jnp.bfloat16)
     grad_up = (grad_hidden * gate * sigma).astype(jnp.bfloat16)
-    gate_grad = product_left(normed_two, grad_gate)
-    up_grad = product_left(normed_two, grad_up)
-    grad_normed_two = product_right(grad_gate, w_gate) + product_right(grad_up, w_up)
-    grad_middle, mlp_gain_grad = norm_back(
+    gate_grad = plain_product_left(normed_two, grad_gate)
+    up_grad = plain_product_left(normed_two, grad_up)
+    grad_normed_two = plain_product_right(grad_gate, w_gate) + plain_product_right(grad_up, w_up)
+    grad_middle, mlp_gain_grad = plain_norm_back(
         middle, inverse_two, gain_two.astype(jnp.float32), grad_normed_two
     )
     grad_middle = grad_middle + upstream.astype(jnp.float32)
     grad_branch = grad_middle.astype(jnp.bfloat16)
-    out_proj_grad = product_left(attended_rows, grad_branch)
+    out_proj_grad = plain_product_left(attended_rows, grad_branch)
     grad_attended = (
-        product_right(grad_branch, w_out).astype(jnp.bfloat16).reshape(groups, rows, width)
-    )
-    grad_query, grad_keys_all, grad_values_all = attend_back(
+        plain_product_right(grad_branch, w_out).astype(jnp.bfloat16).reshape(groups, rows, width)
+    )
+    grad_query, grad_keys_all, grad_values_all = plain_attend_back(
         query, keys, values, allowed, logsum, grad_attended
     )
     grad_keys, grad_values = (
@@ -245,15 +1234,15 @@
     grad_query = grad_query.astype(jnp.bfloat16).reshape(groups * rows, width)
     grad_keys = grad_keys.astype(jnp.bfloat16).reshape(groups * rows, width)
     grad_values = grad_values.astype(jnp.bfloat16).reshape(groups * rows, width)
-    query_grad = product_left(normed, grad_query)
-    key_grad = product_left(normed, grad_keys)
-    value_grad = product_left(normed, grad_values)
+    query_grad = plain_product_left(normed, grad_query)
+    key_grad = plain_product_left(normed, grad_keys)
+    value_grad = plain_product_left(normed, grad_values)
     grad_normed = (
-        product_right(grad_query, w_query)
-        + product_right(grad_keys, w_key)
-        + product_right(grad_values, w_value)
-    )
-    grad_inputs, attn_gain_grad = norm_back(
+        plain_product_right(grad_query, w_query)
+        + plain_product_right(grad_keys, w_key)
+        + plain_product_right(grad_values, w_value)
+    )
+    grad_inputs, attn_gain_grad = plain_norm_back(
         inputs, inverse_one, gain_one.astype(jnp.float32), grad_normed
     )
     input_grad = (grad_middle + grad_inputs).reshape(groups, rows, width)
@@ -298,8 +1287,10 @@
         P(("dp", "ctx"), None),
         P("dp", "ctx", None),
     )
+    fits = mesh.shape["dp"] == 4 and mesh.shape["ctx"] == 8
+    body = grouped if fits else on_device
     return jax.shard_map(
-        on_device,
+        body,
         mesh=mesh,
         in_specs=placed,
         out_specs=(

time: 2620 us -> 353 us (0.13)
  waiting for transfers between devices: 2230 us -> 0 us
  Pallas kernels: 0 us -> 340 us
  matrix products: 155 us -> 0 us
  local copies, waits for them, and re-layouts: 108 us -> 12.2 us
  blocking collectives: 79.4 us -> 0 us
    reduce_scatter x9 -> x0, waiting for transfers between devices: 1730 us -> none  [the longest x1 363 us: on_device(): lax.psum_scatter(gate_grad, ('dp', 'ctx'), scatter_dimension=0, tiled=True)]
    all_gather x9 -> x0, waiting for transfers between devices: 490 us -> none  [the longest x1 77.6 us: on_device(): lax.all_gather(gate_weight, ('dp', 'ctx'), axis=0, tiled=True)]
    pallas_call x0 -> x1, Pallas kernels: none -> 340 us  [grouped(): pl.pallas_call(layer_body, name='layer', out_shape=outs, in_specs=[ANY, A...]
    dot_general x77 -> x0, matrix products: 155 us -> none  [the longest x7 42.4 us: product_left(): lax.dot_general(left, right, (((0,), (0,)), ((), ())), preferred_element_...]
    unnamed x2 -> x0, blocking collectives: 79.4 us -> none
    dynamic_slice x65 -> x0, local copies, waits for them, and re-layouts: 56.3 us -> none  [the longest x56 56.3 us: head_pair(): piece = lax.dynamic_slice_in_dim(array, start, 2 * HEAD, 2)]
  transfers between devices with their start and end apart: 18 -> 0, of which waited for: 18 -> 0; matrix products, arithmetic and copies ran while one was open for 6% -> 0% of each run, Pallas kernels for 0% -> 0%
where the time goes in v2:
time: 353 us
  Pallas kernels  340 us (96%)
  local copies, waits for them, and re-layouts  12.2 us (3%)
    pallas_call x1, Pallas kernels, grouped(): pl.pallas_call(layer_body, name='layer', out_shape=outs, in_specs=[ANY, A...  340 us
    unnamed x33, local copies, waits for them, and re-layouts  9.69 us

profile of v2, /device:TPU:19, one launch (start us, length us, event | category | flops | bytes accessed | tf_op | source)
XLA Modules:
  0.0 352.9 jit_solution(18037406122917328672)
XLA Ops:
  0.7 0.0 copy-start.10
  0.7 0.0 copy-start.11
  0.7 0.0 copy-start.9
  0.7 0.6 copy-done.10
  1.4 0.0 copy-done.11
  1.4 0.5 dynamic_update_slice.3.gains
  1.9 0.0 copy-done.9
  1.9 0.0 copy-start.8
  1.9 0.6 reshape.31.ids
  2.5 0.0 copy-done.8
  2.5 339.9 %layer.1 = (bf16[2,128,1024]{2,1,0:T(8,128)(2,1)}, f32[2,128,1024]{2,1,0:T(8,128)}, f32[32,1024]{1,0:T(8,128)}, f32[32,1024]{1,0:T(8,128)}, f32[32,1024]{1,0:T(8...) custom-call(bf16[2,128,1024]{2,1,0:T(8,128)(2,1)} %rows.1, ...), custom_call_target="tpu_custom_call" | custom-call | tf_op jit(solution)/shard_map/layer/pallas_call | solution.py:974
  342.5 0.0 copy-start
  342.5 1.4 dynamic-slice_bitcast_fusion
  343.9 1.9 copy.33
  345.8 0.0 copy-done
  345.8 0.0 copy-start.7
  345.8 0.0 copy-start.6
  345.8 0.0 copy-start.5
  345.8 1.0 copy.34
  346.7 0.0 copy-done.7
  346.8 0.0 copy-start.3
  346.8 0.7 copy.35
  347.4 0.0 copy-done.6
  347.4 0.7 copy.36
  348.1 0.0 copy-done.5
  348.1 0.0 copy-start.4
  348.1 0.7 copy.37
  348.7 0.3 copy-done.4
  349.0 0.7 copy.38
  349.7 0.0 copy-done.3
  349.7 0.0 copy-start.2
  349.7 0.8 copy.39
  350.5 0.4 copy-done.2
  350.9 0.0 copy-start.1
  350.9 0.8 copy.40
  351.7 0.4 copy-done.1
  352.1 0.8 copy.41
  (2 shorter events, 0.0 us)
Async XLA Ops:
  0.7 0.7 copy-start.10
  0.7 0.7 copy-start.11
  0.7 1.2 copy-start.9
  1.9 0.6 copy-start.8
  342.5 3.3 copy-start
  345.8 1.0 copy-start.7
  345.8 1.7 copy-start.6
  345.8 2.3 copy-start.5
  346.8 2.9 copy-start.3
  348.1 1.0 copy-start.4
  349.7 1.2 copy-start.2
  350.9 1.2 copy-start.1

commit v3 on v2

--- a/solution.py
+++ b/solution.py
@@ -23,7 +23,8 @@
     def __init__(self, send, recv):
         dp, ctx = lax.axis_index("dp"), lax.axis_index("ctx")
         self.x, self.y = ctx % 2, dp // 2
-        self.z, self.k = ctx // 2, dp % 2
+        self.zh, self.zb = ctx // 4, (ctx // 2) % 2
+        self.zl, self.k = (self.zb + self.zh) % 2, dp % 2
         self.send, self.recv = send, recv
         self.used = 0
 
@@ -32,8 +33,19 @@
         self.used += count
         return first
 
-    def at(self, x, y, z, k):
-        return (2 * y + k, 2 * z + x)
+    def at(self, x=None, y=None, zh=None, zl=None, k=None):
+        x = self.x if x is None else x
+        y = self.y if y is None else y
+        zh = self.zh if zh is None else zh
+        zl = self.zl if zl is None else zl
+        k = self.k if k is None else k
+        return (2 * y + k, 4 * zh + 2 * ((zl + zh) % 2) + x)
+
+    def across(self):
+        return self.at(zl=1 - self.zl)
+
+    def core(self):
+        return self.at(k=1 - self.k)
 
     def copy(self, source, target, device, slot, recv_slot=None):
         return pltpu.make_async_remote_copy(
@@ -45,79 +57,95 @@
             device_id_type=MESH,
         )
 
-    def greet(self, peers):
+    def greet(self):
         barrier = pltpu.get_barrier_semaphore()
+        peers = [self.at(y=1 - self.y)]
+        for n in range(1, 16):
+            bits = [(n >> i) % 2 for i in range(4)]
+            x, zh, zl, k = [
+                1 - own if bit else own
+                for own, bit in zip((self.x, self.zh, self.zl, self.k), bits)
+            ]
+            peers.append(self.at(x=x, zh=zh, zl=zl, k=k))
         for peer in peers:
             pl.semaphore_signal(barrier, inc=1, device_id=peer, device_id_type=MESH)
         pl.semaphore_wait(barrier, len(peers))
 
-    def group_peers(self):
-        x, y, z, k = self.x, self.y, self.z, self.k
-        return [self.at(1 - x, y, z, k), self.at(x, y, z, 1 - k), self.at(1 - x, y, z, 1 - k)]
-
-    def line_peers(self):
-        x, y, z, k = self.x, self.y, self.z, self.k
-        return [self.at(x, y, (z + i) % 4, k) for i in (1, 2, 3)]
-
-    def cross_peers(self):
-        x, y, z, k = self.x, self.y, self.z, self.k
-        return [self.at(x, y, (z + i) % 4, 1 - k) for i in (1, 2, 3)]
-
-    def pair_peer(self):
-        return self.at(self.x, 1 - self.y, self.z, self.k)
-
-
-class Spread:
-    def __init__(self, wires, block, own=None):
-        self.w, self.block, self.own = wires, block, own
-        self.lines, self.pairs = wires.slots(4), wires.slots(4)
-
-    def line(self, i, z, own=None):
+
+class Pairs:
+    def __init__(self, wires, order):
+        self.w, self.order = wires, order
+
+    def place(self, z, a, b):
         w = self.w
-        ref = self.block(w.y, z)
-        target = w.at(w.x, w.y, (w.z + i) % 4, w.k)
-        return w.copy(ref if own is None else own, ref, target, self.lines + i)
-
-    def pair(self, i, y, own=None):
-        w = self.w
-        ref = self.block(y, (w.z + 4 - i) % 4)
-        return w.copy(ref if own is None else own, ref, w.pair_peer(), self.pairs + i)
+        x, y = (a, b) if self.order == "xy" else (b, a)
+        flip = lambda own, turn: 1 - own if turn else own
+        return flip(w.x, x), flip(w.y, y), flip(w.zh, z)
+
+    def partner(self, z, a, b):
+        x, y, zh = self.place(z, a, b)
+        return self.w.at(x=x, y=y, zh=zh)
+
+
+class Spread(Pairs):
+    SENDS = ((0, 0, 0), (0, 0, 0), (1, 0, 0), (0, 0, 0), (1, 0, 0), (0, 1, 0), (1, 1, 0))
+    STEPS = ((1, 0, 0), (0, 1, 0), (0, 1, 0), (0, 0, 1), (0, 0, 1), (0, 0, 1), (0, 0, 1))
+
+    def __init__(self, wires, order, block, own=None):
+        super().__init__(wires, order)
+        self.block, self.own = block, own
+        self.first = wires.slots(7)
+
+    def piece(self, n):
+        ref = self.block(*self.place(*self.SENDS[n]))
+        source = self.own if self.own is not None and not any(self.SENDS[n]) else ref
+        return self.w.copy(source, ref, self.partner(*self.STEPS[n]), self.first + n)
+
+    def landed(self, n):
+        came = [i ^ j for i, j in zip(self.SENDS[n], self.STEPS[n])]
+        ref = self.block(*self.place(*came))
+        return self.w.copy(ref, ref, self.partner(*self.STEPS[n]), self.first + n)
 
     def start(self):
-        for i in (2, 1, 3):
-            self.line(i, self.w.z, self.own).start()
-        self.pair(0, self.w.y, self.own).start()
-
-    def forward(self, i):
-        self.line(i, (self.w.z + 4 - i) % 4).wait_recv()
-        self.pair(i, self.w.y).start()
-
-    def arrive(self, i):
-        self.pair(i, 1 - self.w.y).wait_recv()
+        for n in (0, 1, 3):
+            self.piece(n).start()
+
+    def got_first(self):
+        self.landed(1).wait_recv()
+        self.piece(5).start()
+
+    def got_z(self):
+        self.landed(0).wait_recv()
+        self.piece(2).start()
+        self.piece(4).start()
+
+    def got_last(self):
+        self.landed(2).wait_recv()
+        self.piece(6).start()
+
+    def arrive(self):
+        for n in (3, 4, 5, 6):
+            self.landed(n).wait_recv()
 
     def drain(self):
-        for i in (1, 2, 3):
-            self.line(i, self.w.z, self.own).wait_send()
-        for i in range(4):
-            self.pair(i, self.w.y).wait_send()
+        for n in range(7):
+            self.piece(n).wait_send()
 
 
 class Share:
-    def __init__(self, wires, block, own=None):
-        self.w, self.block, self.own = wires, block, own
+    def __init__(self, wires, block):
+        self.w, self.block = wires, block
         self.first = wires.slots(3)
 
     def piece(self, i):
         w = self.w
-        core, across = w.at(w.x, w.y, w.z, 1 - w.k), w.at(1 - w.x, w.y, w.z, w.k)
-        ref = self.block(w.x if i < 2 else 1 - w.x, w.k)
-        source = ref if self.own is None or i == 2 else self.own
-        return w.copy(source, ref, across if i == 0 else core, self.first + i)
+        ref = self.block(w.zl if i < 2 else 1 - w.zl, w.k)
+        return w.copy(ref, ref, w.across() if i == 0 else w.core(), self.first + i)
 
     def landed(self, i):
         w = self.w
-        ref = self.block(*[(1 - w.x, w.k), (w.x, 1 - w.k), (1 - w.x, 1 - w.k)][i])
-        return w.copy(ref, ref, w.at(w.x, w.y, w.z, 1 - w.k), self.first + i)
+        ref = self.block(*[(1 - w.zl, w.k), (w.zl, 1 - w.k), (1 - w.zl, 1 - w.k)][i])
+        return w.copy(ref, ref, w.core(), self.first + i)
 
     def start(self):
         self.piece(0).start()
@@ -143,19 +171,19 @@
 
     def mate(self, i):
         w = self.w
-        return [(1 - w.x, w.k), (w.x, 1 - w.k), (1 - w.x, 1 - w.k)][i]
+        return [(1 - w.zl, w.k), (w.zl, 1 - w.k), (1 - w.zl, 1 - w.k)][i]
 
     def piece(self, i):
         w = self.w
-        x, k = self.mate(i)
+        zl, k = self.mate(i)
         return w.copy(
-            self.outgoing(x, k), self.incoming(w.x, w.k), w.at(x, w.y, w.z, k), self.first + i
+            self.outgoing(zl, k), self.incoming(w.zl, w.k), w.at(zl=zl, k=k), self.first + i
         )
 
     def landed(self, i):
-        x, k = self.mate(i)
-        ref = self.incoming(x, k)
-        return self.w.copy(ref, ref, self.w.at(x, self.w.y, self.w.z, k), self.first + i)
+        zl, k = self.mate(i)
+        ref = self.incoming(zl, k)
+        return self.w.copy(ref, ref, self.w.at(zl=zl, k=k), self.first + i)
 
     def start(self):
         for i in range(3):
@@ -168,6 +196,13 @@
     def drain(self):
         for i in range(3):
             self.piece(i).wait_send()
+
+
+def every(*tests):
+    all_of = tests[0]
+    for test in tests[1:]:
+        all_of = jnp.logical_and(all_of, test)
+    return all_of
 
 
 class Visit:
@@ -175,29 +210,27 @@
         self.w, self.home, self.full, self.local = wires, home, full, local
         self.first = wires.slots(2)
         w = wires
-        self.own = [jnp.logical_and(w.z == 2 * w.k + j, w.z % 2 == w.k) for j in range(2)]
+        self.own = [every(w.x == j, w.zh == w.k, w.zl == w.x, w.zb == w.k) for j in range(2)]
+        self.here = [every(w.zh == i, w.zl == w.x, w.zb == w.k, w.zh == w.k) for i in range(2)]
 
     def piece(self, j):
         w = self.w
         return w.copy(
             self.home.at[j],
-            self.full(w.x, w.z),
-            w.at(w.x, w.y, 2 * w.k + j, w.z % 2),
+            self.full(w.zh, w.zb, w.x),
+            w.at(x=j, zh=w.k, zl=w.x, k=w.zb),
             self.first + j,
-            self.first + w.z // 2,
+            self.first + w.zh,
         )
 
     def stay(self, j):
-        return pltpu.make_async_copy(self.home.at[j], self.full(self.w.x, self.w.z), self.local)
+        w = self.w
+        return pltpu.make_async_copy(self.home.at[j], self.full(w.zh, w.zb, w.x), self.local)
 
     def landed(self, i):
         w = self.w
-        ref = self.full(w.x, w.k + 2 * i)
-        return w.copy(ref, ref, w.pair_peer(), self.first + i)
-
-    def here(self, i):
-        w = self.w
-        return jnp.logical_and(w.k + 2 * i == w.z, w.z // 2 == w.k)
+        ref = self.full(i, w.k, w.zl)
+        return w.copy(ref, ref, w.core(), self.first + i)
 
     def start(self):
         for j in range(2):
@@ -208,7 +241,7 @@
         for j in range(2):
             pl.when(self.own[j])(lambda: self.stay(j).wait())
         for i in range(2):
-            pl.when(jnp.logical_not(self.here(i)))(lambda: self.landed(i).wait_recv())
+            pl.when(jnp.logical_not(self.here[i]))(lambda: self.landed(i).wait_recv())
 
     def drain(self):
         for j in range(2):
@@ -219,46 +252,41 @@
     def __init__(self, wires, done, home, local):
         self.w, self.done, self.home, self.local = wires, done, home, local
         self.first = wires.slots(2)
-
-    def own(self, i):
-        w = self.w
-        return jnp.logical_and(2 * i + w.k == w.z, w.z // 2 == w.k)
+        w = wires
+        self.own = [every(w.x == w.zl, w.zh == i, w.zb == w.k, w.k == w.zh) for i in range(2)]
+        self.here = [every(w.x == j, w.zh == w.k, w.zl == w.x, w.zb == w.k) for j in range(2)]
 
     def piece(self, i):
         w = self.w
         return w.copy(
             self.done(i),
-            self.home.at[w.z % 2],
-            w.at(w.x, w.y, 2 * i + w.k, w.z // 2),
+            self.home.at[w.x],
+            w.at(x=w.zl, zh=i, zl=(w.k + i) % 2, k=w.zh),
             self.first + i,
-            self.first + w.z % 2,
+            self.first + w.x,
         )
 
     def stay(self, i):
-        return pltpu.make_async_copy(self.done(i), self.home.at[self.w.z % 2], self.local)
-
-    def here(self, j):
-        w = self.w
-        return jnp.logical_and(2 * w.k + j == w.z, w.z % 2 == w.k)
+        return pltpu.make_async_copy(self.done(i), self.home.at[self.w.x], self.local)
 
     def landed(self, j):
         ref = self.home.at[j]
-        return self.w.copy(ref, ref, self.w.pair_peer(), self.first + j)
+        return self.w.copy(ref, ref, self.w.core(), self.first + j)
 
     def start(self):
         for i in range(2):
-            pl.when(self.own(i))(lambda: self.stay(i).start())
-            pl.when(jnp.logical_not(self.own(i)))(lambda: self.piece(i).start())
+            pl.when(self.own[i])(lambda: self.stay(i).start())
+            pl.when(jnp.logical_not(self.own[i]))(lambda: self.piece(i).start())
 
     def arrive(self):
         for i in range(2):
-            pl.when(self.own(i))(lambda: self.stay(i).wait())
+            pl.when(self.own[i])(lambda: self.stay(i).wait())
         for j in range(2):
-            pl.when(jnp.logical_not(self.here(j)))(lambda: self.landed(j).wait_recv())
+            pl.when(jnp.logical_not(self.here[j]))(lambda: self.landed(j).wait_recv())
 
     def drain(self):
         for i in range(2):
-            pl.when(jnp.logical_not(self.own(i)))(lambda: self.piece(i).wait_send())
+            pl.when(jnp.logical_not(self.own[i]))(lambda: self.piece(i).wait_send())
 
 
 def shaped(*shape, dtype=BF16):
@@ -279,8 +307,13 @@
 
 
 def hidden_columns(rank):
-    x, k = rank // 2, rank % 2
-    return [(128 * (8 * (2 * y + k) + 2 * z + x), 128) for y in range(2) for z in range(4)]
+    zl, k = rank // 2, rank % 2
+    return [
+        (128 * (16 * y + 8 * k + 4 * zh + 2 * (zl ^ zh) + x), 128)
+        for y in range(2)
+        for zh in range(2)
+        for x in range(2)
+    ]
 
 
 class Total:
@@ -292,7 +325,7 @@
     def core(self, i):
         w = self.w
         return w.copy(
-            self.part.at[0, i], self.got_core.at[i], w.at(w.x, w.y, w.z, 1 - w.k), self.first + i
+            self.part.at[0, i], self.got_core.at[i], w.core(), self.first + i
         )
 
     def rows(self, x):
@@ -301,9 +334,9 @@
     def across(self, i):
         w = self.w
         return w.copy(
-            self.part.at[1, i, self.rows(1 - w.x)],
+            self.part.at[1, i, self.rows(1 - w.zl)],
             self.got_across.at[i],
-            w.at(1 - w.x, w.y, w.z, w.k),
+            w.across(),
             self.first + 2 + i,
         )
 
@@ -318,7 +351,7 @@
 
     def take(self, i):
         self.across(i).wait_recv()
-        own = self.part[1, i, self.rows(self.w.x)]
+        own = self.part[1, i, self.rows(self.w.zl)]
         return own.astype(F32) + self.got_across[i].astype(F32)
 
     def drain(self):
@@ -327,48 +360,69 @@
             self.across(i).wait_send()
 
 
-class Fold:
-    def __init__(self, wires, whole, block, got_pair, pair_block, got_line):
-        self.w, self.whole, self.block = wires, whole, block
-        self.got_pair, self.pair_block, self.got_line = got_pair, pair_block, got_line
-        self.pairs, self.lines = wires.slots(1), wires.slots(4)
-
-    def pair(self):
+class Fold(Pairs):
+    def __init__(self, wires, order, whole, block, got_b, got_b_block, got_a, got_z):
+        super().__init__(wires, order)
+        self.whole, self.block = whole, block
+        self.got_b, self.got_b_block, self.got_a, self.got_z = got_b, got_b_block, got_a, got_z
+        self.first = wires.slots(4)
+
+    def stage_b(self):
         w = self.w
-        return w.copy(self.whole(1 - w.y), self.got_pair, w.pair_peer(), self.pairs)
-
-    def line(self, i):
-        w = self.w
-        z = (w.z + i) % 4
-        return w.copy(
-            self.block(w.y, z), self.got_line.at[i - 1], w.at(w.x, w.y, z, w.k), self.lines + i
-        )
-
-    def both(self, z):
-        return self.block(self.w.y, z)[...].astype(F32) + self.pair_block(z)[...].astype(F32)
+        b = w.y if self.order == "xy" else w.x
+        return w.copy(self.whole(1 - b), self.got_b, self.partner(0, 0, 1), self.first)
+
+    def stage_a(self, z):
+        x, y, zh = self.place(z, 1, 0)
+        return self.w.copy(
+            self.block(x, y, zh), self.got_a.at[zh], self.partner(0, 1, 0), self.first + 1 + z,
+            self.first + 1 + z,
+        )
+
+    def landed_a(self, z):
+        x, y, zh = self.place(z, 0, 0)
+        ref = self.got_a.at[zh]
+        return self.w.copy(ref, ref, self.partner(0, 1, 0), self.first + 1 + z)
+
+    def stage_z(self):
+        ref = self.block(*self.place(1, 0, 0))
+        return self.w.copy(ref, self.got_z, self.partner(1, 0, 0), self.first + 3)
+
+    def two(self, z, a):
+        x, y, zh = self.place(z, a, 0)
+        own = self.block(x, y, zh)[...].astype(F32)
+        return own + self.got_b_block(x if self.order == "xy" else y, zh)[...].astype(F32)
+
+    def three(self, z):
+        return self.two(z, 0) + self.got_a[self.place(z, 0, 0)[2]].astype(F32)
 
     def start(self):
-        self.pair().start()
-
-    def send(self):
-        w = self.w
-        self.pair().wait_recv()
-        for i in (2, 1, 3):
-            z = (w.z + i) % 4
-            self.block(w.y, z)[...] = self.both(z).astype(self.got_line.dtype)
-            self.line(i).start()
+        self.stage_b().start()
+
+    def second(self):
+        self.stage_b().wait_recv()
+        for z in (1, 0):
+            ref = self.block(*self.place(z, 1, 0))
+            ref[...] = self.two(z, 1).astype(self.got_z.dtype)
+            self.stage_a(z).start()
+
+    def third(self):
+        self.landed_a(1).wait_recv()
+        ref = self.block(*self.place(1, 0, 0))
+        ref[...] = self.three(1).astype(self.got_z.dtype)
+        self.stage_z().start()
 
     def finish(self):
-        total = self.both(self.w.z)
-        for i in (1, 3, 2):
-            self.line(i).wait_recv()
-            total += self.got_line[i - 1].astype(F32)
-        return total
+        self.landed_a(0).wait_recv()
+        total = self.three(0)
+        self.stage_z().wait_recv()
+        return total + self.got_z[...].astype(F32)
 
     def drain(self):
-        self.pair().wait_send()
-        for i in (1, 2, 3):
-            self.line(i).wait_send()
+        self.stage_b().wait_send()
+        for z in range(2):
+            self.stage_a(z).wait_send()
+        self.stage_z().wait_send()
 
 
 def dots(left, right, dims):
@@ -399,13 +453,15 @@
     ("rows_all", (2, 2, 2, 128, 1024), BF16),
     ("cots_all", (2, 2, 2, 128, 1024), BF16),
     ("ids_all", (2, 2, 1, 1024), jnp.int32),
-    ("heads_all", (2, 2, 4, 2, 32, 768), BF16),
-    ("out_all", (2, 2, 4, 2, 32, 1024), BF16),
-    ("hidden_all", (2, 2, 4, 2, 32, 2048), BF16),
-    ("down_all", (2, 4, 128, 1024), BF16),
-    ("gains_all", (2, 2, 4, 2, 16, 128), BF16),
+    ("heads_all", (2, 2, 2, 2, 2, 32, 768), BF16),
+    ("out_all", (2, 2, 2, 2, 2, 32, 1024), BF16),
+    ("gate_all", (2, 2, 2, 2, 2, 32, 1024), BF16),
+    ("up_all", (2, 2, 2, 2, 2, 32, 1024), BF16),
+    ("down_all", (2, 2, 2, 128, 1024), BF16),
+    ("gains_all", (2, 2, 2, 2, 2, 16, 128), BF16),
     ("heads_pack", (4, 32, 768), BF16),
-    ("hidden_pack", (4, 32, 2048), BF16),
+    ("gate_pack", (4, 32, 1024), BF16),
+    ("up_pack", (4, 32, 1024), BF16),
     ("normed", (1024, 1024), BF16),
     ("query", (1024, 256), BF16),
     ("keys", (1024, 256), BF16),
@@ -431,21 +487,30 @@
     ("branch", (2, 2, 2, 128, 1024), BF16),
     ("grad_keys", (1024, 256), F32),
     ("grad_values", (1024, 256), F32),
-    ("heads_part", (2, 2, 4, 2, 32, 768), BF16),
-    ("out_part", (4, 2, 32, 1024), BF16),
-    ("gains_part", (2, 4, 8, 128), F32),
-    ("heads_pair", (2, 4, 2, 32, 768), BF16),
-    ("hidden_pair", (2, 4, 2, 32, 2048), BF16),
-    ("down_pair", (4, 128, 1024), BF16),
-    ("out_pair", (4, 2, 32, 1024), BF16),
-    ("gains_pair", (4, 8, 128), F32),
-    ("heads_line", (3, 2, 2, 32, 768), BF16),
-    ("hidden_line", (3, 2, 2, 32, 2048), BF16),
-    ("down_line", (3, 128, 1024), BF16),
-    ("out_line", (3, 2, 32, 1024), BF16),
-    ("gains_line", (3, 8, 128), F32),
+    ("heads_part", (2, 2, 2, 2, 2, 32, 768), BF16),
+    ("out_part", (2, 2, 2, 32, 1024), BF16),
+    ("gains_part", (2, 2, 2, 8, 128), F32),
+    ("heads_b", (2, 2, 2, 2, 32, 768), BF16),
+    ("heads_a", (2, 2, 2, 32, 768), BF16),
+    ("heads_z", (2, 2, 32, 768), BF16),
+    ("gate_b", (2, 2, 2, 2, 32, 1024), BF16),
+    ("gate_a", (2, 2, 2, 32, 1024), BF16),
+    ("gate_z", (2, 2, 32, 1024), BF16),
+    ("up_b", (2, 2, 2, 2, 32, 1024), BF16),
+    ("up_a", (2, 2, 2, 32, 1024), BF16),
+    ("up_z", (2, 2, 32, 1024), BF16),
+    ("down_b", (2, 2, 128, 1024), BF16),
+    ("down_a", (2, 128, 1024), BF16),
+    ("down_z", (128, 1024), BF16),
+    ("out_b", (2, 2, 2, 32, 1024), BF16),
+    ("out_a", (2, 2, 32, 1024), BF16),
+    ("out_z", (2, 32, 1024), BF16),
+    ("gains_b", (2, 2, 8, 128), F32),
+    ("gains_a", (2, 8, 128), F32),
+    ("gains_z", (8, 128), F32),
     ("heads_dealt", (4, 32, 768), BF16),
-    ("hidden_dealt", (4, 32, 2048), BF16),
+    ("gate_dealt", (4, 32, 1024), BF16),
+    ("up_dealt", (4, 32, 1024), BF16),
     ("gains_deal", (8, 128), F32),
     ("gains_dealt", (4, 8, 128), F32),
     ("out_deal", (32, 1024), BF16),
@@ -463,9 +528,9 @@
     send, recv, local = scratch[-3:]
     m = type("Memory", (), dict(zip([name for name, _, _ in SCRATCH], scratch)))
     w = Wires(send, recv)
-    x, y, z, k = w.x, w.y, w.z, w.k
-    rank = 2 * x + k
-    w.greet(w.group_peers() + w.line_peers() + w.cross_peers() + [w.pair_peer()])
+    x, y, zh, zb, zl, k = w.x, w.y, w.zh, w.zb, w.zl, w.k
+    rank = 2 * zl + k
+    w.greet()
 
     used = [0]
 
@@ -479,66 +544,90 @@
         return copy
 
     def sequence_block(ref):
-        return lambda x, z: ref.at[z // 2, z % 2, x]
+        return lambda zh, zb, x: ref.at[zh, zb, x]
+
+    def deal_rows(packed, whole):
+        return Deal(
+            w,
+            lambda zl, k: packed.at[2 * zl + k],
+            lambda szl, sk: whole.at[y, sk, zh, (szl + zh) % 2, x],
+        )
+
+    def group_rows(ref):
+        return lambda x, y, zh: ref.at[y, :, zh, :, x]
+
+    def own_rows(ref):
+        return lambda x, y, zh: ref.at[y, k, zh, (zl + zh) % 2, x]
 
     visit_rows = Visit(w, rows, sequence_block(m.rows_all), spare())
     visit_rows.start()
     pack_rows(head_columns, (wq, wk, wv), m.heads_pack)
-    deal_heads = Deal(
-        w, lambda x, k: m.heads_pack.at[2 * x + k], lambda sx, sk: m.heads_all.at[y, sk, z, sx]
-    )
+    deal_heads = deal_rows(m.heads_pack, m.heads_all)
     deal_heads.start()
     stays = [
-        stay(m.heads_pack.at[rank], m.heads_all.at[y, k, z, x]),
-        stay(wo, m.out_all.at[y, k, z, x]),
-        stay(gains, m.gains_all.at[y, k, z, x]),
-        stay(wd, m.down_all.at[y, z]),
+        stay(m.heads_pack.at[rank], m.heads_all.at[y, k, zh, zb, x]),
+        stay(wo, m.out_all.at[y, k, zh, zb, x]),
+        stay(gains, m.gains_all.at[y, k, zh, zb, x]),
+        stay(wd, m.down_all.at[y, zh, x]),
         stay(ids, m.ids_all.at[k]),
     ]
-    swap = w.copy(ids, m.ids_all.at[k], w.at(x, y, z, 1 - k), w.slots(1))
+    swap = w.copy(ids, m.ids_all.at[k], w.core(), w.slots(1))
     swap.start()
-    spread_gains = Spread(w, lambda y, z: m.gains_all.at[y, k, z, x], gains)
+    spread_gains = Spread(w, "xy", own_rows(m.gains_all), gains)
     spread_gains.start()
-    pack_rows(hidden_columns, (wg, wu), m.hidden_pack)
-    stays.append(stay(m.hidden_pack.at[rank], m.hidden_all.at[y, k, z, x]))
-    deal_hidden = Deal(
-        w, lambda x, k: m.hidden_pack.at[2 * x + k], lambda sx, sk: m.hidden_all.at[y, sk, z, sx]
-    )
+    pack_rows(hidden_columns, (wg,), m.gate_pack)
+    pack_rows(hidden_columns, (wu,), m.up_pack)
+    stays.append(stay(m.gate_pack.at[rank], m.gate_all.at[y, k, zh, zb, x]))
+    stays.append(stay(m.up_pack.at[rank], m.up_all.at[y, k, zh, zb, x]))
+    deal_gate = deal_rows(m.gate_pack, m.gate_all)
+    deal_up = deal_rows(m.up_pack, m.up_all)
     for copy in stays:
         copy.wait()
     deal_heads.arrive()
-    spread_heads = Spread(w, lambda y, z: m.heads_all.at[y, :, z])
+    spread_heads = Spread(w, "yx", group_rows(m.heads_all))
     spread_heads.start()
+    spread_out = Spread(w, "yx", own_rows(m.out_all), wo)
+    spread_out.start()
     visit_rows.arrive()
-    share_rows = Share(w, lambda x, k: m.rows_all.at[:, k, x])
+    share_rows = Share(w, lambda zl, k: m.rows_all.at[:, k, zl])
     share_rows.start()
-    deal_hidden.start()
-    for i in (1, 3, 2):
-        spread_gains.forward(i)
-    spread_out = Spread(w, lambda y, z: m.out_all.at[y, k, z, x], wo)
-    spread_out.start()
+    deal_gate.start()
+    deal_up.start()
+    spread_gains.got_first()
+    spread_gains.got_z()
+    spread_gains.got_last()
+    spread_heads.got_first()
+    spread_heads.got_z()
     share_rows.forward()
-    deal_hidden.arrive()
-    spread_hidden = Spread(w, lambda y, z: m.hidden_all.at[y, :, z])
-    spread_hidden.start()
-    for i in (1, 3, 2):
-        spread_heads.forward(i)
-    for i in range(4):
-        spread_gains.arrive(i)
-    share_gains = Share(w, lambda x, k: m.gains_all.at[:, k, :, x])
-    share_gains.start()
+    deal_gate.arrive()
+    spread_gate = Spread(w, "xy", group_rows(m.gate_all))
+    spread_gate.start()
+    deal_up.arrive()
+    spread_up = Spread(w, "yx", group_rows(m.up_all))
+    spread_up.start()
+    spread_down = Spread(w, "xy", lambda x, y, zh: m.down_all.at[y, zh, x], wd)
+    spread_down.start()
+    spread_heads.got_last()
+    spread_gains.arrive()
+    share_gains = [
+        Share(w, lambda zl, k: m.gains_all.at[:, k, 0, zl]),
+        Share(w, lambda zl, k: m.gains_all.at[:, k, 1, 1 - zl]),
+    ]
+    for share in share_gains:
+        share.start()
     swap.wait()
-    m.ids_row[...] = m.ids_all[z // 2, z % 2].astype(F32)
+    m.ids_row[...] = m.ids_all[zh, x].astype(F32)
     for j in range(8):
         piece = slice(128 * j, 128 * j + 128)
         m.ids_col[piece, :] = jnp.broadcast_to(m.ids_row[:, piece], (128, 128)).T
-    share_gains.forward()
+    for share in share_gains:
+        share.forward()
     share_rows.arrive()
-    share_gains.arrive()
+    for share in share_gains:
+        share.arrive()
     for j in range(8):
         four = [
-            m.gains_all[j // 4, (j // 2) % 2, 2 * (j % 2) + i // 2, i % 2].astype(F32)
-            for i in range(4)
+            m.gains_all[j // 4, (j // 2) % 2, j % 2, i // 2, i % 2].astype(F32) for i in range(4)
         ]
         total = four[0] + four[1] + four[2] + four[3]
         for i in range(2):
@@ -551,12 +640,14 @@
         return 0
 
     lax.fori_loop(0, 4, first_norm, 0)
+    spread_out.got_first()
+    spread_out.got_z()
     visit_cots = Visit(w, cots, sequence_block(m.cots_all), spare())
     visit_cots.start()
-    for i in (1, 3, 2):
-        spread_out.forward(i)
-    for i in range(4):
-        spread_heads.arrive(i)
+    spread_gate.got_first()
+    spread_up.got_first()
+    spread_down.got_first()
+    spread_heads.arrive()
     heads = m.heads_all[...].reshape(1024, 768)
     for b in range(4):
         span = slice(256 * b, 256 * b + 256)
@@ -565,15 +656,7 @@
         m.values[span, :] = made[:, 512:]
         m.keys_turned[:, span] = made[:, 256:512].T
         m.values_turned[:, span] = made[:, 512:].T
-    for i in range(4):
-        spread_out.arrive(i)
-    share_out = Share(w, lambda x, k: m.out_all.at[:, k, :, x])
-    share_out.start()
-    spread_down = Spread(w, lambda y, z: m.down_all.at[y, z], wd)
-    spread_down.start()
-    visit_cots.arrive()
-    share_cots = Share(w, lambda x, k: m.cots_all.at[:, k, x])
-    share_cots.start()
+    spread_out.got_last()
 
     def bias_of(b):
         start, count = 256 * b, 256 * b + 256
@@ -586,8 +669,8 @@
     def head_rows(h):
         return pl.ds(pl.multiple_of(h * HEAD, HEAD), HEAD)
 
-    def rank_columns(x, k):
-        return pl.ds(pl.multiple_of(256 * (2 * x + k), 256), 256)
+    def rank_columns(zl, k):
+        return pl.ds(pl.multiple_of(256 * (2 * zl + k), 256), 256)
 
     def mix(b):
         span, count = slice(256 * b, 256 * b + 256), 256 * b + 256
@@ -606,34 +689,51 @@
             return 0
 
         lax.fori_loop(0, 4, one, 0)
-        m.mixed_all[b // 2, b % 2, :, rank_columns(x, k)] = m.mixed_turned[:, span].T
+        m.mixed_all[b // 2, b % 2, :, rank_columns(zl, k)] = m.mixed_turned[:, span].T
 
     def share_mixed(b):
-        return Share(w, lambda x, k: m.mixed_all.at[b // 2, b % 2, :, rank_columns(x, k)])
+        return Share(w, lambda zl, k: m.mixed_all.at[b // 2, b % 2, :, rank_columns(zl, k)])
 
     shares = [share_mixed(b) for b in range(4)]
     mix(0)
     shares[0].start()
-    spread_hidden.forward(1)
+    visit_cots.arrive()
+    share_cots = Share(w, lambda zl, k: m.cots_all.at[:, k, zl])
+    share_cots.start()
+    spread_gate.got_z()
     mix(1)
     shares[1].start()
     shares[0].forward()
-    share_out.forward()
-    share_cots.forward()
-    spread_hidden.forward(3)
+    spread_out.arrive()
+    share_out = [
+        Share(w, lambda zl, k: m.out_all.at[:, k, 0, zl]),
+        Share(w, lambda zl, k: m.out_all.at[:, k, 1, 1 - zl]),
+    ]
+    for share in share_out:
+        share.start()
+    spread_up.got_z()
     mix(2)
     shares[2].start()
     shares[1].forward()
-    spread_hidden.forward(2)
+    spread_down.got_z()
+    for share in share_out:
+        share.forward()
+    share_cots.forward()
     mix(3)
     shares[3].start()
     shares[2].forward()
-    share_out.arrive()
+    spread_gate.got_last()
+    for share in share_out:
+        share.arrive()
 
     for b in range(4):
         span = slice(256 * b, 256 * b + 256)
         if b == 2:
             shares[3].forward()
+        if b == 1:
+            spread_up.got_last()
+        if b == 3:
+            spread_down.got_last()
         shares[b].arrive()
         middle = m.rows_all[b // 2, b % 2].reshape(256, 1024).astype(F32)
         whole = m.out_all[...].reshape(1024, 1024)
@@ -644,12 +744,8 @@
         def _():
             m.middle_keep[b // 2] = middle
 
-    for i in (1, 3, 2):
-        spread_down.forward(i)
-    for i in range(4):
-        spread_hidden.arrive(i)
-    for i in range(4):
-        spread_down.arrive(i)
+    for spread in (spread_gate, spread_up, spread_down):
+        spread.arrive()
     share_cots.arrive()
     for share in shares:
         share.drain()
@@ -662,9 +758,9 @@
         normed_two = m.normed_two[span, :]
         for n in range(4):
             columns = slice(256 * n, 256 * n + 256)
-            gate_tile = m.hidden_all[..., 256 * n : 256 * n + 256].reshape(1024, 256)
-            up_tile = m.hidden_all[..., 1024 + 256 * n : 1280 + 256 * n].reshape(1024, 256)
-            down_tile = m.down_all[n // 2, 2 * (n % 2) : 2 * (n % 2) + 2].reshape(256, 1024)
+            gate_tile = m.gate_all[..., columns].reshape(1024, 256)
+            up_tile = m.up_all[..., columns].reshape(1024, 256)
+            down_tile = m.down_all[n // 2, n % 2].reshape(256, 1024)
             gate = dots(normed_two, gate_tile, NN)
             upward = dots(normed_two, up_tile, NN)
             grad_hidden = dots(upstream, down_tile, NT)
@@ -675,9 +771,8 @@
             m.grad_gate[span, columns] = (
                 grad_hidden * upward * (sigma + silu * (1.0 - sigma))
             ).astype(BF16)
-        norm_part = dots(
-            m.grad_gate[span, :], m.hidden_all[..., :1024].reshape(1024, 1024), NT
-        ) + dots(m.grad_up[span, :], m.hidden_all[..., 1024:].reshape(1024, 1024), NT)
+        norm_part = dots(m.grad_gate[span, :], m.gate_all[...].reshape(1024, 1024), NT)
+        norm_part = norm_part + dots(m.grad_up[span, :], m.up_all[...].reshape(1024, 1024), NT)
         return span, norm_part
 
     def out_of(span):
@@ -697,8 +792,8 @@
 
     lax.fori_loop(0, 2, give, 0)
     lax.fori_loop(0, 2, keep, 0)
-    spread_down.drain()
-    spread_hidden.drain()
+    for spread in (spread_gate, spread_up, spread_down):
+        spread.drain()
 
     def lanes(plane, half):
         return pl.ds(pl.multiple_of(512 * plane + 256 * half, 256), 256)
@@ -706,44 +801,52 @@
     def down_part(plane):
         def one(half, _):
             made = dots(m.hidden[:, lanes(plane, half)], m.cots_all[...].reshape(1024, 1024), TN)
-            m.down_all[plane, pl.ds(2 * half, 2)] = made.astype(BF16).reshape(2, 128, 1024)
+            m.down_all[plane, half] = made.astype(BF16).reshape(2, 128, 1024)
             return 0
 
         lax.fori_loop(0, 2, one, 0)
 
-    def hidden_part(plane):
+    def wide_part(whole, right, plane):
         def one(half, _):
-            left = m.normed_two[:, lanes(plane, half)]
-            for j, right in enumerate((m.grad_gate, m.grad_up)):
-                made = dots(left, right[...], TN).astype(BF16).reshape(4, 2, 32, 1024)
-                m.hidden_all[plane, half, :, :, :, 1024 * j : 1024 * j + 1024] = made
+            made = dots(m.normed_two[:, lanes(plane, half)], right[...], TN).astype(BF16)
+            whole[plane, half] = made.reshape(2, 2, 2, 32, 1024)
             return 0
 
         lax.fori_loop(0, 2, one, 0)
 
-    fold_down = Fold(
-        w, lambda y: m.down_all.at[y], lambda y, z: m.down_all.at[y, z],
-        m.down_pair, lambda z: m.down_pair.at[z], m.down_line,
-    )
-    fold_hidden = Fold(
-        w, lambda y: m.hidden_all.at[y], lambda y, z: m.hidden_all.at[y, :, z],
-        m.hidden_pair, lambda z: m.hidden_pair.at[:, z], m.hidden_line,
-    )
-    fold_heads = Fold(
-        w, lambda y: m.heads_part.at[y], lambda y, z: m.heads_part.at[y, :, z],
-        m.heads_pair, lambda z: m.heads_pair.at[:, z], m.heads_line,
-    )
-    fold_gains = Fold(
-        w, lambda y: m.gains_part.at[y], lambda y, z: m.gains_part.at[y, z],
-        m.gains_pair, lambda z: m.gains_pair.at[z], m.gains_line,
-    )
+    def fold_plane(whole, got_b, got_a, got_z):
+        return Fold(
+            w, "xy", lambda y: whole.at[y], lambda x, y, zh: whole.at[y, :, zh, :, x],
+            got_b, lambda x, zh: got_b.at[:, zh, :, x], got_a, got_z,
+        )
+
+    def fold_side(whole, got_b, got_a, got_z):
+        return Fold(
+            w, "yx", lambda x: whole.at[:, :, :, :, x], lambda x, y, zh: whole.at[y, :, zh, :, x],
+            got_b, lambda y, zh: got_b.at[y, :, zh], got_a, got_z,
+        )
+
+    def fold_block(whole, got_b, got_a, got_z):
+        return Fold(
+            w, "xy", lambda y: whole.at[y], lambda x, y, zh: whole.at[y, zh, x],
+            got_b, lambda x, zh: got_b.at[zh, x], got_a, got_z,
+        )
+
+    fold_down = fold_block(m.down_all, m.down_b, m.down_a, m.down_z)
+    fold_gate = fold_plane(m.gate_all, m.gate_b, m.gate_a, m.gate_z)
+    fold_up = fold_side(m.up_all, m.up_b, m.up_a, m.up_z)
+    fold_heads = fold_side(m.heads_part, m.heads_b, m.heads_a, m.heads_z)
+    fold_gains = fold_block(m.gains_part, m.gains_b, m.gains_a, m.gains_z)
     down_part(1 - y)
     fold_down.start()
-    hidden_part(1 - y)
-    fold_hidden.start()
-
-    share_branch = Share(w, lambda x, k: m.branch.at[:, k, x])
-    own_half = total_norm.rows(x)
+    wide_part(m.up_all, m.grad_up, 0)
+    wide_part(m.up_all, m.grad_up, 1)
+    fold_up.start()
+    wide_part(m.gate_all, m.grad_gate, 1 - y)
+    fold_gate.start()
+
+    share_branch = Share(w, lambda zl, k: m.branch.at[:, k, zl])
+    own_half = total_norm.rows(zl)
     gain_sum = jnp.zeros((1, 1024), F32)
     for i in range(2):
         grad, term = norm_back(
@@ -751,32 +854,31 @@
         )
         gain_sum = gain_sum + term
         m.done_out[i] = (m.middle_keep[i, own_half] + total_out.take(i)).astype(BF16)
-        grad = grad + m.cots_all[i, k, x].astype(F32)
+        grad = grad + m.cots_all[i, k, zl].astype(F32)
         m.middle_keep[i, own_half] = grad
-        m.branch[i, k, x] = grad.astype(BF16)
+        m.branch[i, k, zl] = grad.astype(BF16)
     share_branch.start()
     return_out = Return(w, lambda i: m.done_out.at[i], output, spare())
     return_out.start()
 
     def gain_rows_part(row, total):
         for plane in range(2):
-            for zz in range(4):
+            for place in range(4):
                 for half in range(2):
-                    at = 512 * plane + 256 * half + 128 * (zz // 2)
-                    m.gains_part[plane, zz, 2 * row + half : 2 * row + half + 1, :] = total[
-                        :, at : at + 128
-                    ]
+                    at = 512 * plane + 256 * half + 128 * (place // 2)
+                    row_at = slice(2 * row + half, 2 * row + half + 1)
+                    m.gains_part[plane, place // 2, place % 2, row_at, :] = total[:, at : at + 128]
 
     m.gains_part[...] = jnp.zeros_like(m.gains_part)
     gain_rows_part(1, gain_sum)
     down_part(y)
     share_branch.forward()
-    hidden_part(y)
+    wide_part(m.gate_all, m.grad_gate, y)
     share_branch.arrive()
 
     grad_mixed, grad_mixed_turned = m.grad_up.at[:, :256], m.hidden.at[:256]
     grad_heads = m.grad_gate.at[:, :768]
-    out_own = m.out_all[x, k].reshape(256, 1024)
+    out_own = m.out_all[zl, k].reshape(256, 1024)
     for b in range(4):
         span = slice(256 * b, 256 * b + 256)
         made = dots(m.branch[b // 2, b % 2].reshape(256, 1024), out_own, NT).astype(BF16)
@@ -785,11 +887,11 @@
     m.out_part[...] = (
         dots(m.mixed_turned[...], m.branch[...].reshape(1024, 1024), NN)
         .astype(BF16)
-        .reshape(4, 2, 32, 1024)
+        .reshape(2, 2, 2, 32, 1024)
     )
     base = w.slots(6)
-    owner = y == x
-    out_across = w.copy(m.out_part, m.out_pair, w.pair_peer(), base)
+    owner = y == zl
+    out_across = w.copy(m.out_part, m.out_b, w.at(y=1 - y), base)
     pl.when(jnp.logical_not(owner))(lambda: out_across.start())
     m.grad_keys[...] = jnp.zeros_like(m.grad_keys)
     m.grad_values[...] = jnp.zeros_like(m.grad_values)
@@ -820,17 +922,19 @@
         lax.fori_loop(0, 4, one, 0)
         grad_heads[span, :256] = grad_mixed_turned[:, span].T
 
-    for b in range(4):
-        unmix(b)
+    unmix(0)
+    unmix(1)
+    fold_up.second()
+    unmix(2)
+    fold_down.second()
+    unmix(3)
     grad_heads[:, 256:512] = (m.grad_keys[...] * HEAD**-0.5).astype(BF16)
     grad_heads[:, 512:] = m.grad_values[...].astype(BF16)
 
-    def heads_part(plane):
+    for plane in range(2):
         for half in range(2):
             made = dots(m.normed[:, lanes(plane, half)], grad_heads[...], TN)
-            m.heads_part[plane, half] = made.astype(BF16).reshape(4, 2, 32, 768)
-
-    heads_part(1 - y)
+            m.heads_part[plane, half] = made.astype(BF16).reshape(2, 2, 2, 32, 768)
     fold_heads.start()
     total_norm.drain()
     total_first = Total(w, m.part_norm, m.core_norm, m.across_norm)
@@ -843,8 +947,8 @@
         total_first.give(i, first_part(i, 1 - k))
     for i in range(2):
         total_first.keep(i, first_part(i, k))
-    heads_part(y)
-    fold_down.send()
+    fold_up.third()
+    fold_down.third()
     gain_sum = jnp.zeros((1, 1024), F32)
 
     def done_in(i):
@@ -852,7 +956,7 @@
 
     for i in range(2):
         grad, term = norm_back(
-            m.rows_all[i, k, x].astype(F32), m.gain_rows[0], total_first.take(i)
+            m.rows_all[i, k, zl].astype(F32), m.gain_rows[0], total_first.take(i)
         )
         gain_sum = gain_sum + term
         done_in(i)[...] = (m.middle_keep[i, own_half] + grad).astype(BF16)
@@ -861,61 +965,95 @@
     gain_rows_part(0, gain_sum)
     fold_gains.start()
 
-    def out_piece(i):
-        zi = (z + i) % 4
-        return w.copy(m.out_part.at[zi], m.out_line.at[i - 1], w.at(x, y, zi, k), base + i)
+    fold_gate.second()
+
+    def out_side(z):
+        side = 1 - zh if z else zh
+        return w.copy(
+            m.out_part.at[side, :, 1 - x], m.out_a.at[side], w.at(x=1 - x), base + 1 + z
+        )
+
+    def out_side_landed(z):
+        ref = m.out_a.at[1 - zh if z else zh]
+        return w.copy(ref, ref, w.at(x=1 - x), base + 1 + z)
+
+    def out_two(side, x):
+        return m.out_part[side, :, x].astype(F32) + m.out_b[side, :, x].astype(F32)
+
+    out_half = w.copy(m.out_part.at[1 - zh, :, x], m.out_z, w.at(zh=1 - zh), base + 3)
+    out_last = w.copy(m.out_deal, m.out_home, w.across(), base + 4)
 
     @pl.when(owner)
     def _():
         out_across.wait_recv()
-        for i in (2, 1, 3):
-            zi = (z + i) % 4
-            m.out_part[zi] = (m.out_part[zi].astype(F32) + m.out_pair[zi].astype(F32)).astype(BF16)
-            out_piece(i).start()
-
-    fold_hidden.send()
+        for side in (1, 0):
+            at = 1 - zh if side else zh
+            m.out_part[at, :, 1 - x] = out_two(at, 1 - x).astype(BF16)
+            out_side(side).start()
+
+    fold_heads.second()
+    fold_gains.second()
+    fold_gate.third()
+
+    @pl.when(owner)
+    def _():
+        out_side_landed(1).wait_recv()
+        m.out_part[1 - zh, :, x] = (
+            out_two(1 - zh, x) + m.out_a[1 - zh].astype(F32)
+        ).astype(BF16)
+        out_half.start()
+
     d_out[...] = fold_down.finish()
-    fold_gains.send()
-    fold_heads.send()
+
+    def deal_grads(packed, dealt):
+        return Deal(
+            w, lambda zl, k: packed.at[2 * k + (zl + zh) % 2], lambda zl, k: dealt.at[2 * zl + k]
+        )
+
+    deal_up.drain()
+    deal_gate.drain()
+    deal_heads.drain()
+    m.up_pack[...] = fold_up.finish().astype(BF16).reshape(4, 32, 1024)
+    deal_up_grad = deal_grads(m.up_pack, m.up_dealt)
+    deal_up_grad.start()
+    fold_heads.third()
+    fold_gains.third()
+    m.gate_pack[...] = fold_gate.finish().astype(BF16).reshape(4, 32, 1024)
+    deal_gate_grad = deal_grads(m.gate_pack, m.gate_dealt)
+    deal_gate_grad.start()
+
+    @pl.when(owner)
+    def _():
+        out_side_landed(0).wait_recv()
+        out_half.wait_recv()
+        out_total = out_two(zh, x) + m.out_a[zh].astype(F32) + m.out_z[...].astype(F32)
+        first, second = out_total[0], out_total[1]
+        m.out_deal[...] = jnp.where(zb == 0, second, first).astype(BF16)
+        out_last.start()
+        o_out[...] = jnp.where(zb == 0, first, second)
+
     return_in.arrive()
     input_grad[...] = m.input_home[...].astype(F32)
-    out_last = w.copy(m.out_deal, m.out_home, w.at(1 - x, y, z, k), base + 4)
-
-    @pl.when(owner)
-    def _():
-        out_total = m.out_part[z].astype(F32) + m.out_pair[z].astype(F32)
-        for i in (1, 3, 2):
-            out_piece(i).wait_recv()
-            out_total += m.out_line[i - 1].astype(F32)
-        first, second = out_total[0], out_total[1]
-        m.out_deal[...] = jnp.where(x == 0, second, first).astype(BF16)
-        out_last.start()
-        o_out[...] = jnp.where(x == 0, first, second)
-
-    deal_hidden.drain()
-    deal_heads.drain()
-    m.hidden_pack[...] = fold_hidden.finish().astype(BF16).reshape(4, 32, 2048)
-    deal_hidden_grad = Deal(
-        w, lambda x, k: m.hidden_pack.at[2 * k + x], lambda x, k: m.hidden_dealt.at[2 * x + k]
-    )
-    deal_hidden_grad.start()
     m.gains_deal[...] = fold_gains.finish()
     m.gains_dealt[rank] = m.gains_deal[...]
-    deal_gains = Deal(w, lambda x, k: m.gains_deal, lambda x, k: m.gains_dealt.at[2 * x + k])
+    deal_gains = Deal(w, lambda zl, k: m.gains_deal, lambda zl, k: m.gains_dealt.at[2 * zl + k])
     deal_gains.start()
     m.heads_pack[...] = fold_heads.finish().astype(BF16).reshape(4, 32, 768)
-    deal_heads_grad = Deal(
-        w, lambda x, k: m.heads_pack.at[2 * k + x], lambda x, k: m.heads_dealt.at[2 * x + k]
-    )
+    deal_heads_grad = deal_grads(m.heads_pack, m.heads_dealt)
     deal_heads_grad.start()
-    m.hidden_dealt[rank] = m.hidden_pack[2 * k + x]
-    m.heads_dealt[rank] = m.heads_pack[2 * k + x]
-    deal_hidden_grad.arrive()
-    for r in range(4):
-        for half, target in enumerate((g_out, u_out)):
+    m.up_dealt[rank] = m.up_pack[2 * k + zb]
+    m.gate_dealt[rank] = m.gate_pack[2 * k + zb]
+    m.heads_dealt[rank] = m.heads_pack[2 * k + zb]
+    for deal, dealt, target in (
+        (deal_up_grad, m.up_dealt, u_out),
+        (deal_gate_grad, m.gate_dealt, g_out),
+    ):
+        deal.arrive()
+        for r in range(4):
             for j, (start, width) in enumerate(hidden_columns(r)):
-                at = 128 * j + half * 1024
-                target[:, start : start + width] = m.hidden_dealt[r, :, at : at + width].astype(F32)
+                target[:, start : start + width] = dealt[
+                    r, :, 128 * j : 128 * j + width
+                ].astype(F32)
     deal_gains.arrive()
     gain_out[...] = m.gains_dealt[0] + m.gains_dealt[1] + m.gains_dealt[2] + m.gains_dealt[3]
     deal_heads_grad.arrive()
@@ -931,17 +1069,18 @@
 
     return_out.arrive()
     for part in [
-        visit_rows, visit_cots, spread_gains, spread_heads, spread_out,
-        share_rows, share_cots, share_gains, share_out, share_branch, total_out, total_first,
-        fold_down, fold_hidden, fold_heads, fold_gains, return_out, return_in,
-        deal_hidden_grad, deal_heads_grad, deal_gains,
-    ]:
+        visit_rows, visit_cots, spread_gains, spread_heads, spread_out, share_rows, share_cots,
+        share_branch, total_out, total_first, fold_down, fold_gate, fold_up, fold_heads,
+        fold_gains, return_out, return_in, deal_up_grad, deal_gate_grad, deal_heads_grad,
+        deal_gains,
+    ] + share_gains + share_out:
         part.drain()
 
     @pl.when(owner)
     def _():
-        for i in (1, 2, 3):
-            out_piece(i).wait_send()
+        for side in range(2):
+            out_side(side).wait_send()
+        out_half.wait_send()
         out_last.wait_send()
 
     pl.when(jnp.logical_not(owner))(lambda: out_across.wait_send())
@@ -952,9 +1091,9 @@
     mlp_gain, gate_weight, up_weight, down_weight, out_grad,
 ):
     dp, ctx = lax.axis_index("dp"), lax.axis_index("ctx")
-    x, y, z, k = ctx % 2, dp // 2, ctx // 2, dp % 2
+    k = dp % 2
     piece = attn_gain.shape[0]
-    lane = piece * (2 * (z % 2) + x)
+    lane = piece * (ctx % 4)
     gains = jnp.zeros((16, 128), BF16)
     gains = lax.dynamic_update_slice(gains, jnp.stack([attn_gain, mlp_gain]), (0, lane))
     d, f = layer_input.shape[2], gate_weight.shape[1]
@@ -979,8 +1118,8 @@
         out_specs=(ANY,) + (VMEM,) * 9,
         scratch_shapes=rooms
         + [
-            pltpu.SemaphoreType.DMA((160,)),
-            pltpu.SemaphoreType.DMA((160,)),
+            pltpu.SemaphoreType.DMA((192,)),
+            pltpu.SemaphoreType.DMA((192,)),
             pltpu.SemaphoreType.DMA((16,)),
         ],
         compiler_params=pltpu.CompilerParams(

time: 353 us -> 298 us (0.84)
  the two profiles are of different devices: /device:TPU:19 before, /device:TPU:7 now
where the time goes in v3:
time: 298 us
  Pallas kernels  285 us (96%)
  local copies, waits for them, and re-layouts  12.2 us (4%)
    pallas_call x1, Pallas kernels, grouped(): pl.pallas_call(layer_body, name='layer', out_shape=outs, in_specs=[ANY, A...  285 us
    unnamed x33, local copies, waits for them, and re-layouts  9.69 us

profile of v3, /device:TPU:7, one launch (start us, length us, event | category | flops | bytes accessed | tf_op | source)
XLA Modules:
  0.0 298.0 jit_solution(139364124305257106)
XLA Ops:
  0.7 0.0 copy-start.10
  0.7 0.0 copy-start.11
  0.7 0.0 copy-start.9
  0.7 0.6 copy-done.10
  1.3 0.0 copy-done.11
  1.4 0.5 dynamic_update_slice.3.gains
  1.9 0.0 copy-done.9
  1.9 0.0 copy-start.8
  1.9 0.6 reshape.31.ids
  2.5 0.0 copy-done.8
  2.5 285.1 %layer.1 = (bf16[2,128,1024]{2,1,0:T(8,128)(2,1)}, f32[2,128,1024]{2,1,0:T(8,128)}, f32[32,1024]{1,0:T(8,128)}, f32[32,1024]{1,0:T(8,128)}, f32[32,1024]{1,0:T(8...) custom-call(bf16[2,128,1024]{2,1,0:T(8,128)(2,1)} %rows.1, ...), custom_call_target="tpu_custom_call" | custom-call | tf_op jit(solution)/shard_map/layer/pallas_call | solution.py:1113
  287.6 0.0 copy-start
  287.6 1.4 dynamic-slice_bitcast_fusion
  289.0 1.9 copy.33
  290.8 0.0 copy-done
  290.8 0.0 copy-start.7
  290.9 0.0 copy-start.6
  290.9 0.0 copy-start.5
  290.9 1.0 copy.34
  291.8 0.0 copy-done.7
  291.8 0.0 copy-start.3
  291.9 0.7 copy.35
  292.5 0.0 copy-done.6
  292.5 0.7 copy.36
  293.2 0.0 copy-done.5
  293.2 0.0 copy-start.4
  293.2 0.7 copy.37
  293.8 0.3 copy-done.4
  294.1 0.7 copy.38
  294.8 0.0 copy-done.3
  294.8 0.0 copy-start.2
  294.8 0.8 copy.39
  295.6 0.4 copy-done.2
  296.0 0.0 copy-start.1
  296.0 0.8 copy.40
  296.8 0.4 copy-done.1
  297.2 0.8 copy.41
  (2 shorter events, 0.0 us)
Async XLA Ops:
  0.7 0.7 copy-start.10
  0.7 0.7 copy-start.11
  0.7 1.2 copy-start.9
  1.9 0.6 copy-start.8
  287.6 3.3 %copy-start = (f32[2,128,1024]{2,1,0:T(8,128)S(1)}, f32[2,128,1024]{2,1,0:T(8,128)}, u32[]{:S(2)}) copy-start(f32[2,128,1024]{2,1,0:T(8,128)} %get-tuple-element.45) | copy-start | bytes 3145732
  290.8 1.0 copy-start.7
  290.9 1.7 copy-start.6
  290.9 2.3 copy-start.5
  291.8 2.9 copy-start.3
  293.2 1.0 copy-start.4
  294.8 1.2 copy-start.2
  296.0 1.2 copy-start.1

commit v4 on v3

--- a/solution.py
+++ b/solution.py
@@ -24,7 +24,7 @@
         dp, ctx = lax.axis_index("dp"), lax.axis_index("ctx")
         self.x, self.y = ctx % 2, dp // 2
         self.zh, self.zb = ctx // 4, (ctx // 2) % 2
-        self.zl, self.k = (self.zb + self.zh) % 2, dp % 2
+        self.v, self.k = (self.zb + self.zh) % 2, dp % 2
         self.send, self.recv = send, recv
         self.used = 0
 
@@ -33,16 +33,16 @@
         self.used += count
         return first
 
-    def at(self, x=None, y=None, zh=None, zl=None, k=None):
-        x = self.x if x is None else x
+    def at(self, v=None, y=None, zh=None, x=None, k=None):
+        v = self.v if v is None else v
         y = self.y if y is None else y
         zh = self.zh if zh is None else zh
-        zl = self.zl if zl is None else zl
+        x = self.x if x is None else x
         k = self.k if k is None else k
-        return (2 * y + k, 4 * zh + 2 * ((zl + zh) % 2) + x)
+        return (2 * y + k, 4 * zh + 2 * ((v + zh) % 2) + x)
 
     def across(self):
-        return self.at(zl=1 - self.zl)
+        return self.at(x=1 - self.x)
 
     def core(self):
         return self.at(k=1 - self.k)
@@ -58,144 +58,26 @@
         )
 
     def greet(self):
+        v, zh, zb, k = self.v, self.zh, self.zb, self.k
         barrier = pltpu.get_barrier_semaphore()
-        peers = [self.at(y=1 - self.y)]
-        for n in range(1, 16):
-            bits = [(n >> i) % 2 for i in range(4)]
-            x, zh, zl, k = [
-                1 - own if bit else own
-                for own, bit in zip((self.x, self.zh, self.zl, self.k), bits)
-            ]
-            peers.append(self.at(x=x, zh=zh, zl=zl, k=k))
-        for peer in peers:
+
+        def call(peer):
             pl.semaphore_signal(barrier, inc=1, device_id=peer, device_id_type=MESH)
-        pl.semaphore_wait(barrier, len(peers))
-
-
-class Pairs:
-    def __init__(self, wires, order):
-        self.w, self.order = wires, order
-
-    def place(self, z, a, b):
-        w = self.w
-        x, y = (a, b) if self.order == "xy" else (b, a)
-        flip = lambda own, turn: 1 - own if turn else own
-        return flip(w.x, x), flip(w.y, y), flip(w.zh, z)
-
-    def partner(self, z, a, b):
-        x, y, zh = self.place(z, a, b)
-        return self.w.at(x=x, y=y, zh=zh)
-
-
-class Spread(Pairs):
-    SENDS = ((0, 0, 0), (0, 0, 0), (1, 0, 0), (0, 0, 0), (1, 0, 0), (0, 1, 0), (1, 1, 0))
-    STEPS = ((1, 0, 0), (0, 1, 0), (0, 1, 0), (0, 0, 1), (0, 0, 1), (0, 0, 1), (0, 0, 1))
-
-    def __init__(self, wires, order, block, own=None):
-        super().__init__(wires, order)
-        self.block, self.own = block, own
-        self.first = wires.slots(7)
-
-    def piece(self, n):
-        ref = self.block(*self.place(*self.SENDS[n]))
-        source = self.own if self.own is not None and not any(self.SENDS[n]) else ref
-        return self.w.copy(source, ref, self.partner(*self.STEPS[n]), self.first + n)
-
-    def landed(self, n):
-        came = [i ^ j for i, j in zip(self.SENDS[n], self.STEPS[n])]
-        ref = self.block(*self.place(*came))
-        return self.w.copy(ref, ref, self.partner(*self.STEPS[n]), self.first + n)
-
-    def start(self):
-        for n in (0, 1, 3):
-            self.piece(n).start()
-
-    def got_first(self):
-        self.landed(1).wait_recv()
-        self.piece(5).start()
-
-    def got_z(self):
-        self.landed(0).wait_recv()
-        self.piece(2).start()
-        self.piece(4).start()
-
-    def got_last(self):
-        self.landed(2).wait_recv()
-        self.piece(6).start()
-
-    def arrive(self):
-        for n in (3, 4, 5, 6):
-            self.landed(n).wait_recv()
-
-    def drain(self):
-        for n in range(7):
-            self.piece(n).wait_send()
-
-
-class Share:
-    def __init__(self, wires, block):
-        self.w, self.block = wires, block
-        self.first = wires.slots(3)
-
-    def piece(self, i):
-        w = self.w
-        ref = self.block(w.zl if i < 2 else 1 - w.zl, w.k)
-        return w.copy(ref, ref, w.across() if i == 0 else w.core(), self.first + i)
-
-    def landed(self, i):
-        w = self.w
-        ref = self.block(*[(1 - w.zl, w.k), (w.zl, 1 - w.k), (1 - w.zl, 1 - w.k)][i])
-        return w.copy(ref, ref, w.core(), self.first + i)
-
-    def start(self):
-        self.piece(0).start()
-        self.piece(1).start()
-
-    def forward(self):
-        self.landed(0).wait_recv()
-        self.piece(2).start()
-
-    def arrive(self):
-        self.landed(1).wait_recv()
-        self.landed(2).wait_recv()
-
-    def drain(self):
-        for i in range(3):
-            self.piece(i).wait_send()
-
-
-class Deal:
-    def __init__(self, wires, outgoing, incoming):
-        self.w, self.outgoing, self.incoming = wires, outgoing, incoming
-        self.first = wires.slots(3)
-
-    def mate(self, i):
-        w = self.w
-        return [(1 - w.zl, w.k), (w.zl, 1 - w.k), (1 - w.zl, 1 - w.k)][i]
-
-    def piece(self, i):
-        w = self.w
-        zl, k = self.mate(i)
-        return w.copy(
-            self.outgoing(zl, k), self.incoming(w.zl, w.k), w.at(zl=zl, k=k), self.first + i
-        )
-
-    def landed(self, i):
-        zl, k = self.mate(i)
-        ref = self.incoming(zl, k)
-        return self.w.copy(ref, ref, self.w.at(zl=zl, k=k), self.first + i)
-
-    def start(self):
-        for i in range(3):
-            self.piece(i).start()
-
-    def arrive(self):
-        for i in range(3):
-            self.landed(i).wait_recv()
-
-    def drain(self):
-        for i in range(3):
-            self.piece(i).wait_send()
+
+        for peer in (
+            self.across(), self.core(), self.at(x=1 - self.x, k=1 - k),
+            self.at(v=1 - v), self.at(y=1 - self.y), self.at(zh=1 - zh),
+        ):
+            call(peer)
+        count = 6
+        for n in range(2):
+            away = jnp.logical_not(every(v == n, zh == k, zb == k))
+            pl.when(away)(lambda: call(self.at(v=n, zh=k, k=zb)))
+            count = count + jnp.where(away, 1, 0)
+            away = jnp.logical_not(every(zh == n, zb == k, zh == k))
+            pl.when(away)(lambda: call(self.at(zh=n, v=(k + n) % 2, k=zh)))
+            count = count + jnp.where(away, 1, 0)
+        pl.semaphore_wait(barrier, count)
 
 
 def every(*tests):
@@ -205,20 +87,153 @@
     return all_of
 
 
+class Pairs:
+    def __init__(self, wires, order):
+        self.w, self.order = wires, order
+
+    def place(self, z, a, b):
+        w = self.w
+        v, y = (a, b) if self.order == "vy" else (b, a)
+        flip = lambda own, turn: 1 - own if turn else own
+        return flip(w.v, v), flip(w.y, y), flip(w.zh, z)
+
+    def partner(self, z, a, b):
+        v, y, zh = self.place(z, a, b)
+        return self.w.at(v=v, y=y, zh=zh)
+
+
+class Spread(Pairs):
+    SENDS = ((0, 0, 0), (0, 0, 0), (1, 0, 0), (0, 0, 0), (1, 0, 0), (0, 1, 0), (1, 1, 0))
+    STEPS = ((1, 0, 0), (0, 1, 0), (0, 1, 0), (0, 0, 1), (0, 0, 1), (0, 0, 1), (0, 0, 1))
+
+    def __init__(self, wires, order, block, own=None):
+        super().__init__(wires, order)
+        self.block, self.own = block, own
+        self.first = wires.slots(7)
+
+    def piece(self, n):
+        ref = self.block(*self.place(*self.SENDS[n]))
+        source = self.own if self.own is not None and not any(self.SENDS[n]) else ref
+        return self.w.copy(source, ref, self.partner(*self.STEPS[n]), self.first + n)
+
+    def landed(self, n):
+        came = [i ^ j for i, j in zip(self.SENDS[n], self.STEPS[n])]
+        ref = self.block(*self.place(*came))
+        return self.w.copy(ref, ref, self.partner(*self.STEPS[n]), self.first + n)
+
+    def start(self):
+        self.start_z()
+        self.start_rest()
+
+    def start_z(self):
+        self.piece(0).start()
+
+    def start_rest(self):
+        self.piece(1).start()
+        self.piece(3).start()
+
+    def got_first(self):
+        self.landed(1).wait_recv()
+        self.piece(5).start()
+
+    def got_z(self):
+        self.landed(0).wait_recv()
+        self.piece(2).start()
+        self.piece(4).start()
+
+    def got_last(self):
+        self.landed(2).wait_recv()
+        self.piece(6).start()
+
+    def arrive(self):
+        for n in (3, 4, 5, 6):
+            self.landed(n).wait_recv()
+
+    def drain(self):
+        for n in range(7):
+            self.piece(n).wait_send()
+
+
+class Share:
+    def __init__(self, wires, block):
+        self.w, self.block = wires, block
+        self.first = wires.slots(3)
+
+    def piece(self, i):
+        w = self.w
+        ref = self.block(w.x if i < 2 else 1 - w.x, w.k)
+        return w.copy(ref, ref, w.across() if i == 0 else w.core(), self.first + i)
+
+    def landed(self, i):
+        w = self.w
+        ref = self.block(*[(1 - w.x, w.k), (w.x, 1 - w.k), (1 - w.x, 1 - w.k)][i])
+        return w.copy(ref, ref, w.core(), self.first + i)
+
+    def start(self):
+        self.piece(0).start()
+        self.piece(1).start()
+
+    def forward(self):
+        self.landed(0).wait_recv()
+        self.piece(2).start()
+
+    def arrive(self):
+        self.landed(1).wait_recv()
+        self.landed(2).wait_recv()
+
+    def drain(self):
+        for i in range(3):
+            self.piece(i).wait_send()
+
+
+class Deal:
+    def __init__(self, wires, outgoing, incoming):
+        self.w, self.outgoing, self.incoming = wires, outgoing, incoming
+        self.first = wires.slots(3)
+
+    def mate(self, i):
+        w = self.w
+        return [(1 - w.x, w.k), (w.x, 1 - w.k), (1 - w.x, 1 - w.k)][i]
+
+    def piece(self, i):
+        w = self.w
+        x, k = self.mate(i)
+        return w.copy(
+            self.outgoing(x, k), self.incoming(w.x, w.k), w.at(x=x, k=k), self.first + i
+        )
+
+    def landed(self, i):
+        x, k = self.mate(i)
+        ref = self.incoming(x, k)
+        return self.w.copy(ref, ref, self.w.at(x=x, k=k), self.first + i)
+
+    def start(self):
+        for i in range(3):
+            self.piece(i).start()
+
+    def arrive(self):
+        for i in range(3):
+            self.landed(i).wait_recv()
+
+    def drain(self):
+        for i in range(3):
+            self.piece(i).wait_send()
+
+
 class Visit:
     def __init__(self, wires, home, full, local):
         self.w, self.home, self.full, self.local = wires, home, full, local
         self.first = wires.slots(2)
         w = wires
-        self.own = [every(w.x == j, w.zh == w.k, w.zl == w.x, w.zb == w.k) for j in range(2)]
-        self.here = [every(w.zh == i, w.zl == w.x, w.zb == w.k, w.zh == w.k) for i in range(2)]
+        self.own = [every(w.v == j, w.zh == w.k, w.zb == w.k) for j in range(2)]
+        self.here = [every(w.zh == i, w.zb == w.k, w.zh == w.k) for i in range(2)]
 
     def piece(self, j):
         w = self.w
         return w.copy(
             self.home.at[j],
             self.full(w.zh, w.zb, w.x),
-            w.at(x=j, zh=w.k, zl=w.x, k=w.zb),
+            w.at(v=j, zh=w.k, k=w.zb),
             self.first + j,
             self.first + w.zh,
         )
@@ -229,7 +244,7 @@
 
     def landed(self, i):
         w = self.w
-        ref = self.full(i, w.k, w.zl)
+        ref = self.full(i, w.k, w.x)
         return w.copy(ref, ref, w.core(), self.first + i)
 
     def start(self):
@@ -253,21 +268,21 @@
         self.w, self.done, self.home, self.local = wires, done, home, local
         self.first = wires.slots(2)
         w = wires
-        self.own = [every(w.x == w.zl, w.zh == i, w.zb == w.k, w.k == w.zh) for i in range(2)]
-        self.here = [every(w.x == j, w.zh == w.k, w.zl == w.x, w.zb == w.k) for j in range(2)]
+        self.own = [every(w.zh == i, w.zb == w.k, w.k == w.zh) for i in range(2)]
+        self.here = [every(w.v == j, w.zh == w.k, w.zb == w.k) for j in range(2)]
 
     def piece(self, i):
         w = self.w
         return w.copy(
             self.done(i),
-            self.home.at[w.x],
-            w.at(x=w.zl, zh=i, zl=(w.k + i) % 2, k=w.zh),
+            self.home.at[w.v],
+            w.at(zh=i, v=(w.k + i) % 2, k=w.zh),
             self.first + i,
-            self.first + w.x,
+            self.first + w.v,
         )
 
     def stay(self, i):
-        return pltpu.make_async_copy(self.done(i), self.home.at[self.w.x], self.local)
+        return pltpu.make_async_copy(self.done(i), self.home.at[self.w.v], self.local)
 
     def landed(self, j):
         ref = self.home.at[j]
@@ -307,12 +322,12 @@
 
 
 def hidden_columns(rank):
-    zl, k = rank // 2, rank % 2
+    x, k = rank // 2, rank % 2
     return [
-        (128 * (16 * y + 8 * k + 4 * zh + 2 * (zl ^ zh) + x), 128)
+        (128 * (16 * y + 8 * k + 4 * zh + 2 * (v ^ zh) + x), 128)
         for y in range(2)
         for zh in range(2)
-        for x in range(2)
+        for v in range(2)
     ]
 
 
@@ -328,13 +343,13 @@
             self.part.at[0, i], self.got_core.at[i], w.core(), self.first + i
         )
 
-    def rows(self, x):
-        return pl.ds(pl.multiple_of(self.half * x, self.half), self.half)
+    def rows(self, v):
+        return pl.ds(pl.multiple_of(self.half * v, self.half), self.half)
 
     def across(self, i):
         w = self.w
         return w.copy(
-            self.part.at[1, i, self.rows(1 - w.zl)],
+            self.part.at[1, i, self.rows(1 - w.x)],
             self.got_across.at[i],
             w.across(),
             self.first + 2 + i,
@@ -351,13 +366,30 @@
 
     def take(self, i):
         self.across(i).wait_recv()
-        own = self.part[1, i, self.rows(self.w.zl)]
+        own = self.part[1, i, self.rows(self.w.x)]
         return own.astype(F32) + self.got_across[i].astype(F32)
 
     def drain(self):
         for i in range(2):
             self.core(i).wait_send()
             self.across(i).wait_send()
+
+
+class Parts:
+    def __init__(self, copies):
+        self.copies = copies
+
+    def start(self):
+        for copy in self.copies:
+            copy.start()
+
+    def wait_send(self):
+        for copy in self.copies:
+            copy.wait_send()
+
+    def wait_recv(self):
+        for copy in self.copies:
+            copy.wait_recv()
 
 
 class Fold(Pairs):
@@ -365,22 +397,27 @@
         super().__init__(wires, order)
         self.whole, self.block = whole, block
         self.got_b, self.got_b_block, self.got_a, self.got_z = got_b, got_b_block, got_a, got_z
-        self.first = wires.slots(4)
+        self.first = wires.slots(5)
 
     def stage_b(self):
         w = self.w
-        b = w.y if self.order == "xy" else w.x
-        return w.copy(self.whole(1 - b), self.got_b, self.partner(0, 0, 1), self.first)
+        b = w.y if self.order == "vy" else w.v
+        return Parts(
+            [
+                w.copy(source, target, self.partner(0, 0, 1), self.first + 4 * i)
+                for i, (source, target) in enumerate(zip(self.whole(1 - b), self.got_b))
+            ]
+        )
 
     def stage_a(self, z):
-        x, y, zh = self.place(z, 1, 0)
+        v, y, zh = self.place(z, 1, 0)
         return self.w.copy(
-            self.block(x, y, zh), self.got_a.at[zh], self.partner(0, 1, 0), self.first + 1 + z,
+            self.block(v, y, zh), self.got_a.at[zh], self.partner(0, 1, 0), self.first + 1 + z,
             self.first + 1 + z,
         )
 
     def landed_a(self, z):
-        x, y, zh = self.place(z, 0, 0)
+        v, y, zh = self.place(z, 0, 0)
         ref = self.got_a.at[zh]
         return self.w.copy(ref, ref, self.partner(0, 1, 0), self.first + 1 + z)
 
@@ -389,9 +426,9 @@
         return self.w.copy(ref, self.got_z, self.partner(1, 0, 0), self.first + 3)
 
     def two(self, z, a):
-        x, y, zh = self.place(z, a, 0)
-        own = self.block(x, y, zh)[...].astype(F32)
-        return own + self.got_b_block(x if self.order == "xy" else y, zh)[...].astype(F32)
+        v, y, zh = self.place(z, a, 0)
+        own = self.block(v, y, zh)[...].astype(F32)
+        return own + self.got_b_block(v if self.order == "vy" else y, zh)[...].astype(F32)
 
     def three(self, z):
         return self.two(z, 0) + self.got_a[self.place(z, 0, 0)[2]].astype(F32)
@@ -508,28 +545,24 @@
     ("gains_b", (2, 2, 8, 128), F32),
     ("gains_a", (2, 8, 128), F32),
     ("gains_z", (8, 128), F32),
-    ("heads_dealt", (4, 32, 768), BF16),
-    ("gate_dealt", (4, 32, 1024), BF16),
-    ("up_dealt", (4, 32, 1024), BF16),
     ("gains_deal", (8, 128), F32),
     ("gains_dealt", (4, 8, 128), F32),
     ("out_deal", (32, 1024), BF16),
     ("out_home", (32, 1024), BF16),
     ("done_out", (2, 128, 1024), BF16),
-    ("input_home", (2, 128, 1024), BF16),
 ]
 
 
 def layer_body(
     rows, cots, ids, wq, wk, wv, wo, wg, wu, wd, gains,
-    output, input_grad, q_out, k_out, v_out, o_out, g_out, u_out, d_out, gain_out,
+    output, input_home, heads_dealt, o_out, gate_dealt, up_dealt, d_out, gain_out,
     *scratch,
 ):
     send, recv, local = scratch[-3:]
     m = type("Memory", (), dict(zip([name for name, _, _ in SCRATCH], scratch)))
     w = Wires(send, recv)
-    x, y, zh, zb, zl, k = w.x, w.y, w.zh, w.zb, w.zl, w.k
-    rank = 2 * zl + k
+    v, y, zh, zb, x, k = w.v, w.y, w.zh, w.zb, w.x, w.k
+    rank = 2 * x + k
     w.greet()
 
     used = [0]
@@ -549,79 +582,82 @@
     def deal_rows(packed, whole):
         return Deal(
             w,
-            lambda zl, k: packed.at[2 * zl + k],
-            lambda szl, sk: whole.at[y, sk, zh, (szl + zh) % 2, x],
+            lambda x, k: packed.at[2 * x + k],
+            lambda sx, sk: whole.at[y, sk, zh, zb, sx],
         )
 
     def group_rows(ref):
-        return lambda x, y, zh: ref.at[y, :, zh, :, x]
+        return lambda v, y, zh: ref.at[y, :, zh, (v + zh) % 2]
 
     def own_rows(ref):
-        return lambda x, y, zh: ref.at[y, k, zh, (zl + zh) % 2, x]
+        return lambda v, y, zh: ref.at[y, k, zh, (v + zh) % 2, x]
 
     visit_rows = Visit(w, rows, sequence_block(m.rows_all), spare())
     visit_rows.start()
     pack_rows(head_columns, (wq, wk, wv), m.heads_pack)
     deal_heads = deal_rows(m.heads_pack, m.heads_all)
     deal_heads.start()
+    spread_gains = Spread(w, "vy", own_rows(m.gains_all), gains)
+    spread_gains.start()
+    swap = w.copy(ids, m.ids_all.at[k], w.core(), w.slots(1))
+    swap.start()
+    spread_out = Spread(w, "vy", own_rows(m.out_all), wo)
+    spread_out.start()
+    pack_rows(hidden_columns, (wg,), m.gate_pack)
+    pack_rows(hidden_columns, (wu,), m.up_pack)
     stays = [
         stay(m.heads_pack.at[rank], m.heads_all.at[y, k, zh, zb, x]),
+        stay(m.gate_pack.at[rank], m.gate_all.at[y, k, zh, zb, x]),
+        stay(m.up_pack.at[rank], m.up_all.at[y, k, zh, zb, x]),
         stay(wo, m.out_all.at[y, k, zh, zb, x]),
         stay(gains, m.gains_all.at[y, k, zh, zb, x]),
-        stay(wd, m.down_all.at[y, zh, x]),
+        stay(wd, m.down_all.at[y, zh, v]),
         stay(ids, m.ids_all.at[k]),
     ]
-    swap = w.copy(ids, m.ids_all.at[k], w.core(), w.slots(1))
-    swap.start()
-    spread_gains = Spread(w, "xy", own_rows(m.gains_all), gains)
-    spread_gains.start()
-    pack_rows(hidden_columns, (wg,), m.gate_pack)
-    pack_rows(hidden_columns, (wu,), m.up_pack)
-    stays.append(stay(m.gate_pack.at[rank], m.gate_all.at[y, k, zh, zb, x]))
-    stays.append(stay(m.up_pack.at[rank], m.up_all.at[y, k, zh, zb, x]))
     deal_gate = deal_rows(m.gate_pack, m.gate_all)
     deal_up = deal_rows(m.up_pack, m.up_all)
     for copy in stays:
         copy.wait()
     deal_heads.arrive()
-    spread_heads = Spread(w, "yx", group_rows(m.heads_all))
+    spread_heads = Spread(w, "vy", group_rows(m.heads_all))
     spread_heads.start()
-    spread_out = Spread(w, "yx", own_rows(m.out_all), wo)
-    spread_out.start()
-    visit_rows.arrive()
-    share_rows = Share(w, lambda zl, k: m.rows_all.at[:, k, zl])
-    share_rows.start()
+    spread_down = Spread(w, "vy", lambda v, y, zh: m.down_all.at[y, zh, v], wd)
+    spread_down.start_rest()
+    spread_gains.got_first()
     deal_gate.start()
     deal_up.start()
-    spread_gains.got_first()
+    visit_rows.arrive()
+    share_rows = Share(w, lambda x, k: m.rows_all.at[:, k, x])
+    share_rows.start()
     spread_gains.got_z()
+    spread_heads.got_first()
+    spread_out.got_first()
     spread_gains.got_last()
-    spread_heads.got_first()
+    deal_gate.arrive()
+    spread_gate = Spread(w, "vy", group_rows(m.gate_all))
+    spread_gate.start_rest()
+    deal_up.arrive()
+    spread_up = Spread(w, "yv", group_rows(m.up_all))
+    spread_up.start_rest()
     spread_heads.got_z()
-    share_rows.forward()
-    deal_gate.arrive()
-    spread_gate = Spread(w, "xy", group_rows(m.gate_all))
-    spread_gate.start()
-    deal_up.arrive()
-    spread_up = Spread(w, "yx", group_rows(m.up_all))
-    spread_up.start()
-    spread_down = Spread(w, "xy", lambda x, y, zh: m.down_all.at[y, zh, x], wd)
-    spread_down.start()
-    spread_heads.got_last()
+    spread_down.start_z()
+    spread_gate.start_z()
+    spread_up.start_z()
     spread_gains.arrive()
-    share_gains = [
-        Share(w, lambda zl, k: m.gains_all.at[:, k, 0, zl]),
-        Share(w, lambda zl, k: m.gains_all.at[:, k, 1, 1 - zl]),
-    ]
+    share_gains = [Share(w, lambda x, k: m.gains_all.at[:, k, :, :, x])]
     for share in share_gains:
         share.start()
+    share_rows.forward()
     swap.wait()
-    m.ids_row[...] = m.ids_all[zh, x].astype(F32)
+    m.ids_row[...] = m.ids_all[zh, v].astype(F32)
     for j in range(8):
         piece = slice(128 * j, 128 * j + 128)
         m.ids_col[piece, :] = jnp.broadcast_to(m.ids_row[:, piece], (128, 128)).T
+    spread_out.got_z()
+    spread_heads.got_last()
     for share in share_gains:
         share.forward()
+    spread_down.got_first()
     share_rows.arrive()
     for share in share_gains:
         share.arrive()
@@ -640,13 +676,6 @@
         return 0
 
     lax.fori_loop(0, 4, first_norm, 0)
-    spread_out.got_first()
-    spread_out.got_z()
-    visit_cots = Visit(w, cots, sequence_block(m.cots_all), spare())
-    visit_cots.start()
-    spread_gate.got_first()
-    spread_up.got_first()
-    spread_down.got_first()
     spread_heads.arrive()
     heads = m.heads_all[...].reshape(1024, 768)
     for b in range(4):
@@ -657,6 +686,8 @@
         m.keys_turned[:, span] = made[:, 256:512].T
         m.values_turned[:, span] = made[:, 512:].T
     spread_out.got_last()
+    spread_gate.got_first()
+    spread_up.got_first()
 
     def bias_of(b):
         start, count = 256 * b, 256 * b + 256
@@ -669,8 +700,8 @@
     def head_rows(h):
         return pl.ds(pl.multiple_of(h * HEAD, HEAD), HEAD)
 
-    def rank_columns(zl, k):
-        return pl.ds(pl.multiple_of(256 * (2 * zl + k), 256), 256)
+    def rank_columns(x, k):
+        return pl.ds(pl.multiple_of(256 * (2 * x + k), 256), 256)
 
     def mix(b):
         span, count = slice(256 * b, 256 * b + 256), 256 * b + 256
@@ -689,40 +720,35 @@
             return 0
 
         lax.fori_loop(0, 4, one, 0)
-        m.mixed_all[b // 2, b % 2, :, rank_columns(zl, k)] = m.mixed_turned[:, span].T
+        m.mixed_all[b // 2, b % 2, :, rank_columns(x, k)] = m.mixed_turned[:, span].T
 
     def share_mixed(b):
-        return Share(w, lambda zl, k: m.mixed_all.at[b // 2, b % 2, :, rank_columns(zl, k)])
+        return Share(w, lambda x, k: m.mixed_all.at[b // 2, b % 2, :, rank_columns(x, k)])
 
     shares = [share_mixed(b) for b in range(4)]
     mix(0)
     shares[0].start()
-    visit_cots.arrive()
-    share_cots = Share(w, lambda zl, k: m.cots_all.at[:, k, zl])
-    share_cots.start()
-    spread_gate.got_z()
+    spread_down.got_z()
     mix(1)
     shares[1].start()
+    visit_cots = Visit(w, cots, sequence_block(m.cots_all), spare())
+    visit_cots.start()
     shares[0].forward()
     spread_out.arrive()
-    share_out = [
-        Share(w, lambda zl, k: m.out_all.at[:, k, 0, zl]),
-        Share(w, lambda zl, k: m.out_all.at[:, k, 1, 1 - zl]),
-    ]
+    share_out = [Share(w, lambda x, k: m.out_all.at[:, k, :, :, x])]
     for share in share_out:
         share.start()
-    spread_up.got_z()
+    spread_gate.got_z()
     mix(2)
     shares[2].start()
     shares[1].forward()
-    spread_down.got_z()
     for share in share_out:
         share.forward()
-    share_cots.forward()
+    spread_up.got_z()
+    spread_down.got_last()
     mix(3)
     shares[3].start()
     shares[2].forward()
-    spread_gate.got_last()
     for share in share_out:
         share.arrive()
 
@@ -730,10 +756,7 @@
         span = slice(256 * b, 256 * b + 256)
         if b == 2:
             shares[3].forward()
-        if b == 1:
-            spread_up.got_last()
-        if b == 3:
-            spread_down.got_last()
+            spread_gate.got_last()
         shares[b].arrive()
         middle = m.rows_all[b // 2, b % 2].reshape(256, 1024).astype(F32)
         whole = m.out_all[...].reshape(1024, 1024)
@@ -744,6 +767,11 @@
         def _():
             m.middle_keep[b // 2] = middle
 
+    visit_cots.arrive()
+    share_cots = Share(w, lambda x, k: m.cots_all.at[:, k, x])
+    share_cots.start()
+    spread_up.got_last()
+    share_cots.forward()
     for spread in (spread_gate, spread_up, spread_down):
         spread.arrive()
     share_cots.arrive()
@@ -816,26 +844,27 @@
 
     def fold_plane(whole, got_b, got_a, got_z):
         return Fold(
-            w, "xy", lambda y: whole.at[y], lambda x, y, zh: whole.at[y, :, zh, :, x],
-            got_b, lambda x, zh: got_b.at[:, zh, :, x], got_a, got_z,
+            w, "vy", lambda y: [whole.at[y]], lambda v, y, zh: whole.at[y, :, zh, (v + zh) % 2],
+            [got_b], lambda v, zh: got_b.at[:, zh, (v + zh) % 2], got_a, got_z,
         )
 
     def fold_side(whole, got_b, got_a, got_z):
         return Fold(
-            w, "yx", lambda x: whole.at[:, :, :, :, x], lambda x, y, zh: whole.at[y, :, zh, :, x],
-            got_b, lambda y, zh: got_b.at[y, :, zh], got_a, got_z,
+            w, "yv", lambda v: [whole.at[:, :, 0, v], whole.at[:, :, 1, 1 - v]],
+            lambda v, y, zh: whole.at[y, :, zh, (v + zh) % 2],
+            [got_b.at[0], got_b.at[1]], lambda y, zh: got_b.at[zh, y], got_a, got_z,
         )
 
     def fold_block(whole, got_b, got_a, got_z):
         return Fold(
-            w, "xy", lambda y: whole.at[y], lambda x, y, zh: whole.at[y, zh, x],
-            got_b, lambda x, zh: got_b.at[zh, x], got_a, got_z,
+            w, "vy", lambda y: [whole.at[y]], lambda v, y, zh: whole.at[y, zh, v],
+            [got_b], lambda v, zh: got_b.at[zh, v], got_a, got_z,
         )
 
     fold_down = fold_block(m.down_all, m.down_b, m.down_a, m.down_z)
     fold_gate = fold_plane(m.gate_all, m.gate_b, m.gate_a, m.gate_z)
     fold_up = fold_side(m.up_all, m.up_b, m.up_a, m.up_z)
-    fold_heads = fold_side(m.heads_part, m.heads_b, m.heads_a, m.heads_z)
+    fold_heads = fold_plane(m.heads_part, m.heads_b, m.heads_a, m.heads_z)
     fold_gains = fold_block(m.gains_part, m.gains_b, m.gains_a, m.gains_z)
     down_part(1 - y)
     fold_down.start()
@@ -845,8 +874,8 @@
     wide_part(m.gate_all, m.grad_gate, 1 - y)
     fold_gate.start()
 
-    share_branch = Share(w, lambda zl, k: m.branch.at[:, k, zl])
-    own_half = total_norm.rows(zl)
+    share_branch = Share(w, lambda x, k: m.branch.at[:, k, x])
+    own_half = total_norm.rows(x)
     gain_sum = jnp.zeros((1, 1024), F32)
     for i in range(2):
         grad, term = norm_back(
@@ -854,9 +883,9 @@
         )
         gain_sum = gain_sum + term
         m.done_out[i] = (m.middle_keep[i, own_half] + total_out.take(i)).astype(BF16)
-        grad = grad + m.cots_all[i, k, zl].astype(F32)
+        grad = grad + m.cots_all[i, k, x].astype(F32)
         m.middle_keep[i, own_half] = grad
-        m.branch[i, k, zl] = grad.astype(BF16)
+        m.branch[i, k, x] = grad.astype(BF16)
     share_branch.start()
     return_out = Return(w, lambda i: m.done_out.at[i], output, spare())
     return_out.start()
@@ -878,7 +907,7 @@
 
     grad_mixed, grad_mixed_turned = m.grad_up.at[:, :256], m.hidden.at[:256]
     grad_heads = m.grad_gate.at[:, :768]
-    out_own = m.out_all[zl, k].reshape(256, 1024)
+    out_own = m.out_all[x, k].reshape(256, 1024)
     for b in range(4):
         span = slice(256 * b, 256 * b + 256)
         made = dots(m.branch[b // 2, b % 2].reshape(256, 1024), out_own, NT).astype(BF16)
@@ -890,7 +919,7 @@
         .reshape(2, 2, 2, 32, 1024)
     )
     base = w.slots(6)
-    owner = y == zl
+    owner = y == x
     out_across = w.copy(m.out_part, m.out_b, w.at(y=1 - y), base)
     pl.when(jnp.logical_not(owner))(lambda: out_across.start())
     m.grad_keys[...] = jnp.zeros_like(m.grad_keys)
@@ -956,11 +985,11 @@
 
     for i in range(2):
         grad, term = norm_back(
-            m.rows_all[i, k, zl].astype(F32), m.gain_rows[0], total_first.take(i)
+            m.rows_all[i, k, x].astype(F32), m.gain_rows[0], total_first.take(i)
         )
         gain_sum = gain_sum + term
         done_in(i)[...] = (m.middle_keep[i, own_half] + grad).astype(BF16)
-    return_in = Return(w, done_in, m.input_home, spare())
+    return_in = Return(w, done_in, input_home, spare())
     return_in.start()
     gain_rows_part(0, gain_sum)
     fold_gains.start()
@@ -970,17 +999,19 @@
     def out_side(z):
         side = 1 - zh if z else zh
         return w.copy(
-            m.out_part.at[side, :, 1 - x], m.out_a.at[side], w.at(x=1 - x), base + 1 + z
+            m.out_part.at[side, (1 - v + side) % 2], m.out_a.at[side], w.at(v=1 - v), base + 1 + z
         )
 
     def out_side_landed(z):
         ref = m.out_a.at[1 - zh if z else zh]
-        return w.copy(ref, ref, w.at(x=1 - x), base + 1 + z)
-
-    def out_two(side, x):
-        return m.out_part[side, :, x].astype(F32) + m.out_b[side, :, x].astype(F32)
-
-    out_half = w.copy(m.out_part.at[1 - zh, :, x], m.out_z, w.at(zh=1 - zh), base + 3)
+        return w.copy(ref, ref, w.at(v=1 - v), base + 1 + z)
+
+    def out_two(side, v):
+        at = (v + side) % 2
+        return m.out_part[side, at].astype(F32) + m.out_b[side, at].astype(F32)
+
+    far = (v + 1 - zh) % 2
+    out_half = w.copy(m.out_part.at[1 - zh, far], m.out_z, w.at(zh=1 - zh), base + 3)
     out_last = w.copy(m.out_deal, m.out_home, w.across(), base + 4)
 
     @pl.when(owner)
@@ -988,7 +1019,7 @@
         out_across.wait_recv()
         for side in (1, 0):
             at = 1 - zh if side else zh
-            m.out_part[at, :, 1 - x] = out_two(at, 1 - x).astype(BF16)
+            m.out_part[at, (1 - v + at) % 2] = out_two(at, 1 - v).astype(BF16)
             out_side(side).start()
 
     fold_heads.second()
@@ -998,8 +1029,8 @@
     @pl.when(owner)
     def _():
         out_side_landed(1).wait_recv()
-        m.out_part[1 - zh, :, x] = (
-            out_two(1 - zh, x) + m.out_a[1 - zh].astype(F32)
+        m.out_part[1 - zh, far] = (
+            out_two(1 - zh, v) + m.out_a[1 - zh].astype(F32)
         ).astype(BF16)
         out_half.start()
 
@@ -1007,60 +1038,47 @@
 
     def deal_grads(packed, dealt):
         return Deal(
-            w, lambda zl, k: packed.at[2 * k + (zl + zh) % 2], lambda zl, k: dealt.at[2 * zl + k]
+            w, lambda x, k: packed.at[2 * k + x], lambda x, k: dealt.at[2 * x + k]
         )
 
     deal_up.drain()
     deal_gate.drain()
     deal_heads.drain()
     m.up_pack[...] = fold_up.finish().astype(BF16).reshape(4, 32, 1024)
-    deal_up_grad = deal_grads(m.up_pack, m.up_dealt)
+    deal_up_grad = deal_grads(m.up_pack, up_dealt)
     deal_up_grad.start()
     fold_heads.third()
     fold_gains.third()
     m.gate_pack[...] = fold_gate.finish().astype(BF16).reshape(4, 32, 1024)
-    deal_gate_grad = deal_grads(m.gate_pack, m.gate_dealt)
+    deal_gate_grad = deal_grads(m.gate_pack, gate_dealt)
     deal_gate_grad.start()
 
     @pl.when(owner)
     def _():
         out_side_landed(0).wait_recv()
         out_half.wait_recv()
-        out_total = out_two(zh, x) + m.out_a[zh].astype(F32) + m.out_z[...].astype(F32)
+        out_total = out_two(zh, v) + m.out_a[zh].astype(F32) + m.out_z[...].astype(F32)
         first, second = out_total[0], out_total[1]
-        m.out_deal[...] = jnp.where(zb == 0, second, first).astype(BF16)
+        m.out_deal[...] = jnp.where(x == 0, second, first).astype(BF16)
         out_last.start()
-        o_out[...] = jnp.where(zb == 0, first, second)
+        o_out[...] = jnp.where(x == 0, first, second)
 
     return_in.arrive()
-    input_grad[...] = m.input_home[...].astype(F32)
     m.gains_deal[...] = fold_gains.finish()
     m.gains_dealt[rank] = m.gains_deal[...]
-    deal_gains = Deal(w, lambda zl, k: m.gains_deal, lambda zl, k: m.gains_dealt.at[2 * zl + k])
+    deal_gains = Deal(w, lambda x, k: m.gains_deal, lambda x, k: m.gains_dealt.at[2 * x + k])
     deal_gains.start()
     m.heads_pack[...] = fold_heads.finish().astype(BF16).reshape(4, 32, 768)
-    deal_heads_grad = deal_grads(m.heads_pack, m.heads_dealt)
+    deal_heads_grad = deal_grads(m.heads_pack, heads_dealt)
     deal_heads_grad.start()
-    m.up_dealt[rank] = m.up_pack[2 * k + zb]
-    m.gate_dealt[rank] = m.gate_pack[2 * k + zb]
-    m.heads_dealt[rank] = m.heads_pack[2 * k + zb]
-    for deal, dealt, target in (
-        (deal_up_grad, m.up_dealt, u_out),
-        (deal_gate_grad, m.gate_dealt, g_out),
-    ):
-        deal.arrive()
-        for r in range(4):
-            for j, (start, width) in enumerate(hidden_columns(r)):
-                target[:, start : start + width] = dealt[
-                    r, :, 128 * j : 128 * j + width
-                ].astype(F32)
+    up_dealt[rank] = m.up_pack[2 * k + x]
+    gate_dealt[rank] = m.gate_pack[2 * k + x]
+    heads_dealt[rank] = m.heads_pack[2 * k + x]
+    deal_up_grad.arrive()
+    deal_gate_grad.arrive()
     deal_gains.arrive()
     gain_out[...] = m.gains_dealt[0] + m.gains_dealt[1] + m.gains_dealt[2] + m.gains_dealt[3]
     deal_heads_grad.arrive()
-    for r in range(4):
-        for j, target in enumerate((q_out, k_out, v_out)):
-            at = 256 * j
-            target[:, 256 * r : 256 * r + 256] = m.heads_dealt[r, :, at : at + 256].astype(F32)
 
     @pl.when(jnp.logical_not(owner))
     def _():
@@ -1084,6 +1102,25 @@
         out_last.wait_send()
 
     pl.when(jnp.logical_not(owner))(lambda: out_across.wait_send())
+
+
+def finish_body(
+    output, input_home, heads, out, gate, up, down,
+    output_to, input_to, q_to, k_to, v_to, out_to, gate_to, up_to, down_to,
+):
+    for dealt, target in ((gate, gate_to), (up, up_to)):
+        for r in range(4):
+            for j, (start, width) in enumerate(hidden_columns(r)):
+                piece = dealt[r, :, 128 * j : 128 * j + width]
+                target[:, start : start + width] = piece.astype(F32)
+    for r in range(4):
+        for j, target in enumerate((q_to, k_to, v_to)):
+            piece = heads[r, :, 256 * j : 256 * j + 256]
+            target[:, 256 * r : 256 * r + 256] = piece.astype(F32)
+    output_to[...] = output[...]
+    input_to[...] = input_home[...].astype(F32)
+    out_to[...] = out[...]
+    down_to[...] = down[...]
 
 
 def grouped(
@@ -1099,6 +1136,16 @@
     d, f = layer_input.shape[2], gate_weight.shape[1]
     outs = (
         shaped(*layer_input.shape),
+        shaped(*layer_input.shape),
+        shaped(4, piece, 3 * d // 4),
+        shaped(piece, d, dtype=F32),
+        shaped(4, piece, f // 4),
+        shaped(4, piece, f // 4),
+        shaped(*down_weight.shape, dtype=F32),
+        shaped(8, 128, dtype=F32),
+    )
+    finals = (
+        shaped(*layer_input.shape),
         shaped(*layer_input.shape, dtype=F32),
         shaped(piece, d, dtype=F32),
         shaped(piece, d, dtype=F32),
@@ -1107,7 +1154,6 @@
         shaped(piece, f, dtype=F32),
         shaped(piece, f, dtype=F32),
         shaped(*down_weight.shape, dtype=F32),
-        shaped(8, 128, dtype=F32),
     )
     rooms = [pltpu.VMEM(shape, dtype) for _, shape, dtype in SCRATCH]
     made = pl.pallas_call(
@@ -1115,7 +1161,7 @@
         name="layer",
         out_shape=outs,
         in_specs=[ANY, ANY, ANY, VMEM, VMEM, VMEM, ANY, VMEM, VMEM, ANY, ANY],
-        out_specs=(ANY,) + (VMEM,) * 9,
+        out_specs=(VMEM,) * len(outs),
         scratch_shapes=rooms
         + [
             pltpu.SemaphoreType.DMA((192,)),
@@ -1129,7 +1175,15 @@
         layer_input, out_grad, doc_ids.reshape(2, 1, -1), query_weight, key_weight, value_weight,
         out_weight, gate_weight, up_weight, down_weight, gains,
     )
-    output, input_grad, q, k_, v, o, g, u, down, gain = made
+    gain = made[-1]
+    output, input_grad, q, k_, v, o, g, u, down = pl.pallas_call(
+        finish_body,
+        name="finish",
+        out_shape=finals,
+        in_specs=[VMEM] * 7,
+        out_specs=(VMEM,) * len(finals),
+        compiler_params=pltpu.CompilerParams(vmem_limit_bytes=58 << 20),
+    )(*made[:-1])
 
     def gain_of(row):
         return lax.dynamic_slice(gain, (row + k, lane), (1, piece)).reshape(piece)

time: 298 us -> 272 us (0.913)
  the two profiles are of different devices: /device:TPU:7 before, /device:TPU:19 now
where the time goes in v4:
time: 272 us; the launch traced here: 271 us
  Pallas kernels  267 us (98%)
  local copies, waits for them, and re-layouts  3.13 us (1%)
    pallas_call x1, Pallas kernels, grouped(): pl.pallas_call(layer_body, name='layer', out_shape=outs, in_specs=[ANY, A...  264 us

profile of v4, /device:TPU:19, one launch (start us, length us, event | category | flops | bytes accessed | tf_op | source)
XLA Modules:
  0.0 271.3 jit_solution(15285127996534842801)
XLA Ops:
  0.7 0.0 copy-start.2
  0.7 0.0 copy-start.3
  0.7 0.0 copy-start.1
  0.7 0.6 copy-done.2
  1.3 0.0 copy-done.3
  1.4 0.5 dynamic_update_slice.3.gains
  1.9 0.0 copy-done.1
  1.9 0.0 copy-start
  1.9 0.6 reshape.31.ids
  2.5 0.0 copy-done
  2.5 263.9 %layer.1 = (bf16[2,128,1024]{2,1,0:T(8,128)(2,1)}, bf16[2,128,1024]{2,1,0:T(8,128)(2,1)}, bf16[4,32,768]{2,1,0:T(8,128)(2,1)}, f32[32,1024]{1,0:T(8,128)}, bf16[...) custom-call(bf16[2,128,1024]{2,1,0:T(8,128)(2,1)} %rows.1, ...), custom_call_target="tpu_custom_call" | custom-call | tf_op jit(solution)/shard_map/layer/pallas_call | solution.py:1159
  266.5 1.3 dynamic-slice_bitcast_fusion
  267.8 3.5 %finish.1 = (bf16[2,128,1024]{2,1,0:T(8,128)(2,1)}, f32[2,128,1024]{2,1,0:T(8,128)}, f32[32,1024]{1,0:T(8,128)}, f32[32,1024]{1,0:T(8,128)}, f32[32,1024]{1,0:T(...) custom-call(bf16[2,128,1024]{2,1,0:T(8,128)(2,1)} %get-tuple-element.28.output, ...), custom_call_target="tpu_custom_call" | custom-call | tf_op jit(solution)/shard_map/finish/pallas_call | solution.py:1179
  (2 shorter events, 0.0 us)
Async XLA Ops:
  0.7 0.7 copy-start.2
  0.7 0.7 copy-start.3
  0.7 1.2 copy-start.1
  1.9 0.6 copy-start

commit v5 on v4

--- a/solution.py
+++ b/solution.py
@@ -288,10 +288,9 @@
         ref = self.home.at[j]
         return self.w.copy(ref, ref, self.w.core(), self.first + j)
 
-    def start(self):
-        for i in range(2):
-            pl.when(self.own[i])(lambda: self.stay(i).start())
-            pl.when(jnp.logical_not(self.own[i]))(lambda: self.piece(i).start())
+    def start(self, i):
+        pl.when(self.own[i])(lambda: self.stay(i).start())
+        pl.when(jnp.logical_not(self.own[i]))(lambda: self.piece(i).start())
 
     def arrive(self):
         for i in range(2):
@@ -362,6 +361,8 @@
     def keep(self, i, value):
         self.core(i).wait_recv()
         self.part[1, i] = (value + self.got_core[i].astype(F32)).astype(BF16)
+
+    def send(self, i):
         self.across(i).start()
 
     def take(self, i):
@@ -815,6 +816,7 @@
     def keep(i, _):
         span, norm_part = feed(i, k)
         total_norm.keep(i, norm_part)
+        total_norm.send(i)
         total_out.keep(i, out_of(span))
         return 0
 
@@ -866,29 +868,28 @@
     fold_up = fold_side(m.up_all, m.up_b, m.up_a, m.up_z)
     fold_heads = fold_plane(m.heads_part, m.heads_b, m.heads_a, m.heads_z)
     fold_gains = fold_block(m.gains_part, m.gains_b, m.gains_a, m.gains_z)
+    shares_branch = [Share(w, lambda x, k, i=i: m.branch.at[i, k, x]) for i in range(2)]
+    own_half, other_half = total_norm.rows(x), total_norm.rows(1 - x)
+
+    def back_two(i):
+        grad, term = norm_back(m.middle_keep[i, own_half], m.gain_rows[1], total_norm.take(i))
+        grad = grad + m.cots_all[i, k, x].astype(F32)
+        m.middle_keep[i, other_half] = grad
+        m.branch[i, k, x] = grad.astype(BF16)
+        shares_branch[i].start()
+        return term
+
+    gain_sum = back_two(0)
     down_part(1 - y)
     fold_down.start()
     wide_part(m.up_all, m.grad_up, 0)
     wide_part(m.up_all, m.grad_up, 1)
     fold_up.start()
+    gain_sum = gain_sum + back_two(1)
     wide_part(m.gate_all, m.grad_gate, 1 - y)
     fold_gate.start()
-
-    share_branch = Share(w, lambda x, k: m.branch.at[:, k, x])
-    own_half = total_norm.rows(x)
-    gain_sum = jnp.zeros((1, 1024), F32)
     for i in range(2):
-        grad, term = norm_back(
-            m.middle_keep[i, own_half], m.gain_rows[1], total_norm.take(i)
-        )
-        gain_sum = gain_sum + term
-        m.done_out[i] = (m.middle_keep[i, own_half] + total_out.take(i)).astype(BF16)
-        grad = grad + m.cots_all[i, k, x].astype(F32)
-        m.middle_keep[i, own_half] = grad
-        m.branch[i, k, x] = grad.astype(BF16)
-    share_branch.start()
-    return_out = Return(w, lambda i: m.done_out.at[i], output, spare())
-    return_out.start()
+        total_out.send(i)
 
     def gain_rows_part(row, total):
         for plane in range(2):
@@ -900,15 +901,19 @@
 
     m.gains_part[...] = jnp.zeros_like(m.gains_part)
     gain_rows_part(1, gain_sum)
+    shares_branch[0].forward()
     down_part(y)
-    share_branch.forward()
+    shares_branch[1].forward()
     wide_part(m.gate_all, m.grad_gate, y)
-    share_branch.arrive()
 
     grad_mixed, grad_mixed_turned = m.grad_up.at[:, :256], m.hidden.at[:256]
     grad_heads = m.grad_gate.at[:, :768]
     out_own = m.out_all[x, k].reshape(256, 1024)
     for b in range(4):
+        if b % 2 == 0:
+            shares_branch[b // 2].arrive()
+        if b == 2:
+            fold_down.second()
         span = slice(256 * b, 256 * b + 256)
         made = dots(m.branch[b // 2, b % 2].reshape(256, 1024), out_own, NT).astype(BF16)
         grad_mixed[span, :] = made
@@ -951,50 +956,56 @@
         lax.fori_loop(0, 4, one, 0)
         grad_heads[span, :256] = grad_mixed_turned[:, span].T
 
+    for i in range(2):
+        m.done_out[i] = (m.middle_keep[i, own_half] + total_out.take(i)).astype(BF16)
+    return_out = Return(w, lambda i: m.done_out.at[i], output, spare())
+    for i in range(2):
+        return_out.start(i)
+    fold_up.second()
     unmix(0)
+    fold_gate.second()
     unmix(1)
-    fold_up.second()
+    fold_down.third()
     unmix(2)
-    fold_down.second()
+    fold_up.third()
     unmix(3)
+    fold_gate.third()
     grad_heads[:, 256:512] = (m.grad_keys[...] * HEAD**-0.5).astype(BF16)
     grad_heads[:, 512:] = m.grad_values[...].astype(BF16)
 
+    total_norm.drain()
+    total_first = Total(w, m.part_norm, m.core_norm, m.across_norm)
+
+    def first_part(i, part):
+        span = pl.ds(pl.multiple_of(256 * (2 * i + part), 256), 256)
+        return dots(grad_heads[span, :], m.heads_all[...].reshape(1024, 768), NT)
+
+    for i in range(2):
+        total_first.give(i, first_part(i, 1 - k))
     for plane in range(2):
         for half in range(2):
             made = dots(m.normed[:, lanes(plane, half)], grad_heads[...], TN)
             m.heads_part[plane, half] = made.astype(BF16).reshape(2, 2, 2, 32, 768)
     fold_heads.start()
-    total_norm.drain()
-    total_first = Total(w, m.part_norm, m.core_norm, m.across_norm)
-
-    def first_part(i, part):
-        span = pl.ds(pl.multiple_of(256 * (2 * i + part), 256), 256)
-        return dots(grad_heads[span, :], m.heads_all[...].reshape(1024, 768), NT)
-
-    for i in range(2):
-        total_first.give(i, first_part(i, 1 - k))
     for i in range(2):
         total_first.keep(i, first_part(i, k))
-    fold_up.third()
-    fold_down.third()
+        total_first.send(i)
     gain_sum = jnp.zeros((1, 1024), F32)
 
     def done_in(i):
         return m.normed_two.at[pl.ds(128 * i, 128)]
 
+    return_in = Return(w, done_in, input_home, spare())
     for i in range(2):
         grad, term = norm_back(
             m.rows_all[i, k, x].astype(F32), m.gain_rows[0], total_first.take(i)
         )
         gain_sum = gain_sum + term
-        done_in(i)[...] = (m.middle_keep[i, own_half] + grad).astype(BF16)
-    return_in = Return(w, done_in, input_home, spare())
-    return_in.start()
+        done_in(i)[...] = (m.middle_keep[i, other_half] + grad).astype(BF16)
+        return_in.start(i)
     gain_rows_part(0, gain_sum)
     fold_gains.start()
 
-    fold_gate.second()
 
     def out_side(z):
         side = 1 - zh if z else zh
@@ -1024,7 +1035,6 @@
 
     fold_heads.second()
     fold_gains.second()
-    fold_gate.third()
 
     @pl.when(owner)
     def _():
@@ -1088,10 +1098,10 @@
     return_out.arrive()
     for part in [
         visit_rows, visit_cots, spread_gains, spread_heads, spread_out, share_rows, share_cots,
-        share_branch, total_out, total_first, fold_down, fold_gate, fold_up, fold_heads,
+        total_out, total_first, fold_down, fold_gate, fold_up, fold_heads,
         fold_gains, return_out, return_in, deal_up_grad, deal_gate_grad, deal_heads_grad,
         deal_gains,
-    ] + share_gains + share_out:
+    ] + share_gains + share_out + shares_branch:
         part.drain()
 
     @pl.when(owner)

time: 272 us -> 263 us (0.967)
  Pallas kernels: 267 us -> 259 us
    pallas_call x1, Pallas kernels: 264 us -> 255 us  [grouped(): pl.pallas_call(layer_body, name='layer', out_shape=outs, in_specs=[ANY, A...]
where the time goes in v5:
time: 263 us
  Pallas kernels  259 us (98%)
  local copies, waits for them, and re-layouts  3.13 us (1%)
    pallas_call x1, Pallas kernels, grouped(): pl.pallas_call(layer_body, name='layer', out_shape=outs, in_specs=[ANY, A...  255 us

profile of v5, /device:TPU:19, one launch (start us, length us, event | category | flops | bytes accessed | tf_op | source)
XLA Modules:
  0.0 262.5 jit_solution(1762462058405646386)
XLA Ops:
  0.7 0.0 copy-start.2
  0.7 0.0 copy-start.3
  0.7 0.0 copy-start.1
  0.7 0.6 copy-done.2
  1.3 0.0 copy-done.3
  1.4 0.5 dynamic_update_slice.3.gains
  1.9 0.0 copy-done.1
  1.9 0.0 copy-start
  1.9 0.6 reshape.31.ids
  2.5 0.0 copy-done
  2.5 255.2 %layer.1 = (bf16[2,128,1024]{2,1,0:T(8,128)(2,1)}, bf16[2,128,1024]{2,1,0:T(8,128)(2,1)}, bf16[4,32,768]{2,1,0:T(8,128)(2,1)}, f32[32,1024]{1,0:T(8,128)}, bf16[...) custom-call(bf16[2,128,1024]{2,1,0:T(8,128)(2,1)} %rows.1, ...), custom_call_target="tpu_custom_call" | custom-call | tf_op jit(solution)/shard_map/layer/pallas_call | solution.py:1169
  257.7 1.3 dynamic-slice_bitcast_fusion
  259.0 3.5 %finish.1 = (bf16[2,128,1024]{2,1,0:T(8,128)(2,1)}, f32[2,128,1024]{2,1,0:T(8,128)}, f32[32,1024]{1,0:T(8,128)}, f32[32,1024]{1,0:T(8,128)}, f32[32,1024]{1,0:T(...) custom-call(bf16[2,128,1024]{2,1,0:T(8,128)(2,1)} %get-tuple-element.28.output, ...), custom_call_target="tpu_custom_call" | custom-call | tf_op jit(solution)/shard_map/finish/pallas_call | solution.py:1189
  (2 shorter events, 0.0 us)
Async XLA Ops:
  0.7 0.7 copy-start.2
  0.7 0.7 copy-start.3
  0.7 1.2 copy-start.1
  1.9 0.6 copy-start

commit v6 on v5

--- a/solution.py
+++ b/solution.py
@@ -497,6 +497,8 @@
     ("up_all", (2, 2, 2, 2, 2, 32, 1024), BF16),
     ("down_all", (2, 2, 2, 128, 1024), BF16),
     ("gains_all", (2, 2, 2, 2, 2, 16, 128), BF16),
+    ("heads_shards", (3, 32, 1024), BF16),
+    ("wide_shards", (2, 32, 4096), BF16),
     ("heads_pack", (4, 32, 768), BF16),
     ("gate_pack", (4, 32, 1024), BF16),
     ("up_pack", (4, 32, 1024), BF16),
@@ -564,7 +566,6 @@
     w = Wires(send, recv)
     v, y, zh, zb, x, k = w.v, w.y, w.zh, w.zb, w.x, w.k
     rank = 2 * x + k
-    w.greet()
 
     used = [0]
 
@@ -576,6 +577,10 @@
         copy = pltpu.make_async_copy(source, target, spare())
         copy.start()
         return copy
+
+    shards = [stay(shard, m.heads_shards.at[i]) for i, shard in enumerate((wq, wk, wv))]
+    shards += [stay(shard, m.wide_shards.at[i]) for i, shard in enumerate((wg, wu))]
+    w.greet()
 
     def sequence_block(ref):
         return lambda zh, zb, x: ref.at[zh, zb, x]
@@ -595,7 +600,9 @@
 
     visit_rows = Visit(w, rows, sequence_block(m.rows_all), spare())
     visit_rows.start()
-    pack_rows(head_columns, (wq, wk, wv), m.heads_pack)
+    for copy in shards:
+        copy.wait()
+    pack_rows(head_columns, [m.heads_shards.at[i] for i in range(3)], m.heads_pack)
     deal_heads = deal_rows(m.heads_pack, m.heads_all)
     deal_heads.start()
     spread_gains = Spread(w, "vy", own_rows(m.gains_all), gains)
@@ -604,8 +611,8 @@
     swap.start()
     spread_out = Spread(w, "vy", own_rows(m.out_all), wo)
     spread_out.start()
-    pack_rows(hidden_columns, (wg,), m.gate_pack)
-    pack_rows(hidden_columns, (wu,), m.up_pack)
+    pack_rows(hidden_columns, (m.wide_shards.at[0],), m.gate_pack)
+    pack_rows(hidden_columns, (m.wide_shards.at[1],), m.up_pack)
     stays = [
         stay(m.heads_pack.at[rank], m.heads_all.at[y, k, zh, zb, x]),
         stay(m.gate_pack.at[rank], m.gate_all.at[y, k, zh, zb, x]),
@@ -961,11 +968,11 @@
     return_out = Return(w, lambda i: m.done_out.at[i], output, spare())
     for i in range(2):
         return_out.start(i)
+    unmix(0)
     fold_up.second()
-    unmix(0)
-    fold_gate.second()
     unmix(1)
     fold_down.third()
+    fold_gate.second()
     unmix(2)
     fold_up.third()
     unmix(3)
@@ -1170,13 +1177,13 @@
         layer_body,
         name="layer",
         out_shape=outs,
-        in_specs=[ANY, ANY, ANY, VMEM, VMEM, VMEM, ANY, VMEM, VMEM, ANY, ANY],
-        out_specs=(VMEM,) * len(outs),
+        in_specs=[ANY] * 11,
+        out_specs=(ANY, ANY) + (VMEM,) * (len(outs) - 2),
         scratch_shapes=rooms
         + [
             pltpu.SemaphoreType.DMA((192,)),
             pltpu.SemaphoreType.DMA((192,)),
-            pltpu.SemaphoreType.DMA((16,)),
+            pltpu.SemaphoreType.DMA((24,)),
         ],
         compiler_params=pltpu.CompilerParams(
             collective_id=0, has_side_effects=True, vmem_limit_bytes=61 << 20

time: 263 us -> 261 us (level); the launches traced: 263 us -> 257 us
  Pallas kernels: 259 us -> 253 us
    pallas_call x1, Pallas kernels: 255 us -> 250 us  [grouped(): pl.pallas_call(layer_body, name='layer', out_shape=outs, in_specs=[ANY] *...]
where the time goes in v6:
time: 261 us; the launch traced here: 257 us
  Pallas kernels  253 us (97%)
  local copies, waits for them, and re-layouts  3.13 us (1%)
    pallas_call x1, Pallas kernels, grouped(): pl.pallas_call(layer_body, name='layer', out_shape=outs, in_specs=[ANY] *...  250 us

profile of v6, /device:TPU:19, one launch (start us, length us, event | category | flops | bytes accessed | tf_op | source)
XLA Modules:
  0.0 257.4 jit_solution(12498112996721475185)
XLA Ops:
  0.7 0.0 copy-start.2
  0.7 0.0 copy-start.3
  0.7 0.0 copy-start.1
  0.7 0.6 copy-done.2
  1.3 0.0 copy-done.3
  1.4 0.5 dynamic_update_slice.3.gains
  1.9 0.0 copy-done.1
  1.9 0.0 copy-start
  1.9 0.6 reshape.31.ids
  2.5 0.0 copy-done
  2.5 250.0 %layer.1 = (bf16[2,128,1024]{2,1,0:T(8,128)(2,1)}, bf16[2,128,1024]{2,1,0:T(8,128)(2,1)}, bf16[4,32,768]{2,1,0:T(8,128)(2,1)}, f32[32,1024]{1,0:T(8,128)}, bf16[...) custom-call(bf16[2,128,1024]{2,1,0:T(8,128)(2,1)} %rows.1, ...), custom_call_target="tpu_custom_call" | custom-call | tf_op jit(solution)/shard_map/layer/pallas_call | solution.py:1176
  252.5 1.3 dynamic-slice_bitcast_fusion
  253.9 3.5 %finish.1 = (bf16[2,128,1024]{2,1,0:T(8,128)(2,1)}, f32[2,128,1024]{2,1,0:T(8,128)}, f32[32,1024]{1,0:T(8,128)}, f32[32,1024]{1,0:T(8,128)}, f32[32,1024]{1,0:T(...) custom-call(bf16[2,128,1024]{2,1,0:T(8,128)(2,1)} %get-tuple-element.28.output, ...), custom_call_target="tpu_custom_call" | custom-call | tf_op jit(solution)/shard_map/finish/pallas_call | solution.py:1196
  (2 shorter events, 0.0 us)
Async XLA Ops:
  0.7 0.7 copy-start.2
  0.7 0.7 copy-start.3
  0.7 1.2 copy-start.1
  1.9 0.6 copy-start

commit v7 on v6

--- a/solution.py
+++ b/solution.py
@@ -989,14 +989,14 @@
 
     for i in range(2):
         total_first.give(i, first_part(i, 1 - k))
+    for i in range(2):
+        total_first.keep(i, first_part(i, k))
+        total_first.send(i)
     for plane in range(2):
         for half in range(2):
             made = dots(m.normed[:, lanes(plane, half)], grad_heads[...], TN)
             m.heads_part[plane, half] = made.astype(BF16).reshape(2, 2, 2, 32, 768)
     fold_heads.start()
-    for i in range(2):
-        total_first.keep(i, first_part(i, k))
-        total_first.send(i)
     gain_sum = jnp.zeros((1, 1024), F32)
 
     def done_in(i):

time: 261 us -> 259 us (level); the launches traced: 257 us -> 258 us
  no operation moved by 1% of the time
where the time goes in v7:
time: 259 us; the launch traced here: 258 us
  Pallas kernels  254 us (98%)
  local copies, waits for them, and re-layouts  3.13 us (1%)
    pallas_call x1, Pallas kernels, grouped(): pl.pallas_call(layer_body, name='layer', out_shape=outs, in_specs=[ANY] *...  251 us

profile of v7, /device:TPU:19, one launch (start us, length us, event | category | flops | bytes accessed | tf_op | source)
XLA Modules:
  0.0 258.1 jit_solution(9983476126590405958)
XLA Ops:
  0.7 0.0 copy-start.2
  0.7 0.0 copy-start.3
  0.7 0.0 copy-start.1
  0.7 0.6 copy-done.2
  1.3 0.0 copy-done.3
  1.4 0.5 dynamic_update_slice.3.gains
  1.9 0.0 copy-done.1
  1.9 0.0 copy-start
  1.9 0.6 reshape.31.ids
  2.5 0.0 copy-done
  2.5 250.7 %layer.1 = (bf16[2,128,1024]{2,1,0:T(8,128)(2,1)}, bf16[2,128,1024]{2,1,0:T(8,128)(2,1)}, bf16[4,32,768]{2,1,0:T(8,128)(2,1)}, f32[32,1024]{1,0:T(8,128)}, bf16[...) custom-call(bf16[2,128,1024]{2,1,0:T(8,128)(2,1)} %rows.1, ...), custom_call_target="tpu_custom_call" | custom-call | tf_op jit(solution)/shard_map/layer/pallas_call | solution.py:1176
  253.2 1.3 dynamic-slice_bitcast_fusion
  254.6 3.5 %finish.1 = (bf16[2,128,1024]{2,1,0:T(8,128)(2,1)}, f32[2,128,1024]{2,1,0:T(8,128)}, f32[32,1024]{1,0:T(8,128)}, f32[32,1024]{1,0:T(8,128)}, f32[32,1024]{1,0:T(...) custom-call(bf16[2,128,1024]{2,1,0:T(8,128)(2,1)} %get-tuple-element.28.output, ...), custom_call_target="tpu_custom_call" | custom-call | tf_op jit(solution)/shard_map/finish/pallas_call | solution.py:1196
  (2 shorter events, 0.0 us)
Async XLA Ops:
  0.7 0.7 copy-start.2
  0.7 0.7 copy-start.3
  0.7 1.2 copy-start.1
  1.9 0.6 copy-start
